TPU v7x, 32 devices: a whole 2x2x4 slice. The times are simulated.
32 devices in a mesh: img: 8 (over y, x, core), band: 4 (over z).
Axes of the slice: x: 2, y: 2, z: 4, core: 2. Of those that a mesh axis runs over, the one named last changes fastest.
Arguments:
- inputs: bfloat16 [32, 256, 768], P('img', 'band'), may hold values from -6 to 6
- keep_mask: int32 [32, 256], P('img', 'band'), may hold values 0 or 1
- crop_rows: int32 [32], P('img'), may hold values from 12 to 16
- crop_cols: int32 [32], P('img'), may hold values from 12 to 16
- gain_one: bfloat16 [768], replicated, may hold values from 0.5 to 1.5
- shift_one: bfloat16 [768], replicated, may hold values from -3 to 3
- w_query: bfloat16 [768, 768], replicated, may hold values from -0.3125 to 0.3125
- b_query: bfloat16 [768], replicated, may hold values from -3 to 3
- w_key: bfloat16 [768, 768], replicated, may hold values from -0.3125 to 0.3125
- w_value: bfloat16 [768, 768], replicated, may hold values from -0.21875 to 0.21875
- b_value: bfloat16 [768], replicated, may hold values from -3 to 3
- w_out: bfloat16 [768, 768], replicated, may hold values from -0.875 to 0.875
- b_out: bfloat16 [768], replicated, may hold values from -3 to 3
- gain_two: bfloat16 [768], replicated, may hold values from 0.5 to 1.5
- shift_two: bfloat16 [768], replicated, may hold values from -3 to 3
- w_up: bfloat16 [768, 3072], replicated, may hold values from -0.21875 to 0.21875
- b_up: bfloat16 [3072], replicated, may hold values from -3 to 3
- w_down: bfloat16 [3072, 768], replicated, may hold values from -0.109375 to 0.109375
- b_down: bfloat16 [768], replicated, may hold values from -3 to 3
- cotangent: bfloat16 [32, 256, 768], P('img', 'band'), may hold values from -6 to 6
Outputs:
- output: bfloat16 [32, 256, 768], P('img', 'band')
- grad_inputs: float32 [32, 256, 768], P('img', 'band')
- grad_gain_one: float32 [768], P(('img', 'band'))
- grad_shift_one: float32 [768], P(('img', 'band'))
- grad_w_query: float32 [768, 768], P(('img', 'band'))
- grad_b_query: float32 [768], P(('img', 'band'))
- grad_w_key: float32 [768, 768], P(('img', 'band'))
- grad_w_value: float32 [768, 768], P(('img', 'band'))
- grad_b_value: float32 [768], P(('img', 'band'))
- grad_w_out: float32 [768, 768], P(('img', 'band'))
- grad_b_out: float32 [768], P(('img', 'band'))
- grad_gain_two: float32 [768], P(('img', 'band'))
- grad_shift_two: float32 [768], P(('img', 'band'))
- grad_w_up: float32 [768, 3072], P(('img', 'band'))
- grad_b_up: float32 [3072], P(('img', 'band'))
- grad_w_down: float32 [3072, 768], P(('img', 'band'))
- grad_b_down: float32 [768], P(('img', 'band'))
Inputs may be any that keep to these rules, and one draw needn't show every extreme that they name: Grid rows 0 to crop_rows[i] - 1 of image i lie in its crop. Grid columns 0 to crop_cols[i] - 1 of image i lie in its crop.
All inputs are finite; a program needn't handle non-finite values. No bound on the sum of `keep_mask` on one device may be relied on, other than what follows from the above.
Results may differ from a plain program's by a relative error of at most 0.015.
The roundings to bfloat16 on the way count: a program that leaves them out, or rounds other values in their place, can miss the bound.
Values may be sent and summed in bfloat16 or wider, within the bound.
No kernel may reach another device: no remote copies, remote signals or barrier semaphores. Data moves between devices by JAX's collectives and lax.ppermute only.
A program may use at most 128 MiB of HBM per device.

v0:
```python
import functools

import jax
import jax.numpy as jnp
from jax import lax
from jax.experimental import pallas as pl
from jax.experimental.pallas import tpu as pltpu
from jax.sharding import PartitionSpec as P

HEADS = 16
HEAD_DIM = 48
SIDE = 16
EPS = 1e-05
F32 = jnp.float32
BF16 = jnp.bfloat16
GROUP = 8
GROUP_LANES = GROUP * HEAD_DIM
SCALE = HEAD_DIM ** (-0.5)


def dot_nn(a, b):
    return lax.dot_general(a, b, (((1,), (0,)), ((), ())), preferred_element_type=F32)


def dot_nt(a, b):
    return lax.dot_general(a, b, (((1,), (1,)), ((), ())), preferred_element_type=F32)


def dot_tn(a, b):
    return lax.dot_general(a, b, (((0,), (0,)), ((), ())), preferred_element_type=F32)


def norm_stats(x):
    mean = jnp.mean(x, axis=-1, keepdims=True)
    centred = x - mean
    var = jnp.mean(centred * centred, axis=-1, keepdims=True)
    r = lax.rsqrt(var + EPS)
    return centred * r, r


def norm_back(grad, n, r, gain):
    e = grad * gain
    return r * (e - jnp.mean(e, axis=-1, keepdims=True) - n * jnp.mean(e * n, axis=-1, keepdims=True))


def colsum(x):
    return jnp.sum(x.astype(F32), axis=0, keepdims=True)


def take(x, index, axis):
    return lax.dynamic_index_in_dim(x, index, axis, keepdims=False)


GAIN1, SHIFT1, BQ, BV, BO, GAIN2, SHIFT2, BDOWN = range(8)


def windows():
    out = []
    for h in range(GROUP):
        first, last = h * HEAD_DIM, (h + 1) * HEAD_DIM
        lo, hi = first // 128 * 128, -(-last // 128) * 128
        out.append((lo, hi, first - lo, last - lo))
    return out


def head_lanes(shape, first, last):
    lane = lax.broadcasted_iota(jnp.int32, shape, 1)
    return (lane >= first) & (lane < last)


def turn(x):
    return jnp.transpose(x.astype(F32)).astype(BF16)


def join(refs, rows):
    return jnp.concatenate([r[:rows, :] for r in refs], axis=0)


def column_of(row):
    n = row.shape[1]
    eye = lax.broadcasted_iota(jnp.int32, (n, n), 0) == lax.broadcasted_iota(jnp.int32, (n, n), 1)
    return jnp.sum(jnp.where(eye, row, 0.0), axis=1, keepdims=True)


def attend_kernel(rows, nb, *refs):
    slots = refs[:nb]
    vec, wq, wk, wv, wo = refs[nb : nb + 5]
    normed_t, q_o, k_o, v_o, att_t, mid_o, two_o, two_t, mask_o, att_o, kt = refs[nb + 5 :]
    tokens = nb * rows
    row = jnp.zeros((1, tokens), F32)
    for s in range(nb):
        row = row + slots[s][rows : rows + 8, :tokens].astype(F32)[s : s + 1, :]
    mask_o[...] = jnp.broadcast_to(row, mask_o.shape)
    x = join(slots, rows).astype(F32)
    n1, _ = norm_stats(x)
    normed = (n1 * vec[GAIN1 : GAIN1 + 1, :] + vec[SHIFT1 : SHIFT1 + 1, :]).astype(BF16)
    normed_t[...] = turn(normed)
    q_o[...] = (dot_nn(normed, wq[...]) + vec[BQ : BQ + 1, :]).astype(BF16)
    k = dot_nn(normed, wk[...]).astype(BF16)
    k_o[...] = k
    kt[...] = turn(k)
    v_o[...] = (dot_nn(normed, wv[...]) + vec[BV : BV + 1, :]).astype(BF16)
    keep = row > 0.5

    def group(g, carry):
        base = pl.multiple_of(g * GROUP_LANES, 128)
        blocks = [jnp.zeros((tokens, 128), F32) for _ in range(GROUP_LANES // 128)]
        for lo, hi, first, last in windows():
            wide = hi - lo
            here = head_lanes((tokens, wide), first, last)
            at = pl.ds(base + lo, wide)
            zero = jnp.zeros((tokens, wide), BF16)
            qm = jnp.where(here, q_o[:, at], zero)
            s = dot_nn(qm, kt[at, :]) * SCALE
            s = jnp.where(keep, s, -1e30)
            e = jnp.exp(s - jnp.max(s, axis=-1, keepdims=True))
            p = (e * (1.0 / jnp.sum(e, axis=-1, keepdims=True))).astype(BF16)
            o = dot_nn(p, jnp.where(here, v_o[:, at], zero))
            for j in range(wide // 128):
                blocks[lo // 128 + j] = blocks[lo // 128 + j] + o[:, j * 128 : (j + 1) * 128]
        att_o[:, pl.ds(base, GROUP_LANES)] = jnp.concatenate(blocks, axis=1).astype(BF16)
        return carry

    lax.fori_loop(0, HEADS // GROUP, group, 0)
    att_t[...] = turn(att_o[...])
    middle = x + (dot_nn(att_o[...], wo[...]) + vec[BO : BO + 1, :])
    mid_o[...] = middle
    n2, _ = norm_stats(middle)
    two = (n2 * vec[GAIN2 : GAIN2 + 1, :] + vec[SHIFT2 : SHIFT2 + 1, :]).astype(BF16)
    two_o[...] = two
    two_t[...] = turn(two)


def up_kernel(rows, nb, steps, core, *refs):
    two, middle, mask, vec, w_up, b_up, w_down = refs[:7]
    cots = refs[7 : 7 + nb]
    act_o, slope_o, gd_o, gd_keep, gd_send = refs[7 + nb : 12 + nb]
    outs = refs[12 + nb : 12 + 2 * nb]
    acc = refs[12 + 2 * nb]
    j = pl.program_id(0)
    c = core[0]

    @pl.when(j == 0)
    def _():
        col = column_of(mask[0:1, :])
        gd = (join(cots, rows).astype(F32) * col).astype(BF16)
        gd_o[...] = gd
        half = gd.shape[1] // 2
        first, second = gd[:, :half], gd[:, half:]
        gd_keep[...] = jnp.where(c == 0, first, second)
        gd_send[...] = jnp.where(c == 0, second, first)

    hidden = dot_nn(two[...], w_up[...]) + b_up[0:1, :]
    cdf = 0.5 * (1.0 + lax.erf(hidden * 0.7071067811865476))
    pdf = jnp.exp(-0.5 * hidden * hidden) * 0.3989422804014327
    act = (hidden * cdf).astype(BF16)
    act_o[...] = turn(act)
    slope_o[...] = cdf + hidden * pdf
    part = dot_nn(act, w_down[...])
    acc[...] = jnp.where(j == 0, part, acc[...] + part)

    @pl.when(j == steps - 1)
    def _():
        col = column_of(mask[0:1, :])
        out = (col * (middle[...] + (acc[...] + vec[BDOWN : BDOWN + 1, :]))).astype(BF16)
        for s in range(nb):
            outs[s][...] = out[s * rows : (s + 1) * rows, :]


def down_send_kernel(core, gd, slope, w_up, w_down, gh_o, bsum, acc):
    j = pl.program_id(0)
    gh = (dot_nt(gd[...], w_down[...]) * slope[...]).astype(BF16)
    gh_o[...] = gh
    bsum[...] = jnp.broadcast_to(colsum(gh), bsum.shape)
    part = dot_nt(gh, w_up[...])
    acc[...] = jnp.where(j == 0, part, acc[...] + part)


def down_keep_kernel(rows, nb, steps, core, *refs):
    gd, slope, w_up, w_down, before, middle, mask, vec = refs[:8]
    cots = refs[8 : 8 + nb]
    gh_o, bsum, gm_o, gb_o, gb_keep, gb_send, sums, acc = refs[8 + nb :]
    j = pl.program_id(0)
    c = core[0]
    gh = (dot_nt(gd[...], w_down[...]) * slope[...]).astype(BF16)
    gh_o[...] = gh
    bsum[...] = jnp.broadcast_to(colsum(gh), bsum.shape)
    acc[...] = jnp.where(j == 0, before[...], acc[...]) + dot_nt(gh, w_up[...])

    @pl.when(j == steps - 1)
    def _():
        grad = acc[...]
        n2, r2 = norm_stats(middle[...])
        col = column_of(mask[0:1, :])
        result = join(cots, rows).astype(F32) * col
        gm = result + norm_back(grad, n2, r2, vec[GAIN2 : GAIN2 + 1, :])
        gm_o[...] = gm
        gb = gm.astype(BF16)
        gb_o[...] = gb
        half = gb.shape[1] // 2
        first, second = gb[:, :half], gb[:, half:]
        gb_keep[...] = jnp.where(c == 0, first, second)
        gb_send[...] = jnp.where(c == 0, second, first)
        sums[0:1, :] = colsum(grad * n2)
        sums[1:2, :] = colsum(grad)
        sums[2:3, :] = colsum(gb)
        sums[3:4, :] = colsum(gd[...])
        sums[4:8, :] = jnp.zeros((4, sums.shape[1]), F32)


def attend_back_kernel(core, gb, q, k, v, mask, wo, keep_o, send_o, gq_o, gk_o, gv_o, sums, ga, qt, kt, vt, gat, gkt, gvt):
    tokens, width = gb.shape
    c = core[0]
    g_att = dot_nt(gb[...], wo[...]).astype(BF16)
    ga[...] = g_att
    gat[...] = turn(g_att)
    qt[...] = turn(q[...])
    kt[...] = turn(k[...])
    vt[...] = turn(v[...])
    keep = mask[0:1, :] > 0.5

    def group(g, carry):
        base = pl.multiple_of(g * GROUP_LANES, 128)
        blocks = [jnp.zeros((tokens, 128), F32) for _ in range(GROUP_LANES // 128)]
        for h, (lo, hi, first, last) in enumerate(windows()):
            wide = hi - lo
            here = head_lanes((tokens, wide), first, last)
            at = pl.ds(base + lo, wide)
            own = pl.ds(pl.multiple_of(base + h * HEAD_DIM, 16), HEAD_DIM)
            zero = jnp.zeros((tokens, wide), BF16)
            s = dot_nn(jnp.where(here, q[:, at], zero), kt[at, :]) * SCALE
            s = jnp.where(keep, s, -1e30)
            e = jnp.exp(s - jnp.max(s, axis=-1, keepdims=True))
            p = e * (1.0 / jnp.sum(e, axis=-1, keepdims=True))
            dp = dot_nn(jnp.where(here, ga[:, at], zero), vt[at, :])
            gvt[own, :] = dot_nn(gat[own, :], p.astype(BF16))
            ds = (p * (dp - jnp.sum(p * dp, axis=-1, keepdims=True))).astype(BF16)
            gkt[own, :] = dot_nn(qt[own, :], ds)
            o = dot_nn(ds, jnp.where(here, k[:, at], zero))
            for j in range(wide // 128):
                blocks[lo // 128 + j] = blocks[lo // 128 + j] + o[:, j * 128 : (j + 1) * 128]
        gq_o[:, pl.ds(base, GROUP_LANES)] = (jnp.concatenate(blocks, axis=1) * SCALE).astype(BF16)
        return carry

    lax.fori_loop(0, HEADS // GROUP, group, 0)
    gq = gq_o[...]
    gk = (jnp.transpose(gkt[...]) * SCALE).astype(BF16)
    gv = jnp.transpose(gvt[...]).astype(BF16)
    gk_o[...] = gk
    gv_o[...] = gv
    sums[0:1, :] = colsum(gq)
    sums[1:2, :] = colsum(gv)
    sums[2:8, :] = jnp.zeros((6, width), F32)
    half = width // 2
    for i, t in enumerate((gq, gk, gv)):
        first, second = t[:, :half], t[:, half:]
        keep_o[:, i * half : (i + 1) * half] = jnp.where(c == 0, first, second)
        send_o[:, i * half : (i + 1) * half] = jnp.where(c == 0, second, first)


def input_back_kernel(rows, nb, *refs):
    slots = refs[:nb]
    gq, gk, gv, wq, wk, wv, gm, vec, down_sums, attend_sums, up_cols = refs[nb : nb + 11]
    outs = refs[nb + 11 : 2 * nb + 11]
    cols_o = refs[2 * nb + 11]
    grad = dot_nt(gq[...], wq[...]) + dot_nt(gk[...], wk[...]) + dot_nt(gv[...], wv[...])
    n1, r1 = norm_stats(join(slots, rows).astype(F32))
    gx = (gm[...] + norm_back(grad, n1, r1, vec[GAIN1 : GAIN1 + 1, :])).astype(BF16)
    for s in range(nb):
        outs[s][...] = gx[s * rows : (s + 1) * rows, :]
    width = gx.shape[1]
    table = jnp.concatenate(
        [
            down_sums[...], attend_sums[...], colsum(grad * n1), colsum(grad),
            jnp.zeros((COLS - 18, width), F32),
        ],
        axis=0,
    )
    cols_o[...] = jnp.transpose(table) + up_cols[...]


def weight_kernel(count, extra, by_rows, cut, place, *refs):
    t = pl.program_id(0)
    parts = []
    for i in range(count):
        left, right, left_got, right_got = refs[4 * i : 4 * i + 4]
        parts.append(dot_nn(left[...], right[...]) + dot_nn(left_got[...], right_got[...]))
    at = 4 * count
    if extra:
        parts.append(refs[at][...])
        at += 1
    a_send, a_keep, b_send, b_keep = refs[at:]
    low = [p.astype(BF16) for p in parts]
    g = low[0] if len(low) == 1 else jnp.concatenate(low, axis=1)
    a, b = (g[:cut, :], g[cut:, :]) if by_rows else (g[:, :cut], g[:, cut:])

    @pl.when(t < 2)
    def _():
        a_send[0] = a

    @pl.when(t >= 2)
    def _():
        a_keep[0] = a

    @pl.when((t == 0) | (t == 3))
    def _():
        b_send[0] = b

    @pl.when((t == 1) | (t == 2))
    def _():
        b_keep[0] = b


def second_kernel(a_keep, a_got, b_keep, b_got, a_o, b_o):
    a_o[...] = (a_keep[0].astype(F32) + a_got[0].astype(F32)).astype(BF16)
    b_o[...] = (b_keep[0].astype(F32) + b_got[0].astype(F32)).astype(BF16)


def third_kernel(nb, size, by_rows, cut, core, band, a_keep, a_got, a_more, b_keep, b_got, b_more, *refs):
    sends, own, held = refs[: 2 * nb - 1], refs[2 * nb - 1], refs[2 * nb]
    a = a_keep[0].astype(F32) + a_got[0].astype(F32) + a_more[...].astype(F32)
    b = b_keep[0].astype(F32) + b_got[0].astype(F32) + b_more[...].astype(F32)
    if by_rows:
        held[:cut, :] = a
        held[cut:, :] = b
    else:
        held[:, :cut] = a
        held[:, cut:] = b
    for i, (t, s) in enumerate(targets(nb)):
        c = core[0] if t == 0 else 1 - core[0]
        block = c * nb + lax.rem(band[0] + s, nb)
        piece = held[pl.ds(pl.multiple_of(block * size, 8), size), :]
        if i == 0:
            own[...] = piece
        else:
            sends[i - 1][...] = piece.astype(BF16)


def last_kernel(nb, widths, extra, core, own, *refs):
    gots, outs = refs[: 2 * nb - 1], refs[2 * nb - 1 :]
    same, other = own[...], None
    for i, (t, _) in enumerate(targets(nb)[1:]):
        got = gots[i][...].astype(F32)
        if t == 0:
            same = same + got
        else:
            other = got if other is None else other + got
    first = core[0] == 0
    at = 0
    for w, out in zip(widths, outs):
        x, y = same[:, at : at + w], other[:, at : at + w]
        out[:, :w] = jnp.where(first, x, y)
        out[:, w:] = jnp.where(first, y, x)
        at += w
    if extra:
        outs[-1][...] = same[:, at:] + other[:, at:]


def targets(nb):
    return [(t, s) for t in range(2) for s in range(nb)]


COLS = 128


VM = pl.BlockSpec(memory_space=pltpu.VMEM)
SM = pl.BlockSpec(memory_space=pltpu.SMEM)


def shape(*dims, dtype=BF16):
    return jax.ShapeDtypeStruct(dims, dtype)


CHEAP = pl.CostEstimate(flops=1000, bytes_accessed=1000, transcendentals=0)


def after(x, *others):
    return lax.optimization_barrier((x, others))[0]


class Links:
    def __init__(self, n_img, n_band):
        self.n_img, self.nb = n_img, n_band
        self.hi = n_img // 8
        i = lax.axis_index("img")
        self.c = i & 1
        self.p = (i >> 1) & 1
        self.q = (i >> 2) & 1
        self.h = i >> 3
        self.b = lax.axis_index("band")

    def flip(self, x, bit):
        return lax.ppermute(x, "img", [(k, k ^ bit) for k in range(self.n_img)])

    def band_shift(self, x, s):
        return lax.ppermute(x, "band", [(k, (k + s) % self.nb) for k in range(self.nb)])

    def hi_shift(self, x, s):
        n = self.n_img
        return lax.ppermute(x, "img", [(k, (k + 8 * s) % n) for k in range(n)])

    def scatter_in(self, x):
        slots = [take(x, self.b, 0)]
        for s in range(1, self.nb):
            blk = take(x, (self.b + s) % self.nb, 0)
            slots.append(self.band_shift(blk, s))
        return slots

    def scatter_back(self, slots):
        got = [slots[0]]
        for s in range(1, self.nb):
            got.append(self.band_shift(slots[s], -s))
        stacked = jnp.stack(got + got)
        return lax.dynamic_slice_in_dim(stacked, (self.nb - self.b) % self.nb, self.nb, axis=0)

    def both_shift(self, x, t, s):
        n, nb = self.n_img, self.nb
        perm = [(k * nb + b, (k ^ t) * nb + (b + s) % nb) for k in range(n) for b in range(nb)]
        return lax.ppermute(x, ("img", "band"), perm)


class Unit:
    def __init__(self, links, pairs, extra=None, by_rows=False):
        self.links, self.by_rows, self.extra = links, by_rows, extra is not None
        hi = links.hi
        total_rows, tokens = pairs[0][0].shape
        self.block = total_rows // 4
        self.widths = [p[1].shape[1] for p in pairs]
        self.cols = sum(self.widths) + (extra.shape[1] if self.extra else 0)
        block, cols = self.block, self.cols
        self.cut = block // 2 if by_rows else -(-cols // 256) * 128

        def order(x):
            if hi == 1:
                return x
            return x.reshape(hi, 4, -1, x.shape[1]).swapaxes(0, 1).reshape(x.shape)

        which = lambda t, pq: ((pq[1] ^ ((t == 0) | (t == 3)).astype(jnp.int32)) * 2 + (pq[0] ^ (t < 2).astype(jnp.int32)), 0)
        args, specs = [], []
        for left, right, left_got, right_got in pairs:
            args += [order(left), right, order(left_got), right_got]
            l_spec = pl.BlockSpec((block, tokens), which)
            r_spec = pl.BlockSpec((tokens, right.shape[1]), lambda t, pq: (0, 0))
            specs += [l_spec, r_spec, l_spec, r_spec]
        if self.extra:
            args.append(order(extra))
            specs.append(pl.BlockSpec((block, extra.shape[1]), which))
        a_dims = (self.cut, cols) if by_rows else (block, self.cut)
        b_dims = (block - self.cut, cols) if by_rows else (block, cols - self.cut)
        self.dims = (a_dims, b_dims)
        out = lambda dims, f: pl.BlockSpec((1,) + dims, lambda t, pq: (f(t), 0, 0))
        one = lambda c: c.astype(jnp.int32)
        pq = jnp.stack([links.p, links.q]).astype(jnp.int32)
        self.a_send, self.a_keep, self.b_send, self.b_keep = pl.pallas_call(
            functools.partial(weight_kernel, len(pairs), self.extra, by_rows, self.cut),
            grid_spec=pltpu.PrefetchScalarGridSpec(
                num_scalar_prefetch=1,
                grid=(4,),
                in_specs=specs,
                out_specs=[
                    out(a_dims, lambda t: one(t == 0)),
                    out(a_dims, lambda t: one(t == 3)),
                    out(b_dims, lambda t: one(t == 0)),
                    out(b_dims, lambda t: one(t < 2)),
                ],
            ),
            out_shape=[shape(2, *a_dims)] * 2 + [shape(2, *b_dims)] * 2,
            cost_estimate=CHEAP,
            name="weight_grad",
        )(pq, *args)

    def start(self):
        self.a_got = self.links.flip(self.a_send, 2)
        self.b_got = self.links.flip(self.b_send, 4)

    def second(self, *deps):
        a_dims, b_dims = self.dims
        pick = lambda dims: pl.BlockSpec((1,) + dims, lambda i: (1, 0, 0))
        whole = lambda dims: pl.BlockSpec(dims, lambda i: (0, 0))
        a, b = pl.pallas_call(
            second_kernel,
            grid=(1,),
            in_specs=[pick(a_dims)] * 2 + [pick(b_dims)] * 2,
            out_specs=[whole(a_dims), whole(b_dims)],
            out_shape=[shape(*a_dims), shape(*b_dims)],
            cost_estimate=CHEAP,
            name="second",
        )(after(self.a_keep, *deps), self.a_got, self.b_keep, self.b_got)
        self.a_more = self.links.flip(a, 4)
        self.b_more = self.links.flip(b, 2)
        return a

    def third(self, *deps):
        links, nb = self.links, self.links.nb
        size = self.block // (links.hi * 2 * nb)
        self.size = size
        a_dims, b_dims = self.dims
        a_keep = after(self.a_keep, *deps)
        if links.hi > 1 or size % 8:
            a = a_keep[0].astype(F32) + self.a_got[0].astype(F32) + self.a_more.astype(F32)
            b = self.b_keep[0].astype(F32) + self.b_got[0].astype(F32) + self.b_more.astype(F32)
            held = jnp.concatenate([a, b], axis=0 if self.by_rows else 1)
            held = held.reshape(links.hi, 2 * nb * size, self.cols)
            total = take(held, links.h, 0)
            for s in range(1, links.hi):
                total = total + links.hi_shift(take(held, (links.h + s) % links.hi, 0).astype(BF16), s).astype(F32)
            held = total.reshape(2, nb, size, self.cols)
            pieces = [take(take(held, links.c ^ t, 0), (links.b + s) % nb, 0) for t, s in targets(nb)]
            self.own, sends = pieces[0], [x.astype(BF16) for x in pieces[1:]]
        else:
            pick = lambda dims: pl.BlockSpec((1,) + dims, lambda i: (0, 0, 0))
            whole = lambda dims: pl.BlockSpec(dims, lambda i: (0, 0))
            scalar = lambda x: x.astype(jnp.int32).reshape(1)
            *sends, self.own = pl.pallas_call(
                functools.partial(third_kernel, nb, size, self.by_rows, self.cut),
                grid=(1,),
                in_specs=[SM, SM] + [pick(a_dims)] * 2 + [whole(a_dims)] + [pick(b_dims)] * 2 + [whole(b_dims)],
                out_specs=[whole((size, self.cols))] * (2 * nb),
                out_shape=[shape(size, self.cols)] * (2 * nb - 1) + [shape(size, self.cols, dtype=F32)],
                scratch_shapes=[pltpu.VMEM((self.block, self.cols), F32)],
                cost_estimate=CHEAP,
                name="third",
            )(
                scalar(links.c), scalar(links.b), a_keep, self.a_got, self.a_more,
                self.b_keep, self.b_got, self.b_more,
            )
        self.gots = [links.both_shift(x, t, s) for x, (t, s) in zip(sends, targets(nb)[1:])]
        return self.own

    def last(self, *deps):
        links, nb, size = self.links, self.links.nb, self.size
        outs = [shape(size, 2 * w, dtype=F32) for w in self.widths]
        if self.extra:
            outs.append(shape(size, COLS, dtype=F32))
        return pl.pallas_call(
            functools.partial(last_kernel, nb, self.widths, self.extra),
            in_specs=[SM] + [VM] * (2 * nb),
            out_specs=[VM] * len(outs),
            out_shape=outs,
            cost_estimate=CHEAP,
            name="last",
        )(links.c.astype(jnp.int32).reshape(1), after(self.own, *deps), *self.gots)


def per_device(
    inputs, keep_mask, crop_rows, crop_cols, gain_one, shift_one, w_query, b_query, w_key, w_value,
    b_value, w_out, b_out, gain_two, shift_two, w_up, b_up, w_down, b_down, cotangent, *, n_img, nb,
):
    images, rows, width = inputs.shape
    hidden_width = w_up.shape[1]
    assert images == nb
    tokens = nb * rows
    links = Links(n_img, nb)
    core = links.c.astype(jnp.int32).reshape(1)
    f = lambda v: v.astype(F32)
    position = links.b * rows + jnp.arange(rows, dtype=jnp.int32)
    inside = (
        (keep_mask > 0)
        & (position[None, :] // SIDE < crop_rows[:, None])
        & (position[None, :] % SIDE < crop_cols[:, None])
    )
    flags = jnp.tile(inside.astype(BF16), (1, nb))[:, None, :]
    slot_of = jnp.arange(tokens, dtype=jnp.int32) // rows
    flags = jnp.where(jnp.arange(8)[None, :, None] == slot_of[None, None, :], flags, jnp.zeros((), BF16))
    flags = jnp.pad(flags, ((0, 0), (0, 0), (0, width - tokens)))
    packed = jnp.concatenate([inputs, flags], axis=1)
    slots = links.scatter_in(packed)
    later = lax.optimization_barrier((cotangent, slots[nb - 1], slots[1], slots[2 % nb]))
    cots = links.scatter_in(later[0])
    vec = jnp.stack([f(t) for t in (gain_one, shift_one, b_query, b_value, b_out, gain_two, shift_two, b_down)])
    b_up_row = f(b_up)[None, :]

    full = shape(tokens, width)
    tall_t = shape(width, tokens)
    normed_t, q, k, v, attended_t, middle, two, two_t, mask = pl.pallas_call(
        functools.partial(attend_kernel, rows, nb),
        in_specs=[VM] * (nb + 5),
        out_specs=[VM] * 9,
        out_shape=[tall_t] + [full] * 3 + [tall_t, shape(tokens, width, dtype=F32), full, tall_t, shape(8, tokens, dtype=F32)],
        scratch_shapes=[pltpu.VMEM((tokens, width), BF16), pltpu.VMEM((width, tokens), BF16)],
        cost_estimate=CHEAP,
        name="attend",
    )(*slots, vec, w_query, w_key, w_value, w_out)

    attended_got = links.flip(attended_t, 1)
    normed_got = links.flip(normed_t, 1)
    two_got = links.flip(two_t, 1)

    steps = 4
    block = hidden_width // steps
    half = width // 2
    fixed = lambda *dims: pl.BlockSpec(dims, lambda j, c: (0,) * len(dims))
    tall = lambda *dims: pl.BlockSpec(dims, lambda j, c: (0, j))
    up = pl.pallas_call(
        functools.partial(up_kernel, rows, nb, steps),
        grid_spec=pltpu.PrefetchScalarGridSpec(
            num_scalar_prefetch=1,
            grid=(steps,),
            in_specs=[
                fixed(tokens, width), fixed(tokens, width), fixed(8, tokens), fixed(8, width),
                tall(width, block), tall(1, block),
                pl.BlockSpec((block, width), lambda j, c: (j, 0)),
            ] + [fixed(rows, width)] * nb,
            out_specs=[
                pl.BlockSpec((block, tokens), lambda j, c: (j, 0)), tall(tokens, block), fixed(tokens, width),
                fixed(tokens, half), fixed(tokens, half),
            ] + [fixed(rows, width)] * nb,
            scratch_shapes=[pltpu.VMEM((tokens, width), F32)],
        ),
        out_shape=[
            shape(hidden_width, tokens), shape(tokens, hidden_width, dtype=F32), full,
            shape(tokens, half), shape(tokens, half),
        ] + [shape(rows, width)] * nb,
        cost_estimate=CHEAP,
        name="up",
    )(core, two, middle, mask, vec, w_up, b_up_row, w_down, *cots)
    activated_t, slope, grad_down, gd_keep, gd_send = up[:5]
    out_slots = up[5:]
    act_got = links.flip(activated_t, 1)
    gd_got = links.flip(gd_send, 1)
    output = links.scatter_back(out_slots)

    def halves(sending):
        offset = lambda c: 2 * (1 - c[0]) if sending else 2 * c[0]
        wide = lambda *dims: pl.BlockSpec(dims, lambda j, c: (0, j + offset(c)))
        return [
            fixed(tokens, width), wide(tokens, block), wide(width, block),
            pl.BlockSpec((block, width), lambda j, c: (j + offset(c), 0)),
        ]

    gh_send, send_sum, before = pl.pallas_call(
        down_send_kernel,
        grid_spec=pltpu.PrefetchScalarGridSpec(
            num_scalar_prefetch=1,
            grid=(steps // 2,),
            in_specs=halves(True),
            out_specs=[tall(tokens, block), tall(8, block), fixed(tokens, width)],
        ),
        out_shape=[
            shape(tokens, hidden_width // 2), shape(8, hidden_width // 2, dtype=F32),
            shape(tokens, width, dtype=F32),
        ],
        cost_estimate=CHEAP,
        name="down_send",
    )(core, grad_down, slope, w_up, w_down)
    gh_got = links.flip(gh_send, 1)

    unit_down = Unit(links, [(after(activated_t, before), gd_keep, act_got, gd_got)], by_rows=True)
    unit_down.start()

    gh_keep, keep_sum, grad_middle, grad_branch, gb_keep, gb_send, down_sums = pl.pallas_call(
        functools.partial(down_keep_kernel, rows, nb, steps // 2),
        grid_spec=pltpu.PrefetchScalarGridSpec(
            num_scalar_prefetch=1,
            grid=(steps // 2,),
            in_specs=halves(False)
            + [fixed(tokens, width), fixed(tokens, width), fixed(8, tokens), fixed(8, width)]
            + [fixed(rows, width)] * nb,
            out_specs=[
                tall(tokens, block), tall(8, block), fixed(tokens, width), fixed(tokens, width),
                fixed(tokens, half), fixed(tokens, half), fixed(8, width),
            ],
            scratch_shapes=[pltpu.VMEM((tokens, width), F32)],
        ),
        out_shape=[
            shape(tokens, hidden_width // 2), shape(8, hidden_width // 2, dtype=F32),
            shape(tokens, width, dtype=F32), full, shape(tokens, half), shape(tokens, half),
            shape(8, width, dtype=F32),
        ],
        cost_estimate=CHEAP,
        name="down_keep",
    )(core, after(grad_down, unit_down.a_send), slope, w_up, w_down, before, middle, mask, vec, *cots)
    gb_got = links.flip(gb_send, 1)

    unit_up = Unit(
        links, [(two_t, gh_keep, two_got, gh_got), (attended_t, gb_keep, attended_got, gb_got)]
    )
    unit_up.start()

    low = lambda: pltpu.VMEM((width, tokens), BF16)
    qkv_keep, qkv_send, gq, gk, gv, attend_sums = pl.pallas_call(
        attend_back_kernel,
        in_specs=[SM] + [VM] * 6,
        out_specs=[VM] * 6,
        out_shape=[shape(tokens, 3 * half)] * 2 + [full] * 3 + [shape(8, width, dtype=F32)],
        scratch_shapes=[
            pltpu.VMEM((tokens, width), BF16), low(), low(), low(), low(),
            pltpu.VMEM((width, tokens), F32), pltpu.VMEM((width, tokens), F32),
        ],
        cost_estimate=CHEAP,
        name="attend_back",
    )(core, after(grad_branch, unit_up.a_send), q, k, v, mask, w_out)
    qkv_got = links.flip(qkv_send, 1)

    mark = unit_down.second(attend_sums)

    first = jnp.where(links.c == 0, keep_sum[0], send_sum[0])
    other = jnp.where(links.c == 0, send_sum[0], keep_sum[0])
    up_cols = jnp.concatenate([first, other]).reshape(width, hidden_width // width)
    up_cols = jnp.pad(up_cols, ((0, 0), (18, COLS - 18 - hidden_width // width)))
    back = pl.pallas_call(
        functools.partial(input_back_kernel, rows, nb),
        in_specs=[VM] * (nb + 11),
        out_specs=[VM] * (nb + 1),
        out_shape=[shape(rows, width)] * nb + [shape(width, COLS, dtype=F32)],
        cost_estimate=CHEAP,
        name="input_back",
    )(
        *slots, after(gq, mark), gk, gv, w_query, w_key, w_value, grad_middle, vec, down_sums, attend_sums, up_cols,
    )
    unit_qkv = Unit(links, [(normed_t, qkv_keep, normed_got, qkv_got)], extra=back[nb])
    unit_qkv.widths = [half] * 3
    unit_qkv.start()
    grad_inputs = links.scatter_back(back[:nb])

    mark = unit_up.second(unit_qkv.a_send)
    mark = unit_down.third(mark)
    output = after(output, mark)
    mark = unit_qkv.second(mark)
    mark = unit_up.third(mark)
    (g_w_down,) = unit_down.last(mark)
    mark = unit_qkv.third(g_w_down)
    g_w_up, g_w_out = unit_up.last(mark)
    g_w_query, g_w_key, g_w_value, cols = unit_qkv.last(g_w_up)
    sums = [cols[:, i] for i in range(18)]
    g_b_up = cols[:, 18 : 18 + hidden_width // width].reshape(-1)
    return (
        output.reshape(inputs.shape),
        grad_inputs.astype(F32).reshape(inputs.shape),
        sums[16],
        sums[17],
        g_w_query,
        sums[8],
        g_w_key,
        g_w_value,
        sums[9],
        g_w_out,
        sums[2],
        sums[0],
        sums[1],
        g_w_up,
        g_b_up,
        g_w_down,
        sums[3],
    )


def solution(mesh):
    n_img, nb = mesh.shape["img"], mesh.shape["band"]

    def body(*args):
        return per_device(*args, n_img=n_img, nb=nb)

    both = P(("img", "band"))
    rows = P(("img", "band"), None)
    token = P("img", "band", None)
    return jax.shard_map(
        body,
        mesh=mesh,
        in_specs=(token, P("img", "band"), P("img"), P("img")) + (P(),) * 15 + (token,),
        out_specs=(
            token, token, both, both, rows, both, rows, rows, both, rows, both, both, both, rows, both,
            rows, both,
        ),
        check_vma=False,
    )
```

profile of v0, /device:TPU:0, one launch (start us, length us, event | category | flops | bytes accessed | tf_op | source)
XLA Modules:
  0.0 207.7 jit_solution(4293119170455640500)
XLA Ops:
  3.5 3.1 %collective-permute-start = (bf16[72,768]{1,0:T(8,128)(2,1)S(1)}, bf16[72,768]{1,0:T(8,128)(2,1)S(1)}, u32[]{:S(2)}, u32[]{:S(2)}) collective-permute-start(bf16[72,768]{1,0:T(8,128)(2,1)S(1)} %get-tuple-element.233), channel_id=1, source_target_pairs={{0,1},{1,2},{2,3},{3,0},{4,5},{5,6},{6,7},{7,4},{8,9},{9,10},{10,1... | collective-permute-start | bytes 331784 | tf_op jit(solution)/shard_map/ppermute | solution.py:396
  6.6 2.6 %collective-permute-start.1 = (bf16[72,768]{1,0:T(8,128)(2,1)S(1)}, bf16[72,768]{1,0:T(8,128)(2,1)S(1)}, u32[]{:S(2)}, u32[]{:S(2)}) collective-permute-start(bf16[72,768]{1,0:T(8,128)(2,1)S(1)} %get-tuple-element.232), channel_id=1, source_target_pairs={{0,2},{1,3},{2,0},{3,1},{4,6},{5,7},{6,4},{7,5},{8,10},{9,11},{10,... | collective-permute-start | bytes 331784 | tf_op jit(solution)/shard_map/ppermute | solution.py:396
  12.6 3.9 %collective-permute-done.1.refs_2_ = bf16[72,768]{1,0:T(8,128)(2,1)S(1)} collective-permute-done((bf16[72,768]{1,0:T(8,128)(2,1)S(1)}, bf16[72,768]{1,0:T(8,128)(2,1)S(1)}, u32[]{:S(2)}, u32[]{:S(2)}) %collective-permute-start.1) | collective-permute-done | bytes 110624 | tf_op jit(solution)/shard_map/ppermute | solution.py:396
  17.2 2.8 %collective-permute-start.3 = (bf16[64,768]{1,0:T(8,128)(2,1)S(1)}, bf16[64,768]{1,0:T(8,128)(2,1)S(1)}, u32[]{:S(2)}, u32[]{:S(2)}) collective-permute-start(bf16[64,768]{1,0:T(8,128)(2,1)S(1)} %get-tuple-element.237), channel_id=1, source_target_pairs={{0,1},{1,2},{2,3},{3,0},{4,5},{5,6},{6,7},{7,4},{8,9},{9,10},{10,1... | collective-permute-start | bytes 294920 | tf_op jit(solution)/shard_map/ppermute | solution.py:396
  23.8 8.8 %attend.1 = (bf16[768,256]{1,0:T(8,128)(2,1)}, bf16[256,768]{1,0:T(8,128)(2,1)}, bf16[256,768]{1,0:T(8,128)(2,1)}, bf16[256,768]{1,0:T(8,128)(2,1)}, bf16[768,25...) custom-call(bf16[72,768]{1,0:T(8,128)(2,1)} %get-tuple-element.234.r, ...), custom_call_target="tpu_custom_call" | custom-call | flops 1000 | bytes 1000 | tf_op jit(solution)/shard_map/attend/pallas_call | solution.py:575
  33.3 9.4 %up.1 = (bf16[3072,256]{1,0:T(8,128)(2,1)}, f32[256,3072]{1,0:T(8,128)}, bf16[256,768]{1,0:T(8,128)(2,1)}, bf16[256,384]{1,0:T(8,128)(2,1)}, bf16[256,384]{1,0:T...) custom-call(s32[1]{0:T(128)} %bitcast.core, ...), custom_call_target="tpu_custom_call" | custom-call | flops 1000 | bytes 1000 | tf_op jit(solution)/shard_map/up/pallas_call | solution.py:594
  48.0 5.3 %down_send.1 = (bf16[256,1536]{1,0:T(8,128)(2,1)}, f32[8,1536]{1,0:T(8,128)}, f32[256,768]{1,0:T(8,128)}) custom-call(s32[1]{0:T(128)} %bitcast.core, bf16[256,768]{1,0:T(8,128)(2,1)} %get-tuple-element.137.gd.refs_0_, f32[256,3072]{1,0:T(8,128)} %get-tuple-element.129.slope.refs_1_, bf16[768,3072]{1,0:T(8,128)(2,1)} %refs_2_.1, bf16[3072,768]{1,0:T(8,128)(2,1)} %refs_3_.1), custom_call_target="tpu_custom_call" | custom-call | flops 1000 | bytes 1000 | tf_op jit(solution)/shard_map/down_send/pallas_call | solution.py:631
  54.8 5.5 %collective-permute-done.7 = bf16[64,768]{1,0:T(8,128)(2,1)S(1)} collective-permute-done((bf16[64,768]{1,0:T(8,128)(2,1)S(1)}, bf16[64,768]{1,0:T(8,128)(2,1)S(1)}, u32[]{:S(2)}, u32[]{:S(2)}) %collective-permute-start.7) | collective-permute-done | bytes 98336 | tf_op jit(solution)/shard_map/ppermute | solution.py:396
  60.9 5.8 %collective-permute-done.8 = bf16[64,768]{1,0:T(8,128)(2,1)S(1)} collective-permute-done((bf16[64,768]{1,0:T(8,128)(2,1)S(1)}, bf16[64,768]{1,0:T(8,128)(2,1)S(1)}, u32[]{:S(2)}, u32[]{:S(2)}) %collective-permute-start.8) | collective-permute-done | bytes 98336 | tf_op jit(solution)/shard_map/ppermute | solution.py:396
  69.3 6.4 %weight_grad.3 = (bf16[2,384,384]{2,1,0:T(8,128)(2,1)}, bf16[2,384,384]{2,1,0:T(8,128)(2,1)}, bf16[2,384,384]{2,1,0:T(8,128)(2,1)}, bf16[2,384,384]{2,1,0:T(8,128)(2,1)}) custom-call(s32[2]{0:T(128)} %pad_add_fusion.place, bf16[3072,256]{1,0:T(8,128)(2,1)} %get-tuple-element.131.refs_0_, bf16[256,384]{1,0:T(8,128)(2,1)} %get-tuple-element.132.refs_1_, ...), custom_call_target="tpu_custom_call" | custom-call | flops 1000 | bytes 1000 | tf_op jit(solution)/shard_map/weight_grad/pallas_call | solution.py:454
  77.8 7.0 %down_keep.1 = (bf16[256,1536]{1,0:T(8,128)(2,1)}, f32[8,1536]{1,0:T(8,128)}, f32[256,768]{1,0:T(8,128)}, bf16[256,768]{1,0:T(8,128)(2,1)}, bf16[256,384]{1,0:T(...) custom-call(s32[1]{0:T(128)} %bitcast.core, bf16[256,768]{1,0:T(8,128)(2,1)} %get-tuple-element.137.gd.refs_0_, ...), custom_call_target="tpu_custom_call" | custom-call | flops 1000 | bytes 1000 | tf_op jit(solution)/shard_map/down_keep/pallas_call | solution.py:651
  89.0 7.0 %weight_grad.4 = (bf16[2,192,1024]{2,1,0:T(8,128)(2,1)}, bf16[2,192,1024]{2,1,0:T(8,128)(2,1)}, bf16[2,192,896]{2,1,0:T(8,128)(2,1)}, bf16[2,192,896]{2,1,0:T(8,128)(2,1)}) custom-call(s32[2]{0:T(128)} %pad_add_fusion.place, bf16[768,256]{1,0:T(8,128)(2,1)} %get-tuple-element.135.refs_0_, bf16[256,1536]{1,0:T(8,128)(2,1)} %get-tuple-element.138.refs_1_, ...), custom_call_target="tpu_custom_call" | custom-call | flops 1000 | bytes 1000 | tf_op jit(solution)/shard_map/weight_grad/pallas_call | solution.py:454
  95.9 10.8 %attend_back.1 = (bf16[256,1152]{1,0:T(8,128)(2,1)}, bf16[256,1152]{1,0:T(8,128)(2,1)}, bf16[256,768]{1,0:T(8,128)(2,1)}, bf16[256,768]{1,0:T(8,128)(2,1)}, bf16[256,768]{1,0:T(8,128)(2,1)}, /*index=5*/f32[8,768]{1,0:T(8,128)}) custom-call(s32[1]{0:T(128)} %bitcast.core, bf16[256,768]{1,0:T(8,128)(2,1)} %get-tuple-element.147.gb, ...), custom_call_target="tpu_custom_call" | custom-call | flops 1000 | bytes 1000 | tf_op jit(solution)/shard_map/attend_back/pallas_call | solution.py:681
  115.4 5.1 %input_back.1 = (bf16[64,768]{1,0:T(8,128)(2,1)}, bf16[64,768]{1,0:T(8,128)(2,1)}, bf16[64,768]{1,0:T(8,128)(2,1)}, bf16[64,768]{1,0:T(8,128)(2,1)}, f32[768,128]{1,0:T(8,128)}) custom-call(bf16[72,768]{1,0:T(8,128)(2,1)} %get-tuple-element.234.refs_0_, bf16[72,768]{1,0:T(8,128)(2,1)} %copy-done.8, bf16[72,768]{1,0:T(8,128)(2,1)} %copy-done.9, ...), custom_call_target="tpu_custom_call" | custom-call | flops 1000 | bytes 1000 | tf_op jit(solution)/shard_map/input_back/pallas_call | solution.py:701
  120.7 6.0 %weight_grad.5 = (bf16[2,192,640]{2,1,0:T(8,128)(2,1)}, bf16[2,192,640]{2,1,0:T(8,128)(2,1)}, bf16[2,192,640]{2,1,0:T(8,128)(2,1)}, bf16[2,192,640]{2,1,0:T(8,128)(2,1)}) custom-call(s32[2]{0:T(128)} %pad_add_fusion.place, bf16[768,256]{1,0:T(8,128)(2,1)} %get-tuple-element.144.refs_0_, bf16[256,1152]{1,0:T(8,128)(2,1)} %get-tuple-element.151.refs_1_, ...), custom_call_target="tpu_custom_call" | custom-call | flops 1000 | bytes 1000 | tf_op jit(solution)/shard_map/weight_grad/pallas_call | solution.py:454
  140.5 5.7 %collective-permute-done.22.b_more = bf16[384,384]{1,0:T(8,128)(2,1)S(1)} collective-permute-done((bf16[384,384]{1,0:T(8,128)(2,1)}, bf16[384,384]{1,0:T(8,128)(2,1)S(1)}, u32[]{:S(2)}, u32[]{:S(2)}) %collective-permute-start.22) | collective-permute-done | bytes 294944 | tf_op jit(solution)/shard_map/ppermute | solution.py:393
  147.8 2.5 %third.3 = (bf16[96,384]{1,0:T(8,128)(2,1)}, bf16[96,384]{1,0:T(8,128)(2,1)}, bf16[96,384]{1,0:T(8,128)(2,1)}, bf16[96,384]{1,0:T(8,128)(2,1)}, bf16[96,384]{1,0...) custom-call(s32[1]{0:T(128)} %bitcast.core, s32[1]{0:T(128)} %bitcast.14.band, ...), custom_call_target="tpu_custom_call" | custom-call | flops 1000 | bytes 1000 | tf_op jit(solution)/shard_map/third/pallas_call | solution.py:514
  152.1 2.6 %collective-permute-start.31 = (bf16[96,384]{1,0:T(8,128)(2,1)}, bf16[96,384]{1,0:T(8,128)(2,1)S(1)}, u32[]{:S(2)}, u32[]{:S(2)}) collective-permute-start(bf16[96,384]{1,0:T(8,128)(2,1)} %get-tuple-element.190), channel_id=1, source_target_pairs={{0,2},{1,3},{2,0},{3,1},{4,6},{5,7},{6,4},{7,5},{8,10},{9,11},{10,... | collective-permute-start | bytes 221192 | tf_op jit(solution)/shard_map/ppermute | solution.py:419
  166.8 2.9 %third.4 = (bf16[24,1920]{1,0:T(8,128)(2,1)}, bf16[24,1920]{1,0:T(8,128)(2,1)}, bf16[24,1920]{1,0:T(8,128)(2,1)}, bf16[24,1920]{1,0:T(8,128)(2,1)}, bf16[24,1920...) custom-call(s32[1]{0:T(128)} %bitcast.core, s32[1]{0:T(128)} %bitcast.14.band, ...), custom_call_target="tpu_custom_call" | custom-call | flops 1000 | bytes 1000 | tf_op jit(solution)/shard_map/third/pallas_call | solution.py:514
  171.1 2.8 %collective-permute-start.41 = (bf16[24,1920]{1,0:T(8,128)(2,1)}, bf16[24,1920]{1,0:T(8,128)(2,1)S(1)}, u32[]{:S(2)}, u32[]{:S(2)}) collective-permute-start(bf16[24,1920]{1,0:T(8,128)(2,1)} %get-tuple-element.202), channel_id=1, source_target_pairs={{0,3},{1,0},{2,1},{3,2},{4,7},{5,4},{6,5},{7,6},{8,11},{9,8},{10,9... | collective-permute-start | bytes 276488 | tf_op jit(solution)/shard_map/ppermute | solution.py:419
  177.3 2.5 %third.5 = (bf16[24,1280]{1,0:T(8,128)(2,1)}, bf16[24,1280]{1,0:T(8,128)(2,1)}, bf16[24,1280]{1,0:T(8,128)(2,1)}, bf16[24,1280]{1,0:T(8,128)(2,1)}, bf16[24,1280...) custom-call(s32[1]{0:T(128)} %bitcast.core, s32[1]{0:T(128)} %bitcast.14.band, ...), custom_call_target="tpu_custom_call" | custom-call | flops 1000 | bytes 1000 | tf_op jit(solution)/shard_map/third/pallas_call | solution.py:514
  185.7 2.8 %collective-permute-start.48 = (bf16[24,1280]{1,0:T(8,128)(2,1)}, bf16[24,1280]{1,0:T(8,128)(2,1)S(1)}, u32[]{:S(2)}, u32[]{:S(2)}) collective-permute-start(bf16[24,1280]{1,0:T(8,128)(2,1)} %get-tuple-element.211), channel_id=1, source_target_pairs={{0,3},{1,0},{2,1},{3,2},{4,7},{5,4},{6,5},{7,6},{8,11},{9,8},{10,9... | collective-permute-start | bytes 184328 | tf_op jit(solution)/shard_map/ppermute | solution.py:419
  188.6 4.4 %collective-permute-start.50 = (bf16[24,1280]{1,0:T(8,128)(2,1)}, bf16[24,1280]{1,0:T(8,128)(2,1)S(1)}, u32[]{:S(2)}, u32[]{:S(2)}) collective-permute-start(bf16[24,1280]{1,0:T(8,128)(2,1)} %get-tuple-element.213), channel_id=1, source_target_pairs={{0,5},{1,6},{2,7},{3,4},{4,1},{5,2},{6,3},{7,0},{8,13},{9,14},{10,... | collective-permute-start | bytes 184328 | tf_op jit(solution)/shard_map/ppermute | solution.py:419
  193.0 2.5 %collective-permute-start.51 = (bf16[24,1280]{1,0:T(8,128)(2,1)}, bf16[24,1280]{1,0:T(8,128)(2,1)S(1)}, u32[]{:S(2)}, u32[]{:S(2)}) collective-permute-start(bf16[24,1280]{1,0:T(8,128)(2,1)} %get-tuple-element.214), channel_id=1, source_target_pairs={{0,6},{1,7},{2,4},{3,5},{4,2},{5,3},{6,0},{7,1},{8,14},{9,15},{10,... | collective-permute-start | bytes 184328 | tf_op jit(solution)/shard_map/ppermute | solution.py:419
  (277 shorter events, 88.0 us)
Async XLA Ops:
  17.2 15.4 %collective-permute-start.3 = (bf16[64,768]{1,0:T(8,128)(2,1)S(1)}, bf16[64,768]{1,0:T(8,128)(2,1)S(1)}, u32[]{:S(2)}, u32[]{:S(2)}) collective-permute-start(bf16[64,768]{1,0:T(8,128)(2,1)S(1)} %get-tuple-element.237), channel_id=1, source_target_pairs={{0,1},{1,2},{2,3},{3,0},{4,5},{5,6},{6,7},{7,4},{8,9},{9,10},{10,1... | collective-permute-start | bytes 294920 | tf_op jit(solution)/shard_map/ppermute | solution.py:396
  20.0 12.6 %collective-permute-start.4 = (bf16[64,768]{1,0:T(8,128)(2,1)S(1)}, bf16[64,768]{1,0:T(8,128)(2,1)S(1)}, u32[]{:S(2)}, u32[]{:S(2)}) collective-permute-start(bf16[64,768]{1,0:T(8,128)(2,1)S(1)} %get-tuple-element.236), channel_id=1, source_target_pairs={{0,2},{1,3},{2,0},{3,1},{4,6},{5,7},{6,4},{7,5},{8,10},{9,11},{10,... | collective-permute-start | bytes 294920 | tf_op jit(solution)/shard_map/ppermute | solution.py:396
  42.7 25.3 %collective-permute-start.9 = (bf16[3072,256]{1,0:T(8,128)(2,1)}, bf16[3072,256]{1,0:T(8,128)(2,1)S(1)}, u32[]{:S(2)}, u32[]{:S(2)}) collective-permute-start(bf16[3072,256]{1,0:T(8,128)(2,1)} %get-tuple-element.131.refs_0_), channel_id=1, source_target_pairs={{0,4},{4,0},{8,12},{12,8},{16,20},{20,16},{24,28},{28,24},{1,5},{5... | collective-permute-start | bytes 4718600 | tf_op jit(solution)/shard_map/ppermute | solution.py:393
  43.4 42.3 %collective-permute-start.11 = (bf16[768,256]{1,0:T(8,128)(2,1)}, bf16[768,256]{1,0:T(8,128)(2,1)S(1)}, u32[]{:S(2)}, u32[]{:S(2)}) collective-permute-start(bf16[768,256]{1,0:T(8,128)(2,1)} %get-tuple-element.135.refs_0_), channel_id=1, source_target_pairs={{0,4},{4,0},{8,12},{12,8},{16,20},{20,16},{24,28},{28,24},{1,5},{5... | collective-permute-start | bytes 1179656 | tf_op jit(solution)/shard_map/ppermute | solution.py:393
  43.9 42.2 %collective-permute-start.13 = (bf16[768,256]{1,0:T(8,128)(2,1)}, bf16[768,256]{1,0:T(8,128)(2,1)}, u32[]{:S(2)}, u32[]{:S(2)}) collective-permute-start(bf16[768,256]{1,0:T(8,128)(2,1)} %get-tuple-element.140.refs_4_), channel_id=1, source_target_pairs={{0,4},{4,0},{8,12},{12,8},{16,20},{20,16},{24,28},{28,24},{1,5},{5... | collective-permute-start | bytes 1179656 | tf_op jit(solution)/shard_map/ppermute | solution.py:393
  44.0 24.1 %collective-permute-start.10 = (bf16[256,384]{1,0:T(8,128)(2,1)}, bf16[256,384]{1,0:T(8,128)(2,1)S(1)}, u32[]{:S(2)}, u32[]{:S(2)}) collective-permute-start(bf16[256,384]{1,0:T(8,128)(2,1)} %get-tuple-element.133), channel_id=1, source_target_pairs={{0,4},{4,0},{8,12},{12,8},{16,20},{20,16},{24,28},{28,24},{1,5},{5... | collective-permute-start | bytes 589832 | tf_op jit(solution)/shard_map/ppermute | solution.py:393
  66.7 21.3 %collective-permute-start.12 = (bf16[256,1536]{1,0:T(8,128)(2,1)}, bf16[256,1536]{1,0:T(8,128)(2,1)S(1)}, u32[]{:S(2)}, u32[]{:S(2)}) collective-permute-start(bf16[256,1536]{1,0:T(8,128)(2,1)} %get-tuple-element.139), channel_id=1, source_target_pairs={{0,4},{4,0},{8,12},{12,8},{16,20},{20,16},{24,28},{28,24},{1,5},{5... | collective-permute-start | bytes 2359304 | tf_op jit(solution)/shard_map/ppermute | solution.py:393
  75.6 32.4 %collective-permute-start.17 = (bf16[2,384,384]{2,1,0:T(8,128)(2,1)}, bf16[2,384,384]{2,1,0:T(8,128)(2,1)S(1)}, u32[]{:S(2)}, u32[]{:S(2)}) collective-permute-start(bf16[2,384,384]{2,1,0:T(8,128)(2,1)} %get-tuple-element.136), channel_id=1, source_target_pairs={{0,8},{4,12},{8,0},{12,4},{16,24},{20,28},{24,16},{28,20},{1,9},{5... | collective-permute-start | bytes 1769480 | tf_op jit(solution)/shard_map/ppermute | solution.py:393
  85.7 34.9 %collective-permute-start.15 = (bf16[768,256]{1,0:T(8,128)(2,1)}, bf16[768,256]{1,0:T(8,128)(2,1)}, u32[]{:S(2)}, u32[]{:S(2)}) collective-permute-start(bf16[768,256]{1,0:T(8,128)(2,1)} %get-tuple-element.144.refs_0_), channel_id=1, source_target_pairs={{0,4},{4,0},{8,12},{12,8},{16,20},{20,16},{24,28},{28,24},{1,5},{5... | collective-permute-start | bytes 1179656 | tf_op jit(solution)/shard_map/ppermute | solution.py:393
  86.5 26.0 %collective-permute-start.18 = (bf16[2,384,384]{2,1,0:T(8,128)(2,1)}, bf16[2,384,384]{2,1,0:T(8,128)(2,1)S(1)}, u32[]{:S(2)}, u32[]{:S(2)}) collective-permute-start(bf16[2,384,384]{2,1,0:T(8,128)(2,1)} %get-tuple-element.157), channel_id=1, source_target_pairs={{0,16},{4,20},{8,24},{12,28},{16,0},{20,4},{24,8},{28,12},{1,17},{... | collective-permute-start | bytes 1769480 | tf_op jit(solution)/shard_map/ppermute | solution.py:393
  106.8 13.9 %collective-permute-start.16 = (bf16[256,1152]{1,0:T(8,128)(2,1)}, bf16[256,1152]{1,0:T(8,128)(2,1)}, u32[]{:S(2)}, u32[]{:S(2)}) collective-permute-start(bf16[256,1152]{1,0:T(8,128)(2,1)} %get-tuple-element.152), channel_id=1, source_target_pairs={{0,4},{4,0},{8,12},{12,8},{16,20},{20,16},{24,28},{28,24},{1,5},{5... | collective-permute-start | bytes 1769480 | tf_op jit(solution)/shard_map/ppermute | solution.py:393
  106.8 24.1 %collective-permute-start.20 = (bf16[2,192,896]{2,1,0:T(8,128)(2,1)}, bf16[2,192,896]{2,1,0:T(8,128)(2,1)S(1)}, u32[]{:S(2)}, u32[]{:S(2)}) collective-permute-start(bf16[2,192,896]{2,1,0:T(8,128)(2,1)} %get-tuple-element.170), channel_id=1, source_target_pairs={{0,16},{4,20},{8,24},{12,28},{16,0},{20,4},{24,8},{28,12},{1,17},{... | collective-permute-start | bytes 2064392 | tf_op jit(solution)/shard_map/ppermute | solution.py:393
  108.0 24.2 %collective-permute-start.19 = (bf16[2,192,1024]{2,1,0:T(8,128)(2,1)}, bf16[2,192,1024]{2,1,0:T(8,128)(2,1)S(1)}, u32[]{:S(2)}, u32[]{:S(2)}) collective-permute-start(bf16[2,192,1024]{2,1,0:T(8,128)(2,1)} %get-tuple-element.146), channel_id=1, source_target_pairs={{0,8},{4,12},{8,0},{12,4},{16,24},{20,28},{24,16},{28,20},{1,9},{5... | collective-permute-start | bytes 2359304 | tf_op jit(solution)/shard_map/ppermute | solution.py:393
  126.7 25.3 %collective-permute-start.26 = (bf16[2,192,640]{2,1,0:T(8,128)(2,1)}, bf16[2,192,640]{2,1,0:T(8,128)(2,1)S(1)}, u32[]{:S(2)}, u32[]{:S(2)}) collective-permute-start(bf16[2,192,640]{2,1,0:T(8,128)(2,1)} %get-tuple-element.167), channel_id=1, source_target_pairs={{0,8},{4,12},{8,0},{12,4},{16,24},{20,28},{24,16},{28,20},{1,9},{5... | collective-permute-start | bytes 1474568 | tf_op jit(solution)/shard_map/ppermute | solution.py:393
  130.4 15.8 %collective-permute-start.22 = (bf16[384,384]{1,0:T(8,128)(2,1)}, bf16[384,384]{1,0:T(8,128)(2,1)S(1)}, u32[]{:S(2)}, u32[]{:S(2)}) collective-permute-start(bf16[384,384]{1,0:T(8,128)(2,1)} %get-tuple-element.173), channel_id=1, source_target_pairs={{0,8},{4,12},{8,0},{12,4},{16,24},{20,28},{24,16},{28,20},{1,9},{5... | collective-permute-start | bytes 884744 | tf_op jit(solution)/shard_map/ppermute | solution.py:393
  131.0 24.4 %collective-permute-start.27 = (bf16[2,192,640]{2,1,0:T(8,128)(2,1)}, bf16[2,192,640]{2,1,0:T(8,128)(2,1)S(1)}, u32[]{:S(2)}, u32[]{:S(2)}) collective-permute-start(bf16[2,192,640]{2,1,0:T(8,128)(2,1)} %get-tuple-element.183), channel_id=1, source_target_pairs={{0,16},{4,20},{8,24},{12,28},{16,0},{20,4},{24,8},{28,12},{1,17},{... | collective-permute-start | bytes 1474568 | tf_op jit(solution)/shard_map/ppermute | solution.py:393
  132.2 18.1 %collective-permute-start.25 = (bf16[64,768]{1,0:T(8,128)(2,1)S(1)}, bf16[64,768]{1,0:T(8,128)(2,1)S(1)}, u32[]{:S(2)}, u32[]{:S(2)}) collective-permute-start(bf16[64,768]{1,0:T(8,128)(2,1)S(1)} %copy-done.56), channel_id=1, source_target_pairs={{0,1},{1,2},{2,3},{3,0},{4,5},{5,6},{6,7},{7,4},{8,9},{9,10},{10,1... | collective-permute-start | bytes 294920 | tf_op jit(solution)/shard_map/ppermute | solution.py:396
  139.0 26.2 %collective-permute-start.28 = (bf16[192,1024]{1,0:T(8,128)(2,1)}, bf16[192,1024]{1,0:T(8,128)(2,1)S(1)}, u32[]{:S(2)}, u32[]{:S(2)}) collective-permute-start(bf16[192,1024]{1,0:T(8,128)(2,1)} %get-tuple-element.171), channel_id=1, source_target_pairs={{0,16},{4,20},{8,24},{12,28},{16,0},{20,4},{24,8},{28,12},{1,17},{... | collective-permute-start | bytes 1179656 | tf_op jit(solution)/shard_map/ppermute | solution.py:393
  146.3 17.6 %collective-permute-start.29 = (bf16[192,896]{1,0:T(8,128)(2,1)}, bf16[192,896]{1,0:T(8,128)(2,1)S(1)}, u32[]{:S(2)}, u32[]{:S(2)}) collective-permute-start(bf16[192,896]{1,0:T(8,128)(2,1)} %get-tuple-element.186), channel_id=1, source_target_pairs={{0,8},{4,12},{8,0},{12,4},{16,24},{20,28},{24,16},{28,20},{1,9},{5... | collective-permute-start | bytes 1032200 | tf_op jit(solution)/shard_map/ppermute | solution.py:393
  159.3 14.6 %collective-permute-start.37 = (bf16[192,640]{1,0:T(8,128)(2,1)}, bf16[192,640]{1,0:T(8,128)(2,1)S(1)}, u32[]{:S(2)}, u32[]{:S(2)}) collective-permute-start(bf16[192,640]{1,0:T(8,128)(2,1)} %get-tuple-element.184), channel_id=1, source_target_pairs={{0,16},{4,20},{8,24},{12,28},{16,0},{20,4},{24,8},{28,12},{1,17},{... | collective-permute-start | bytes 737288 | tf_op jit(solution)/shard_map/ppermute | solution.py:393
  171.1 12.7 %collective-permute-start.41 = (bf16[24,1920]{1,0:T(8,128)(2,1)}, bf16[24,1920]{1,0:T(8,128)(2,1)S(1)}, u32[]{:S(2)}, u32[]{:S(2)}) collective-permute-start(bf16[24,1920]{1,0:T(8,128)(2,1)} %get-tuple-element.202), channel_id=1, source_target_pairs={{0,3},{1,0},{2,1},{3,2},{4,7},{5,4},{6,5},{7,6},{8,11},{9,8},{10,9... | collective-permute-start | bytes 276488 | tf_op jit(solution)/shard_map/ppermute | solution.py:419
  185.7 15.7 %collective-permute-start.48 = (bf16[24,1280]{1,0:T(8,128)(2,1)}, bf16[24,1280]{1,0:T(8,128)(2,1)S(1)}, u32[]{:S(2)}, u32[]{:S(2)}) collective-permute-start(bf16[24,1280]{1,0:T(8,128)(2,1)} %get-tuple-element.211), channel_id=1, source_target_pairs={{0,3},{1,0},{2,1},{3,2},{4,7},{5,4},{6,5},{7,6},{8,11},{9,8},{10,9... | collective-permute-start | bytes 184328 | tf_op jit(solution)/shard_map/ppermute | solution.py:419
  188.6 12.9 %collective-permute-start.49 = (bf16[24,1280]{1,0:T(8,128)(2,1)}, bf16[24,1280]{1,0:T(8,128)(2,1)S(1)}, u32[]{:S(2)}, u32[]{:S(2)}) collective-permute-start(bf16[24,1280]{1,0:T(8,128)(2,1)} %get-tuple-element.212), channel_id=1, source_target_pairs={{0,4},{1,5},{2,6},{3,7},{4,0},{5,1},{6,2},{7,3},{8,12},{9,13},{10,... | collective-permute-start | bytes 184328 | tf_op jit(solution)/shard_map/ppermute | solution.py:419
  188.6 12.8 %collective-permute-start.50 = (bf16[24,1280]{1,0:T(8,128)(2,1)}, bf16[24,1280]{1,0:T(8,128)(2,1)S(1)}, u32[]{:S(2)}, u32[]{:S(2)}) collective-permute-start(bf16[24,1280]{1,0:T(8,128)(2,1)} %get-tuple-element.213), channel_id=1, source_target_pairs={{0,5},{1,6},{2,7},{3,4},{4,1},{5,2},{6,3},{7,0},{8,13},{9,14},{10,... | collective-permute-start | bytes 184328 | tf_op jit(solution)/shard_map/ppermute | solution.py:419
  (94 other events, 806.9 us)
where the time goes:
time: 209 us; the launch traced here: 208 us
  Pallas kernels  86.1 us (41%)
  starting transfers between devices  63.2 us (30%)
  waiting for transfers between devices  25.6 us (12%)
  local copies, waits for them, and re-layouts  23.9 us (11%)
  other arithmetic  7.42 us (4%)
    ppermute x21, starting transfers between devices, both_shift(): return lax.ppermute(x, ('img', 'band'), perm)  30.9 us
    pallas_call x3, Pallas kernels, __init__(): pl.pallas_call(functools.partial(weight_kernel, len(pairs), self.extra, b...  19.3 us
    ppermute x12, waiting for transfers between devices, band_shift(): lax.ppermute(x, 'band', [(k, (k + s) % self.nb) for k in range(self.nb)])  17.3 us
    ppermute x12, starting transfers between devices, band_shift(): lax.ppermute(x, 'band', [(k, (k + s) % self.nb) for k in range(self.nb)])  17 us
    unnamed x144, local copies, waits for them, and re-layouts  15.6 us
    ppermute x20, starting transfers between devices, flip(): return lax.ppermute(x, 'img', [(k, k ^ bit) for k in range(self.n_img)])  15.4 us
    pallas_call x1, Pallas kernels, per_device(): pl.pallas_call(attend_back_kernel, in_specs=[SM] + [VM] * 6, out_specs=[V...  10.8 us
    pallas_call x1, Pallas kernels, per_device(): pl.pallas_call(functools.partial(up_kernel, rows, nb, steps), grid_spec=p...  9.41 us
  transfers between devices with their start and end apart: 53, of which 7 were waited for; matrix products, arithmetic and copies ran while one was open for 9% of the time, Pallas kernels for 36%

commit v1 on v0

v1 whole, which is shorter than its diff:
```python
import functools

import jax
import jax.numpy as jnp
from jax import lax
from jax.experimental import pallas as pl
from jax.experimental.pallas import tpu as pltpu
from jax.sharding import PartitionSpec as P

HEADS = 16
HEAD_DIM = 48
SIDE = 16
EPS = 1e-05
F32 = jnp.float32
BF16 = jnp.bfloat16
GROUP = 8
GROUP_LANES = GROUP * HEAD_DIM
SCALE = HEAD_DIM ** (-0.5)


def dot_nn(a, b):
    return lax.dot_general(a, b, (((1,), (0,)), ((), ())), preferred_element_type=F32)


def dot_nt(a, b):
    return lax.dot_general(a, b, (((1,), (1,)), ((), ())), preferred_element_type=F32)


def dot_tn(a, b):
    return lax.dot_general(a, b, (((0,), (0,)), ((), ())), preferred_element_type=F32)


def norm_stats(x):
    mean = jnp.mean(x, axis=-1, keepdims=True)
    centred = x - mean
    var = jnp.mean(centred * centred, axis=-1, keepdims=True)
    r = lax.rsqrt(var + EPS)
    return centred * r, r


def norm_back(grad, n, r, gain):
    e = grad * gain
    return r * (e - jnp.mean(e, axis=-1, keepdims=True) - n * jnp.mean(e * n, axis=-1, keepdims=True))


def colsum(x):
    return jnp.sum(x.astype(F32), axis=0, keepdims=True)


def take(x, index, axis):
    return lax.dynamic_index_in_dim(x, index, axis, keepdims=False)


GAIN1, SHIFT1, BQ, BV, BO, GAIN2, SHIFT2, BDOWN = range(8)


def windows():
    out = []
    for h in range(GROUP):
        first, last = h * HEAD_DIM, (h + 1) * HEAD_DIM
        lo, hi = first // 128 * 128, -(-last // 128) * 128
        out.append((lo, hi, first - lo, last - lo))
    return out


def head_lanes(shape, first, last):
    lane = lax.broadcasted_iota(jnp.int32, shape, 1)
    return (lane >= first) & (lane < last)


def turn(x):
    return jnp.transpose(x.astype(F32)).astype(BF16)


def split_rows(x, block, c, keep, send, at=0):
    for i in range(x.shape[0] // (2 * block)):
        even, odd = x[2 * i * block : (2 * i + 1) * block, :], x[(2 * i + 1) * block : (2 * i + 2) * block, :]
        rows = pl.ds(at + i * block, block)
        keep[rows, :] = jnp.where(c == 0, even, odd)
        send[rows, :] = jnp.where(c == 0, odd, even)


def join(refs, rows):
    return jnp.concatenate([r[:rows, :] for r in refs], axis=0)


def column_of(row):
    n = row.shape[1]
    eye = lax.broadcasted_iota(jnp.int32, (n, n), 0) == lax.broadcasted_iota(jnp.int32, (n, n), 1)
    return jnp.sum(jnp.where(eye, row, 0.0), axis=1, keepdims=True)


def attend_kernel(rows, nb, block, core, *refs):
    slots = refs[:nb]
    c = core[0]
    vec, wq, wk, wv, wo = refs[nb : nb + 5]
    keep_o, send_o, q_o, k_o, v_o, mid_o, two_o, mask_o, att_o, kt = refs[nb + 5 :]
    tokens = nb * rows
    half = q_o.shape[1] // 2
    row = jnp.zeros((1, tokens), F32)
    for s in range(nb):
        row = row + slots[s][rows : rows + 8, :tokens].astype(F32)[s : s + 1, :]
    mask_o[...] = jnp.broadcast_to(row, mask_o.shape)
    x = join(slots, rows).astype(F32)
    n1, _ = norm_stats(x)
    normed = (n1 * vec[GAIN1 : GAIN1 + 1, :] + vec[SHIFT1 : SHIFT1 + 1, :]).astype(BF16)
    split_rows(turn(normed), block, c, keep_o, send_o)
    q_o[...] = (dot_nn(normed, wq[...]) + vec[BQ : BQ + 1, :]).astype(BF16)
    k = dot_nn(normed, wk[...]).astype(BF16)
    k_o[...] = k
    kt[...] = turn(k)
    v_o[...] = (dot_nn(normed, wv[...]) + vec[BV : BV + 1, :]).astype(BF16)
    keep = row > 0.5

    def group(g, carry):
        base = pl.multiple_of(g * GROUP_LANES, 128)
        blocks = [jnp.zeros((tokens, 128), F32) for _ in range(GROUP_LANES // 128)]
        for lo, hi, first, last in windows():
            wide = hi - lo
            here = head_lanes((tokens, wide), first, last)
            at = pl.ds(base + lo, wide)
            zero = jnp.zeros((tokens, wide), BF16)
            qm = jnp.where(here, q_o[:, at], zero)
            s = dot_nn(qm, kt[at, :]) * SCALE
            s = jnp.where(keep, s, -1e30)
            e = jnp.exp(s - jnp.max(s, axis=-1, keepdims=True))
            p = (e * (1.0 / jnp.sum(e, axis=-1, keepdims=True))).astype(BF16)
            o = dot_nn(p, jnp.where(here, v_o[:, at], zero))
            for j in range(wide // 128):
                blocks[lo // 128 + j] = blocks[lo // 128 + j] + o[:, j * 128 : (j + 1) * 128]
        att_o[:, pl.ds(base, GROUP_LANES)] = jnp.concatenate(blocks, axis=1).astype(BF16)
        return carry

    lax.fori_loop(0, HEADS // GROUP, group, 0)
    split_rows(turn(att_o[...]), block, c, keep_o, send_o, half)
    middle = x + (dot_nn(att_o[...], wo[...]) + vec[BO : BO + 1, :])
    mid_o[...] = middle
    n2, _ = norm_stats(middle)
    two = (n2 * vec[GAIN2 : GAIN2 + 1, :] + vec[SHIFT2 : SHIFT2 + 1, :]).astype(BF16)
    two_o[...] = two
    split_rows(turn(two), block, c, keep_o, send_o, 2 * half)


def up_kernel(rows, nb, steps, block, core, *refs):
    two, middle, mask, vec, w_up, b_up, w_down = refs[:7]
    cots = refs[7 : 7 + nb]
    act_keep, act_send, right_o, bsum = refs[7 + nb : 11 + nb]
    outs = refs[11 + nb : 11 + 2 * nb]
    acc = refs[11 + 2 * nb]
    j = pl.program_id(0)
    width = acc.shape[1]

    @pl.when(j == 0)
    def _():
        col = column_of(mask[0:1, :])
        right_o[:, :width] = (join(cots, rows).astype(F32) * col).astype(BF16)

    hidden = dot_nn(two[...], w_up[...]) + b_up[0:1, :]
    cdf = 0.5 * (1.0 + lax.erf(hidden * 0.7071067811865476))
    pdf = jnp.exp(-0.5 * hidden * hidden) * 0.3989422804014327
    act = (hidden * cdf).astype(BF16)
    split_rows(turn(act), block, core[0], act_keep, act_send)
    part = dot_nn(act, w_down[...])
    acc[...] = jnp.where(j == 0, part, acc[...] + part)
    gh = (dot_nt(right_o[:, :width], w_down[...]) * (cdf + hidden * pdf)).astype(BF16)
    right_o[:, pl.ds(pl.multiple_of(width + j * gh.shape[1], 128), gh.shape[1])] = gh
    bsum[...] = jnp.broadcast_to(colsum(gh), bsum.shape)

    @pl.when(j == steps - 1)
    def _():
        col = column_of(mask[0:1, :])
        out = (col * (middle[...] + (acc[...] + vec[BDOWN : BDOWN + 1, :]))).astype(BF16)
        for s in range(nb):
            outs[s][...] = out[s * rows : (s + 1) * rows, :]


def down_kernel(rows, nb, steps, *refs):
    gd, gh, w_up, middle, mask, vec = refs[:6]
    cots = refs[6 : 6 + nb]
    gm_o, gb_o, sums, acc = refs[6 + nb :]
    j = pl.program_id(0)
    part = dot_nt(gh[...], w_up[...])
    acc[...] = jnp.where(j == 0, part, acc[...] + part)

    @pl.when(j == steps - 1)
    def _():
        grad = acc[...]
        n2, r2 = norm_stats(middle[...])
        col = column_of(mask[0:1, :])
        result = join(cots, rows).astype(F32) * col
        gm = result + norm_back(grad, n2, r2, vec[GAIN2 : GAIN2 + 1, :])
        gm_o[...] = gm
        gb = gm.astype(BF16)
        gb_o[...] = gb
        sums[0:1, :] = colsum(grad * n2)
        sums[1:2, :] = colsum(grad)
        sums[2:3, :] = colsum(gb)
        sums[3:4, :] = colsum(gd[...])
        sums[4:8, :] = jnp.zeros((4, sums.shape[1]), F32)


def attend_back_kernel(gb, q, k, v, mask, wo, right_o, sums, gq_o, ga, qt, kt, vt, gat, gkt, gvt):
    tokens, width = gb.shape
    g_att = dot_nt(gb[...], wo[...]).astype(BF16)
    ga[...] = g_att
    gat[...] = turn(g_att)
    qt[...] = turn(q[...])
    kt[...] = turn(k[...])
    vt[...] = turn(v[...])
    keep = mask[0:1, :] > 0.5

    def group(g, carry):
        base = pl.multiple_of(g * GROUP_LANES, 128)
        blocks = [jnp.zeros((tokens, 128), F32) for _ in range(GROUP_LANES // 128)]
        for h, (lo, hi, first, last) in enumerate(windows()):
            wide = hi - lo
            here = head_lanes((tokens, wide), first, last)
            at = pl.ds(base + lo, wide)
            own = pl.ds(pl.multiple_of(base + h * HEAD_DIM, 16), HEAD_DIM)
            zero = jnp.zeros((tokens, wide), BF16)
            s = dot_nn(jnp.where(here, q[:, at], zero), kt[at, :]) * SCALE
            s = jnp.where(keep, s, -1e30)
            e = jnp.exp(s - jnp.max(s, axis=-1, keepdims=True))
            p = e * (1.0 / jnp.sum(e, axis=-1, keepdims=True))
            dp = dot_nn(jnp.where(here, ga[:, at], zero), vt[at, :])
            gvt[own, :] = dot_nn(gat[own, :], p.astype(BF16))
            ds = (p * (dp - jnp.sum(p * dp, axis=-1, keepdims=True))).astype(BF16)
            gkt[own, :] = dot_nn(qt[own, :], ds)
            o = dot_nn(ds, jnp.where(here, k[:, at], zero))
            for j in range(wide // 128):
                blocks[lo // 128 + j] = blocks[lo // 128 + j] + o[:, j * 128 : (j + 1) * 128]
        gq_o[:, pl.ds(base, GROUP_LANES)] = (jnp.concatenate(blocks, axis=1) * SCALE).astype(BF16)
        return carry

    lax.fori_loop(0, HEADS // GROUP, group, 0)
    gq = gq_o[...]
    gk = (jnp.transpose(gkt[...]) * SCALE).astype(BF16)
    gv = jnp.transpose(gvt[...]).astype(BF16)
    for i, t in enumerate((gq, gk, gv)):
        right_o[:, i * width : (i + 1) * width] = t
    sums[0:1, :] = colsum(gq)
    sums[1:2, :] = colsum(gv)
    sums[2:8, :] = jnp.zeros((6, width), F32)


def input_back_kernel(rows, nb, block, core, *refs):
    slots = refs[:nb]
    right, wq, wk, wv, gm, vec, down_sums, attend_sums = refs[nb : nb + 8]
    outs = refs[nb + 8 : 2 * nb + 8]
    keep_o, send_o = refs[2 * nb + 8 :]
    width = gm.shape[1]
    grad = dot_nt(right[:, :width], wq[...])
    grad = grad + dot_nt(right[:, width : 2 * width], wk[...])
    grad = grad + dot_nt(right[:, 2 * width :], wv[...])
    n1, r1 = norm_stats(join(slots, rows).astype(F32))
    gx = (gm[...] + norm_back(grad, n1, r1, vec[GAIN1 : GAIN1 + 1, :])).astype(BF16)
    for s in range(nb):
        outs[s][...] = gx[s * rows : (s + 1) * rows, :]
    table = jnp.concatenate(
        [
            down_sums[...], attend_sums[...], colsum(grad * n1), colsum(grad),
            jnp.zeros((COLS - 18, width), F32),
        ],
        axis=0,
    )
    split_rows(jnp.transpose(table), block, core[0], keep_o, send_o)


def spread_kernel(rows, nb, band, crop_rows, crop_cols, x, keep_mask, *outs):
    width = x.shape[2]
    position = band[0] * rows + lax.broadcasted_iota(jnp.int32, (1, rows), 1)
    slot = lax.broadcasted_iota(jnp.int32, (8, width), 0)
    lane = lax.broadcasted_iota(jnp.int32, (8, width), 1) // rows
    for s in range(nb):
        image = lax.rem(band[0] + s, nb)
        outs[s][:rows, :] = x[image]
        inside = (
            (keep_mask[pl.ds(image, 1), :] > 0)
            & (position // SIDE < crop_rows[image])
            & (position % SIDE < crop_cols[image])
        )
        flags = jnp.concatenate([jnp.where(inside, 1.0, 0.0)] * (width // rows), axis=1)
        outs[s][rows:, :] = jnp.where((slot == s) & (lane == s), flags, 0.0).astype(BF16)


def gather_kernel(nb, band, *refs):
    for s in range(nb):
        image = lax.rem(band[0] + s, nb)
        refs[2 * nb][image] = refs[s][...]
        refs[2 * nb + 1][image] = refs[nb + s][...].astype(F32)


def weight_kernel(groups, quarters, *refs):
    t = pl.program_id(0)
    parts, at = [], 0
    for widths in groups:
        left, left_got = refs[at : at + 2]
        at += 2
        for _ in widths:
            right, right_got = refs[at : at + 2]
            at += 2
            parts.append((dot_nn(left[...], right[...]) + dot_nn(left_got[...], right_got[...])).astype(BF16))
    send, keep = refs[at:]
    g = parts[0] if len(parts) == 1 else jnp.concatenate(parts, axis=1)

    @pl.when(t < 2)
    def _():
        send[0] = g

    @pl.when(t >= 2)
    def _():
        keep[0] = g


def second_kernel(keep, got, out):
    out[...] = (keep[0].astype(F32) + got[0].astype(F32)).astype(BF16)


def third_kernel(size, band, keep, got, more, keep_o, send_o, held):
    held[...] = keep[0].astype(F32) + got[0].astype(F32) + more[...].astype(F32)
    for i in range(2):
        near = jnp.bitwise_xor(band[0], 2 * i)
        far = jnp.bitwise_xor(band[0], 2 * i + 1)
        keep_o[i] = held[pl.ds(pl.multiple_of(near * size, 8), size), :]
        send_o[i] = held[pl.ds(pl.multiple_of(far * size, 8), size), :].astype(BF16)


def last_kernel(widths, keep, got, more, *outs):
    at = 0
    for w, out in zip(widths, outs):
        cols = pl.ds(at, w)
        out[...] = keep[0, :, cols] + got[0, :, cols].astype(F32) + more[:, cols].astype(F32)
        at += w


COLS = 128


VM = pl.BlockSpec(memory_space=pltpu.VMEM)
SM = pl.BlockSpec(memory_space=pltpu.SMEM)


def shape(*dims, dtype=BF16):
    return jax.ShapeDtypeStruct(dims, dtype)


def cost(us):
    return pl.CostEstimate(flops=us * 2500000000, bytes_accessed=us * 10000000, transcendentals=0)


def after(x, *others):
    return lax.optimization_barrier((x, others))[0]


def scalar(x):
    return x.astype(jnp.int32).reshape(1)


class Links:
    def __init__(self, n_img, n_band):
        self.n_img, self.nb = n_img, n_band
        self.hi = n_img // 8
        i = lax.axis_index("img")
        self.c = i & 1
        self.p = (i >> 1) & 1
        self.q = (i >> 2) & 1
        self.h = i >> 3
        self.b = lax.axis_index("band")

    def flip(self, x, bit):
        return lax.ppermute(x, "img", [(k, k ^ bit) for k in range(self.n_img)])

    def flip_by_core(self, x, even, odd):
        return lax.ppermute(x, "img", [(k, k ^ (odd if k & 1 else even)) for k in range(self.n_img)])

    def flip_band(self, x, bit):
        return lax.ppermute(x, "band", [(k, k ^ bit) for k in range(self.nb)])

    def band_shift(self, x, s):
        return lax.ppermute(x, "band", [(k, (k + s) % self.nb) for k in range(self.nb)])

    def hi_shift(self, x, s):
        n = self.n_img
        return lax.ppermute(x, "img", [(k, (k + 8 * s) % n) for k in range(n)])

    def sum_hi(self, x):
        x = x.reshape(self.hi, x.shape[0] // self.hi, *x.shape[1:])
        total = take(x, self.h, 0)
        for s in range(1, self.hi):
            total = total + self.hi_shift(take(x, (self.h + s) % self.hi, 0).astype(BF16), s).astype(F32)
        return total

    def by_quarter(self, x):
        if self.hi == 1:
            return x
        return x.reshape(self.hi, 4, -1, x.shape[1]).swapaxes(0, 1).reshape(x.shape)

    def reclass(self, first, second, block):
        x = jnp.concatenate([first, second], axis=0)
        x = x.reshape(-1, 2, block, x.shape[1])
        own, other = take(x, self.c, 1), take(x, 1 - self.c, 1)
        return own.reshape(-1, x.shape[3]), other.reshape(-1, x.shape[3])


class Unit:
    def __init__(self, links, rows, groups):
        self.links = links
        args, specs, widths = [], [], []
        tokens = groups[0][0].shape[1]
        self.block = block = rows // 4
        for left, left_got, left_at, rights in groups:
            if links.hi > 1:
                left, left_got = (x[left_at * rows : (left_at + 1) * rows, :] for x in (left, left_got))
                left_at = 0
            args += [links.by_quarter(left), links.by_quarter(left_got)]
            specs += [pl.BlockSpec((block, tokens), lambda t, s, i=4 * left_at: (s[t] + i, 0))] * 2
            widths.append([w for w, _, _, _, _ in rights])
            for w, own, own_at, got, got_at in rights:
                args += [own, got]
                specs.append(pl.BlockSpec((tokens, w), lambda t, s, i=own_at: (0, i)))
                specs.append(pl.BlockSpec((tokens, w), lambda t, s, i=got_at: (0, i)))
        self.widths = [w for ws in widths for w in ws]
        self.cols = cols = sum(self.widths)
        p, q = links.p, links.q
        even = links.c == 0
        at = lambda a, b: a * 2 + b
        quarters = jnp.stack(
            [
                jnp.where(even, at(q, 1 - p), at(1 - q, p)), at(1 - q, 1 - p),
                jnp.where(even, at(1 - q, p), at(q, 1 - p)), at(q, p),
            ]
        ).astype(jnp.int32)
        one = lambda x: jnp.asarray(x).astype(jnp.int32)
        self.send, self.keep = pl.pallas_call(
            functools.partial(weight_kernel, widths),
            grid_spec=pltpu.PrefetchScalarGridSpec(
                num_scalar_prefetch=1,
                grid=(4,),
                in_specs=specs,
                out_specs=[
                    pl.BlockSpec((1, block, cols), lambda t, s: (one(t > 0), 0, 0)),
                    pl.BlockSpec((1, block, cols), lambda t, s: (one(t < 3), 0, 0)),
                ],
            ),
            out_shape=[shape(2, block, cols)] * 2,
            cost_estimate=cost(6),
            name="weight_grad",
        )(quarters, *args)
        self.got = links.flip_by_core(self.send, 2, 4)

    def pick(self, i):
        return pl.BlockSpec((1, self.block, self.cols), lambda _: (i, 0, 0))

    def whole(self, *dims):
        return pl.BlockSpec(dims, lambda _: (0,) * len(dims))

    def second(self, *deps):
        dims = (self.block, self.cols)
        sent = pl.pallas_call(
            second_kernel,
            grid=(1,),
            in_specs=[self.pick(1)] * 2,
            out_specs=self.whole(*dims),
            out_shape=shape(*dims),
            cost_estimate=cost(2),
            name="second",
        )(after(self.keep, *deps), self.got)
        self.more = self.links.flip_by_core(sent, 4, 2)
        return sent

    def third(self, *deps):
        links, nb, cols = self.links, self.links.nb, self.cols
        self.size = size = self.block // (links.hi * nb)
        keep = after(self.keep, *deps)
        if links.hi > 1 or size % 8:
            held = links.sum_hi(keep[0].astype(F32) + self.got[0].astype(F32) + self.more.astype(F32))
            held = held.reshape(nb, size, cols)
            piece = lambda bits: take(held, links.b ^ bits, 0)
            self.near = jnp.stack([piece(0), piece(2)])
            sent = jnp.stack([piece(1), piece(3)]).astype(BF16)
        else:
            self.near, sent = pl.pallas_call(
                functools.partial(third_kernel, size),
                grid=(1,),
                in_specs=[SM, self.pick(0), self.pick(0), self.whole(self.block, cols)],
                out_specs=[self.whole(2, size, cols)] * 2,
                out_shape=[shape(2, size, cols, dtype=F32), shape(2, size, cols)],
                scratch_shapes=[pltpu.VMEM((self.block, cols), F32)],
                cost_estimate=cost(3),
                name="third",
            )(scalar(links.b), keep, self.got, self.more)
        self.near_got = links.flip_band(sent, 1)
        return sent

    def fourth(self, *deps):
        dims = (self.size, self.cols)
        pick = pl.BlockSpec((1,) + dims, lambda _: (1, 0, 0))
        sent = pl.pallas_call(
            second_kernel,
            grid=(1,),
            in_specs=[pick] * 2,
            out_specs=self.whole(*dims),
            out_shape=shape(*dims),
            cost_estimate=cost(2),
            name="fourth",
        )(after(self.near, *deps), self.near_got)
        self.far_got = self.links.flip_band(sent, 2)
        return sent

    def last(self, *deps):
        dims = (self.size, self.cols)
        pick = pl.BlockSpec((1,) + dims, lambda _: (0, 0, 0))
        return pl.pallas_call(
            functools.partial(last_kernel, self.widths),
            grid=(1,),
            in_specs=[pick, pick, self.whole(*dims)],
            out_specs=[self.whole(self.size, w) for w in self.widths],
            out_shape=[shape(self.size, w, dtype=F32) for w in self.widths],
            cost_estimate=cost(2),
            name="last",
        )(after(self.near, *deps), self.near_got, self.far_got)


class Table:
    def __init__(self, links, keep, send):
        self.links, self.keep, self.send = links, keep, send

    def start(self, *deps):
        self.got = self.links.flip(after(self.send, *deps), 1)

    def core(self, *deps):
        links = self.links
        x = links.by_quarter(after(self.keep, *deps) + self.got)
        x = x.reshape(2, 2, -1, x.shape[1])
        self.keep = take(x, links.p, 1)
        self.send = take(x, 1 - links.p, 1)
        self.got = links.flip(self.send, 2)
        return self.send

    def near(self, *deps):
        links = self.links
        x = after(self.keep, *deps) + self.got
        self.keep = take(x, links.q, 0)
        self.send = take(x, 1 - links.q, 0)
        self.got = links.flip(self.send, 4)
        return self.send

    def band(self, *deps):
        links, nb = self.links, self.links.nb
        x = links.sum_hi(after(self.keep, *deps) + self.got)
        x = x.reshape(2, 2, -1, x.shape[1])
        low, high = links.b & 1, links.b >> 1
        self.keep = take(x, low, 1)
        self.send = take(x, 1 - low, 1)
        self.got = links.flip_band(self.send, 1)
        return self.send

    def far(self, *deps):
        high = self.links.b >> 1
        x = after(self.keep, *deps) + self.got
        self.keep = take(x, high, 0)
        self.send = take(x, 1 - high, 0)
        self.got = self.links.flip_band(self.send, 2)
        return self.send

    def last(self, *deps):
        return after(self.keep, *deps) + self.got


def per_device(
    inputs, keep_mask, crop_rows, crop_cols, gain_one, shift_one, w_query, b_query, w_key, w_value,
    b_value, w_out, b_out, gain_two, shift_two, w_up, b_up, w_down, b_down, cotangent, *, n_img, nb,
):
    images, rows, width = inputs.shape
    hidden_width = w_up.shape[1]
    assert images == nb and nb == 4
    tokens = nb * rows
    links = Links(n_img, nb)
    core, band = scalar(links.c), scalar(links.b)
    f = lambda v: v.astype(F32)

    blocks = pl.pallas_call(
        functools.partial(spread_kernel, rows, nb),
        in_specs=[SM] * 3 + [VM] * 2,
        out_specs=[VM] * nb,
        out_shape=[shape(rows + 8, width)] * nb,
        cost_estimate=cost(2),
        name="spread",
    )(band, crop_rows, crop_cols, inputs, keep_mask)
    slots = [blocks[0]] + [links.band_shift(blocks[s], s) for s in range(1, nb)]
    given = after(cotangent, *blocks)
    cots = [take(given, links.b, 0)]
    for s in range(1, nb):
        cots.append(links.band_shift(take(given, (links.b + s) % nb, 0), s))
    vec = jnp.stack([f(t) for t in (gain_one, shift_one, b_query, b_value, b_out, gain_two, shift_two, b_down)])
    b_up_row = f(b_up)[None, :]

    block = width // (links.hi * 8)
    aligned = block % 16 == 0
    up_block = hidden_width // (links.hi * 8)
    half = width // 2
    full = shape(tokens, width)
    left_keep, left_send, q, k, v, middle, two, mask = pl.pallas_call(
        functools.partial(attend_kernel, rows, nb, block if aligned else half),
        in_specs=[SM] + [VM] * (nb + 5),
        out_specs=[VM] * 8,
        out_shape=[shape(3 * half, tokens)] * 2 + [full] * 3
        + [shape(tokens, width, dtype=F32), full, shape(8, tokens, dtype=F32)],
        scratch_shapes=[pltpu.VMEM((tokens, width), BF16), pltpu.VMEM((width, tokens), BF16)],
        cost_estimate=cost(9),
        name="attend",
    )(core if aligned else jnp.zeros_like(core), *slots, vec, w_query, w_key, w_value, w_out)
    third_of = lambda x, i: x[i * half : (i + 1) * half, :]
    if not aligned:
        pairs = [links.reclass(third_of(left_keep, i), third_of(left_send, i), block) for i in range(3)]
        left_keep, left_send = (jnp.concatenate(x, axis=0) for x in zip(*pairs))
    left_got = links.flip(left_send, 1)

    steps = 4
    wide = hidden_width // steps
    fixed = lambda *dims: pl.BlockSpec(dims, lambda j, *_: (0,) * len(dims))
    tall = lambda *dims: pl.BlockSpec(dims, lambda j, *_: (0, j))
    up = pl.pallas_call(
        functools.partial(up_kernel, rows, nb, steps, up_block),
        grid_spec=pltpu.PrefetchScalarGridSpec(
            num_scalar_prefetch=1,
            grid=(steps,),
            in_specs=[
                fixed(tokens, width), fixed(tokens, width), fixed(8, tokens), fixed(8, width),
                tall(width, wide), tall(1, wide),
                pl.BlockSpec((wide, width), lambda j, c: (j, 0)),
            ] + [fixed(rows, width)] * nb,
            out_specs=[pl.BlockSpec((wide // 2, tokens), lambda j, c: (j, 0))] * 2
            + [fixed(tokens, width + hidden_width), tall(8, wide)]
            + [fixed(rows, width)] * nb,
            scratch_shapes=[pltpu.VMEM((tokens, width), F32)],
        ),
        out_shape=[shape(hidden_width // 2, tokens)] * 2
        + [shape(tokens, width + hidden_width), shape(8, hidden_width, dtype=F32)]
        + [shape(rows, width)] * nb,
        cost_estimate=cost(10),
        name="up",
    )(core, two, middle, mask, vec, w_up, b_up_row, w_down, *cots)
    act_keep, act_send, right, up_sums = up[:4]
    act_got = links.flip(act_send, 1)
    right_got = links.flip(right, 1)
    out_blocks = [up[4]] + [links.band_shift(up[4 + s], -s) for s in range(1, nb)]

    grad_middle, grad_branch, down_sums = pl.pallas_call(
        functools.partial(down_kernel, rows, nb, steps),
        grid=(steps,),
        in_specs=[
            fixed(tokens, width), pl.BlockSpec((tokens, wide), lambda j: (0, j + width // wide)), tall(width, wide),
            fixed(tokens, width), fixed(8, tokens), fixed(8, width),
        ] + [fixed(rows, width)] * nb,
        out_specs=[fixed(tokens, width), fixed(tokens, width), fixed(8, width)],
        out_shape=[shape(tokens, width, dtype=F32), full, shape(8, width, dtype=F32)],
        scratch_shapes=[pltpu.VMEM((tokens, width), F32)],
        cost_estimate=cost(7),
        name="down",
    )(right, right, w_up, after(middle, left_got), mask, vec, *cots)
    branch_got = links.flip(grad_branch, 1)

    unit_down = Unit(
        links, hidden_width // 2,
        [(after(act_keep, grad_branch), act_got, 0, [(width, right, 0, right_got, 0)])],
    )
    low = lambda: pltpu.VMEM((width, tokens), BF16)
    back_right, attend_sums = pl.pallas_call(
        attend_back_kernel,
        in_specs=[VM] * 6,
        out_specs=[VM] * 2,
        out_shape=[shape(tokens, 3 * width), shape(8, width, dtype=F32)],
        scratch_shapes=[
            pltpu.VMEM((tokens, width), BF16), pltpu.VMEM((tokens, width), BF16), low(), low(), low(), low(),
            pltpu.VMEM((width, tokens), F32), pltpu.VMEM((width, tokens), F32),
        ],
        cost_estimate=cost(11),
        name="attend_back",
    )(after(grad_branch, unit_down.send), q, k, v, mask, w_out)
    back_got = links.flip(back_right, 1)

    mark = unit_down.second(back_right)
    unit_up = Unit(
        links, half,
        [
            (
                after(left_keep, mark, *out_blocks), left_got, 2,
                [(width, right, 1 + i, right_got, 1 + i) for i in range(hidden_width // width)],
            ),
            (left_keep, left_got, 1, [(width, grad_branch, 0, branch_got, 0)]),
        ],
    )
    mark = unit_down.third(unit_up.send)
    unit_qkv = Unit(
        links, half,
        [(after(left_keep, mark), left_got, 0, [(width, back_right, i, back_got, i) for i in range(3)])],
    )

    back = pl.pallas_call(
        functools.partial(input_back_kernel, rows, nb, block if aligned else half),
        in_specs=[SM] + [VM] * (nb + 8),
        out_specs=[VM] * (nb + 2),
        out_shape=[shape(rows, width)] * nb + [shape(half, COLS, dtype=F32)] * 2,
        cost_estimate=cost(5),
        name="input_back",
    )(
        core if aligned else jnp.zeros_like(core),
        *slots, after(back_right, unit_qkv.send), w_query, w_key, w_value, grad_middle, vec, down_sums, attend_sums,
    )
    table_pair = back[nb:]
    if not aligned:
        table_pair = links.reclass(*table_pair, block)
    grad_blocks = [back[0]] + [links.band_shift(back[s], -s) for s in range(1, nb)]
    mark = unit_down.fourth(back[0])
    mark = unit_up.second(mark)
    mark = unit_qkv.second(mark)
    up_cols = after(up_sums, mark)[0].reshape(width, hidden_width // width)
    up_cols = jnp.pad(up_cols, ((0, 0), (18, COLS - 18 - hidden_width // width))).reshape(-1, 2, block, COLS)
    class_of = lambda c: take(up_cols, c, 1).reshape(half, COLS)
    table = Table(links, table_pair[0] + class_of(links.c), table_pair[1] + class_of(1 - links.c))
    table.start()
    mark = unit_up.third(mark)
    mark = table.core(mark)
    mark = unit_qkv.third(mark)
    mark = table.near(mark)
    (g_w_down,) = unit_down.last(mark, *grad_blocks)
    mark = table.band(g_w_down)
    mark = unit_up.fourth(mark)
    mark = table.far(mark)
    mark = unit_qkv.fourth(mark)
    output, grad_inputs = pl.pallas_call(
        functools.partial(gather_kernel, nb),
        in_specs=[SM] + [VM] * (2 * nb),
        out_specs=[VM] * 2,
        out_shape=[shape(nb, rows, width), shape(nb, rows, width, dtype=F32)],
        cost_estimate=cost(2),
        name="gather",
    )(after(band, mark), *out_blocks, *grad_blocks)
    cols = table.last(output)
    unit_up.widths = [hidden_width, width]
    g_w_up, g_w_out = unit_up.last(cols)
    g_w_query, g_w_key, g_w_value = unit_qkv.last(g_w_up)
    sums = [cols[:, i] for i in range(18)]
    g_b_up = cols[:, 18 : 18 + hidden_width // width].reshape(-1)
    return (
        output,
        grad_inputs,
        sums[16],
        sums[17],
        g_w_query,
        sums[8],
        g_w_key,
        g_w_value,
        sums[9],
        g_w_out,
        sums[2],
        sums[0],
        sums[1],
        g_w_up,
        g_b_up,
        g_w_down,
        sums[3],
    )


def solution(mesh):
    n_img, nb = mesh.shape["img"], mesh.shape["band"]

    def body(*args):
        return per_device(*args, n_img=n_img, nb=nb)

    both = P(("img", "band"))
    rows = P(("img", "band"), None)
    token = P("img", "band", None)
    return jax.shard_map(
        body,
        mesh=mesh,
        in_specs=(token, P("img", "band"), P("img"), P("img")) + (P(),) * 15 + (token,),
        out_specs=(
            token, token, both, both, rows, both, rows, rows, both, rows, both, both, both, rows, both,
            rows, both,
        ),
        check_vma=False,
    )
```

time: 209 us -> 179 us (0.86)
  starting transfers between devices: 63.2 us -> 42.7 us
  local copies, waits for them, and re-layouts: 23.9 us -> 16.2 us
  other arithmetic: 7.42 us -> 1.9 us
  Pallas kernels: 86.1 us -> 91 us
    ppermute x21 -> x14, waiting for transfers between devices: 0.52 us -> 20.1 us  [the longest x8 11 us: flip_band(): return lax.ppermute(x, 'band', [(k, k ^ bit) for k in range(self.nb)])]
    ppermute x12, waiting for transfers between devices: 17.3 us -> 3.71 us  [band_shift(): lax.ppermute(x, 'band', [(k, (k + s) % self.nb) for k in range(self.nb)])]
    ppermute x21 -> x14, starting transfers between devices: 30.9 us -> 18.6 us  [the longest x8 11.9 us: flip_band(): return lax.ppermute(x, 'band', [(k, k ^ bit) for k in range(self.nb)])]
    ppermute x20 -> x8, starting transfers between devices: 15.4 us -> 3.77 us  [flip(): return lax.ppermute(x, 'img', [(k, k ^ bit) for k in range(self.n_img)])]
    ppermute x20 -> x8, waiting for transfers between devices: 7.78 us -> 0.8 us  [flip(): return lax.ppermute(x, 'img', [(k, k ^ bit) for k in range(self.n_img)])]
    pallas_call x18 -> x22, Pallas kernels: 86.1 us -> 91 us  [the longest x3 19.9 us: __init__(): pl.pallas_call(functools.partial(weight_kernel, widths), grid_spec=pltpu....]
    ppermute x12, starting transfers between devices: 17 us -> 20.4 us  [band_shift(): lax.ppermute(x, 'band', [(k, (k + s) % self.nb) for k in range(self.nb)])]
    unnamed x144 -> x80, local copies, waits for them, and re-layouts: 15.6 us -> 12.4 us
  transfers between devices with their start and end apart: 53 -> 34, of which waited for: 7 -> 8; matrix products, arithmetic and copies ran while one was open for 9% -> 3% of each run, Pallas kernels for 36% -> 49%
where the time goes in v1:
time: 179 us; the launch traced here: 178 us
  Pallas kernels  91 us (51%)
  starting transfers between devices  42.7 us (24%)
  waiting for transfers between devices  24.7 us (14%)
  local copies, waits for them, and re-layouts  16.2 us (9%)
  other arithmetic  1.9 us (1%)
    ppermute x12, starting transfers between devices, band_shift(): lax.ppermute(x, 'band', [(k, (k + s) % self.nb) for k in range(self.nb)])  20.4 us
    pallas_call x3, Pallas kernels, __init__(): pl.pallas_call(functools.partial(weight_kernel, widths), grid_spec=pltpu....  19.9 us
    unnamed x80, local copies, waits for them, and re-layouts  12.4 us
    ppermute x8, starting transfers between devices, flip_band(): return lax.ppermute(x, 'band', [(k, k ^ bit) for k in range(self.nb)])  11.9 us
    ppermute x8, waiting for transfers between devices, flip_band(): return lax.ppermute(x, 'band', [(k, k ^ bit) for k in range(self.nb)])  11 us
    pallas_call x1, Pallas kernels, per_device(): pl.pallas_call(attend_back_kernel, in_specs=[VM] * 6, out_specs=[VM] * 2,...  10.7 us
    pallas_call x1, Pallas kernels, per_device(): pl.pallas_call(functools.partial(up_kernel, rows, nb, steps, up_block), g...  9.84 us
    ppermute x6, waiting for transfers between devices, flip_by_core(): lax.ppermute(x, 'img', [(k, k ^ (odd if k & 1 else even)) for k in range(...  9.12 us
  transfers between devices with their start and end apart: 34, of which 8 were waited for; matrix products, arithmetic and copies ran while one was open for 3% of the time, Pallas kernels for 49%

profile of v1, /device:TPU:0, one launch (start us, length us, event | category | flops | bytes accessed | tf_op | source)
XLA Modules:
  0.0 177.6 jit_solution(13051305043291789161)
XLA Ops:
  2.8 3.1 %collective-permute-start = (bf16[72,768]{1,0:T(8,128)(2,1)}, bf16[72,768]{1,0:T(8,128)(2,1)S(1)}, u32[]{:S(2)}, u32[]{:S(2)}) collective-permute-start(bf16[72,768]{1,0:T(8,128)(2,1)} %get-tuple-element.94), channel_id=1, source_target_pairs={{0,1},{1,2},{2,3},{3,0},{4,5},{5,6},{6,7},{7,4},{8,9},{9,10},{10,1... | collective-permute-start | bytes 331784 | tf_op jit(solution)/shard_map/ppermute | solution.py:380
  5.8 2.6 %collective-permute-start.1 = (bf16[72,768]{1,0:T(8,128)(2,1)}, bf16[72,768]{1,0:T(8,128)(2,1)S(1)}, u32[]{:S(2)}, u32[]{:S(2)}) collective-permute-start(bf16[72,768]{1,0:T(8,128)(2,1)} %get-tuple-element.95), channel_id=1, source_target_pairs={{0,2},{1,3},{2,0},{3,1},{4,6},{5,7},{6,4},{7,5},{8,10},{9,11},{10,... | collective-permute-start | bytes 331784 | tf_op jit(solution)/shard_map/ppermute | solution.py:380
  12.9 2.8 %collective-permute-start.5 = (bf16[64,768]{1,0:T(8,128)(2,1)S(1)}, bf16[64,768]{1,0:T(8,128)(2,1)S(1)}, u32[]{:S(2)}, u32[]{:S(2)}) collective-permute-start(bf16[64,768]{1,0:T(8,128)(2,1)S(1)} %get-tuple-element.171), channel_id=1, source_target_pairs={{0,3},{1,0},{2,1},{3,2},{4,7},{5,4},{6,5},{7,6},{8,11},{9,8},{10,9... | collective-permute-start | bytes 294920 | tf_op jit(solution)/shard_map/ppermute | solution.py:380
  15.7 3.7 %collective-permute-done.1.refs_2_ = bf16[72,768]{1,0:T(8,128)(2,1)S(1)} collective-permute-done((bf16[72,768]{1,0:T(8,128)(2,1)}, bf16[72,768]{1,0:T(8,128)(2,1)S(1)}, u32[]{:S(2)}, u32[]{:S(2)}) %collective-permute-start.1) | collective-permute-done | bytes 110624 | tf_op jit(solution)/shard_map/ppermute | solution.py:380
  20.1 9.1 %attend.1 = (bf16[1152,256]{1,0:T(8,128)(2,1)}, bf16[1152,256]{1,0:T(8,128)(2,1)}, bf16[256,768]{1,0:T(8,128)(2,1)}, bf16[256,768]{1,0:T(8,128)(2,1)}, bf16[256,...) custom-call(s32[1]{0:T(128)} %bitcast.5.core, ...), custom_call_target="tpu_custom_call" | custom-call | flops 22499999744 | bytes 90000000 | tf_op jit(solution)/shard_map/attend/pallas_call | solution.py:603
  29.9 9.8 %up.1 = (bf16[1536,256]{1,0:T(8,128)(2,1)}, bf16[1536,256]{1,0:T(8,128)(2,1)}, bf16[256,3840]{1,0:T(8,128)(2,1)}, f32[8,3072]{1,0:T(8,128)}, bf16[64,768]{1,0:T(...) custom-call(s32[1]{0:T(128)} %bitcast.5.core, ...), custom_call_target="tpu_custom_call" | custom-call | flops 24999999488 | bytes 100000000 | tf_op jit(solution)/shard_map/up/pallas_call | solution.py:623
  41.0 5.8 %collective-permute-start.10 = (bf16[64,768]{1,0:T(8,128)(2,1)}, bf16[64,768]{1,0:T(8,128)(2,1)S(1)}, u32[]{:S(2)}, u32[]{:S(2)}) collective-permute-start(bf16[64,768]{1,0:T(8,128)(2,1)} %get-tuple-element.118), channel_id=1, source_target_pairs={{0,3},{1,0},{2,1},{3,2},{4,7},{5,4},{6,5},{7,6},{8,11},{9,8},{10,9... | collective-permute-start | bytes 294920 | tf_op jit(solution)/shard_map/ppermute | solution.py:380
  47.4 6.8 %down.1 = (f32[256,768]{1,0:T(8,128)}, bf16[256,768]{1,0:T(8,128)(2,1)}, f32[8,768]{1,0:T(8,128)}) custom-call(bf16[256,3840]{1,0:T(8,128)(2,1)} %get-tuple-element.103.refs_0_.refs_1_.refs_2_.refs_4_.refs_6_.refs_8_, bf16[256,3840]{1,0:T(8,128)(2,1)} %get-tuple-element.103.refs_0_.refs_1_.refs_2_.refs_4_.refs_6_.refs_8_, bf16[768,3072]{1,0:T(8,128)(2,1)} %refs_2_.1, ...), custom_call_target="tpu_custom_call" | custom-call | flops 17500000256 | bytes 70000000 | tf_op jit(solution)/shard_map/down/pallas_call | solution.py:649
  56.3 6.0 %weight_grad.3 = (bf16[2,384,768]{2,1,0:T(8,128)(2,1)}, bf16[2,384,768]{2,1,0:T(8,128)(2,1)}) custom-call(s32[4]{0:T(128)} %pad_add_fusion.quarters, bf16[1536,256]{1,0:T(8,128)(2,1)} %get-tuple-element.107.refs_0_, bf16[1536,256]{1,0:T(8,128)(2,1)} %copy-done.16, bf16[256,3840]{1,0:T(8,128)(2,1)} %get-tuple-element.103.refs_0_.refs_1_.refs_2_.refs_4_.refs_6_.refs_8_, ...), custom_call_target="tpu_custom_call" | custom-call | flops 15000000512 | bytes 60000000 | tf_op jit(solution)/shard_map/weight_grad/pallas_call | solution.py:434
  63.9 10.7 %attend_back.1 = (bf16[256,2304]{1,0:T(8,128)(2,1)}, f32[8,768]{1,0:T(8,128)}) custom-call(bf16[256,768]{1,0:T(8,128)(2,1)} %get-tuple-element.111.gb.refs_12_, bf16[256,768]{1,0:T(8,128)(2,1)} %get-tuple-element.112.q, bf16[256,768]{1,0:T(8,128)(2,1)} %get-tuple-element.113.k, bf16[256,768]{1,0:T(8,128)(2,1)} %get-tuple-element.114.v, ...), custom_call_target="tpu_custom_call" | custom-call | flops 27499999232 | bytes 110000000 | tf_op jit(solution)/shard_map/attend_back/pallas_call | solution.py:669
  74.5 4.2 %collective-permute-done.9.got = bf16[2,384,768]{2,1,0:T(8,128)(2,1)S(1)} collective-permute-done((bf16[2,384,768]{2,1,0:T(8,128)(2,1)}, bf16[2,384,768]{2,1,0:T(8,128)(2,1)S(1)}, u32[]{:S(2)}, u32[]{:S(2)}) %collective-permute-start.9) | collective-permute-done | bytes 1179680 | tf_op jit(solution)/shard_map/ppermute | solution.py:374
  79.8 2.2 %second.3 = bf16[384,768]{1,0:T(8,128)(2,1)} custom-call(bf16[2,384,768]{2,1,0:T(8,128)(2,1)} %get-tuple-element.123.keep, bf16[2,384,768]{2,1,0:T(8,128)(2,1)} %copy-done.14), custom_call_target="tpu_custom_call" | custom-call | flops 5000000000 | bytes 20000000 | tf_op jit(solution)/shard_map/second/pallas_call | solution.py:459
  83.6 7.9 %weight_grad.4 = (bf16[2,96,3840]{2,1,0:T(8,128)(2,1)}, bf16[2,96,3840]{2,1,0:T(8,128)(2,1)}) custom-call(s32[4]{0:T(128)} %pad_add_fusion.quarters, bf16[1152,256]{1,0:T(8,128)(2,1)} %get-tuple-element.125.refs_0_.refs_10_, bf16[1152,256]{1,0:T(8,128)(2,1)} %copy-done.18, ...), custom_call_target="tpu_custom_call" | custom-call | flops 15000000512 | bytes 60000000 | tf_op jit(solution)/shard_map/weight_grad/pallas_call | solution.py:434
  93.8 2.7 %third.3 = (f32[2,96,768]{2,1,0:T(8,128)}, bf16[2,96,768]{2,1,0:T(8,128)(2,1)}) custom-call(s32[1]{0:T(128)} %bitcast.band, bf16[2,384,768]{2,1,0:T(8,128)(2,1)} %get-tuple-element.123.keep, bf16[2,384,768]{2,1,0:T(8,128)(2,1)} %copy-done.14, bf16[384,768]{1,0:T(8,128)(2,1)} %copy-done.19), custom_call_target="tpu_custom_call" | custom-call | flops 7500000256 | bytes 30000000 | tf_op jit(solution)/shard_map/third/pallas_call | solution.py:482
  96.6 2.9 %collective-permute-start.16 = (bf16[2,96,768]{2,1,0:T(8,128)(2,1)}, bf16[2,96,768]{2,1,0:T(8,128)(2,1)S(1)}, u32[]{:S(2)}, u32[]{:S(2)}) collective-permute-start(bf16[2,96,768]{2,1,0:T(8,128)(2,1)} %get-tuple-element.124), channel_id=1, source_target_pairs={{0,1},{1,0},{2,3},{3,2},{4,5},{5,4},{6,7},{7,6},{8,9},{9,8},{10,11... | collective-permute-start | bytes 884744 | tf_op jit(solution)/shard_map/ppermute | solution.py:377
  99.5 6.0 %weight_grad.5 = (bf16[2,96,2304]{2,1,0:T(8,128)(2,1)}, bf16[2,96,2304]{2,1,0:T(8,128)(2,1)}) custom-call(s32[4]{0:T(128)} %pad_add_fusion.quarters, bf16[1152,256]{1,0:T(8,128)(2,1)} %get-tuple-element.125.refs_0_.refs_10_, bf16[1152,256]{1,0:T(8,128)(2,1)} %copy-done.18, bf16[256,2304]{1,0:T(8,128)(2,1)} %get-tuple-element.128.refs_2_.refs_4_.refs_6_, ...), custom_call_target="tpu_custom_call" | custom-call | flops 15000000512 | bytes 60000000 | tf_op jit(solution)/shard_map/weight_grad/pallas_call | solution.py:434
  106.1 5.0 %input_back.1 = (bf16[64,768]{1,0:T(8,128)(2,1)}, bf16[64,768]{1,0:T(8,128)(2,1)}, bf16[64,768]{1,0:T(8,128)(2,1)}, bf16[64,768]{1,0:T(8,128)(2,1)}, f32[384,128]{1,0:T(8,128)}, /*index=5*/f32[384,128]{1,0:T(8,128)}) custom-call(s32[1]{0:T(128)} %bitcast.5.core, bf16[72,768]{1,0:T(8,128)(2,1)} %get-tuple-element.93.refs_0_, bf16[72,768]{1,0:T(8,128)(2,1)} %copy-done.28, ...), custom_call_target="tpu_custom_call" | custom-call | flops 12499999744 | bytes 50000000 | tf_op jit(solution)/shard_map/input_back/pallas_call | solution.py:700
  117.1 2.4 %second.4 = bf16[96,3840]{1,0:T(8,128)(2,1)} custom-call(bf16[2,96,3840]{2,1,0:T(8,128)(2,1)} %get-tuple-element.141.keep, bf16[2,96,3840]{2,1,0:T(8,128)(2,1)} %copy-done.13), custom_call_target="tpu_custom_call" | custom-call | flops 5000000000 | bytes 20000000 | tf_op jit(solution)/shard_map/second/pallas_call | solution.py:459
  126.8 4.4 %collective-permute-done.19.more = bf16[96,3840]{1,0:T(8,128)(2,1)S(1)} collective-permute-done((bf16[96,3840]{1,0:T(8,128)(2,1)}, bf16[96,3840]{1,0:T(8,128)(2,1)S(1)}, u32[]{:S(2)}, u32[]{:S(2)}) %collective-permute-start.19) | collective-permute-done | bytes 737312 | tf_op jit(solution)/shard_map/ppermute | solution.py:374
  132.0 3.1 %third.4 = (f32[2,24,3840]{2,1,0:T(8,128)}, bf16[2,24,3840]{2,1,0:T(8,128)(2,1)}) custom-call(s32[1]{0:T(128)} %bitcast.band, bf16[2,96,3840]{2,1,0:T(8,128)(2,1)} %get-tuple-element.141.keep, bf16[2,96,3840]{2,1,0:T(8,128)(2,1)} %copy-done.13, bf16[96,3840]{1,0:T(8,128)(2,1)} %copy-done.17), custom_call_target="tpu_custom_call" | custom-call | flops 7500000256 | bytes 30000000 | tf_op jit(solution)/shard_map/third/pallas_call | solution.py:482
  138.5 2.4 %third.5 = (f32[2,24,2304]{2,1,0:T(8,128)}, bf16[2,24,2304]{2,1,0:T(8,128)(2,1)}) custom-call(s32[1]{0:T(128)} %bitcast.band, bf16[2,96,2304]{2,1,0:T(8,128)(2,1)} %get-tuple-element.145.keep, bf16[2,96,2304]{2,1,0:T(8,128)(2,1)} %copy-done.15, bf16[96,2304]{1,0:T(8,128)(2,1)} %copy-done.20), custom_call_target="tpu_custom_call" | custom-call | flops 7500000256 | bytes 30000000 | tf_op jit(solution)/shard_map/third/pallas_call | solution.py:482
  148.9 4.2 %collective-permute-done.28.got = bf16[2,24,3840]{2,1,0:T(8,128)(2,1)S(1)} collective-permute-done((bf16[2,24,3840]{2,1,0:T(8,128)(2,1)S(1)}, bf16[2,24,3840]{2,1,0:T(8,128)(2,1)S(1)}, u32[]{:S(2)}, u32[]{:S(2)}) %collective-permute-start.28) | collective-permute-done | bytes 368672 | tf_op jit(solution)/shard_map/ppermute | solution.py:377
  163.2 2.3 %gather.1 = (bf16[4,64,768]{2,1,0:T(8,128)(2,1)}, f32[4,64,768]{2,1,0:T(8,128)}) custom-call(s32[1]{0:T(128)} %bitcast.band, bf16[64,768]{1,0:T(8,128)(2,1)} %get-tuple-element.117.refs_0_, bf16[64,768]{1,0:T(8,128)(2,1)} %copy-done.32, bf16[64,768]{1,0:T(8,128)(2,1)} %copy-done.33, bf16[64,768]{1,0:T(8,128)(2,1)} %collective-permute-done.12.refs_3_, ...), custom_call_target="tpu_custom_call" | custom-call | flops 5000000000 | bytes 20000000 | tf_op jit(solution)/shard_map/gather/pallas_call | solution.py:732
  165.6 5.8 %collective-permute-done.31 = f32[24,128]{0,1:T(8,128)S(1)} collective-permute-done((f32[24,128]{0,1:T(8,128)S(1)}, f32[24,128]{0,1:T(8,128)S(1)}, u32[]{:S(2)}, u32[]{:S(2)}) %collective-permute-start.31) | collective-permute-done | bytes 12320 | tf_op jit(solution)/shard_map/ppermute | solution.py:377
  (180 shorter events, 60.5 us)
Async XLA Ops:
  5.8 13.6 %collective-permute-start.1 = (bf16[72,768]{1,0:T(8,128)(2,1)}, bf16[72,768]{1,0:T(8,128)(2,1)S(1)}, u32[]{:S(2)}, u32[]{:S(2)}) collective-permute-start(bf16[72,768]{1,0:T(8,128)(2,1)} %get-tuple-element.95), channel_id=1, source_target_pairs={{0,2},{1,3},{2,0},{3,1},{4,6},{5,7},{6,4},{7,5},{8,10},{9,11},{10,... | collective-permute-start | bytes 331784 | tf_op jit(solution)/shard_map/ppermute | solution.py:380
  10.4 18.8 %collective-permute-start.3 = (bf16[64,768]{1,0:T(8,128)(2,1)S(1)}, bf16[64,768]{1,0:T(8,128)(2,1)S(1)}, u32[]{:S(2)}, u32[]{:S(2)}) collective-permute-start(bf16[64,768]{1,0:T(8,128)(2,1)S(1)} %get-tuple-element.173), channel_id=1, source_target_pairs={{0,1},{1,2},{2,3},{3,0},{4,5},{5,6},{6,7},{7,4},{8,9},{9,10},{10,1... | collective-permute-start | bytes 294920 | tf_op jit(solution)/shard_map/ppermute | solution.py:380
  11.1 18.2 %collective-permute-start.4 = (bf16[64,768]{1,0:T(8,128)(2,1)S(1)}, bf16[64,768]{1,0:T(8,128)(2,1)S(1)}, u32[]{:S(2)}, u32[]{:S(2)}) collective-permute-start(bf16[64,768]{1,0:T(8,128)(2,1)S(1)} %get-tuple-element.172), channel_id=1, source_target_pairs={{0,2},{1,3},{2,0},{3,1},{4,6},{5,7},{6,4},{7,5},{8,10},{9,11},{10,... | collective-permute-start | bytes 294920 | tf_op jit(solution)/shard_map/ppermute | solution.py:380
  12.9 16.4 %collective-permute-start.5 = (bf16[64,768]{1,0:T(8,128)(2,1)S(1)}, bf16[64,768]{1,0:T(8,128)(2,1)S(1)}, u32[]{:S(2)}, u32[]{:S(2)}) collective-permute-start(bf16[64,768]{1,0:T(8,128)(2,1)S(1)} %get-tuple-element.171), channel_id=1, source_target_pairs={{0,3},{1,0},{2,1},{3,2},{4,7},{5,4},{6,5},{7,6},{8,11},{9,8},{10,9... | collective-permute-start | bytes 294920 | tf_op jit(solution)/shard_map/ppermute | solution.py:380
  29.1 17.6 %collective-permute-start.6 = (bf16[1152,256]{1,0:T(8,128)(2,1)}, bf16[1152,256]{1,0:T(8,128)(2,1)S(1)}, u32[]{:S(2)}, u32[]{:S(2)}) collective-permute-start(bf16[1152,256]{1,0:T(8,128)(2,1)} %get-tuple-element.104), channel_id=1, source_target_pairs={{0,4},{4,0},{8,12},{12,8},{16,20},{20,16},{24,28},{28,24},{1,5},{5... | collective-permute-start | bytes 1769480 | tf_op jit(solution)/shard_map/ppermute | solution.py:371
  39.8 14.5 %collective-permute-start.8 = (bf16[256,3840]{1,0:T(8,128)(2,1)}, bf16[256,3840]{1,0:T(8,128)(2,1)S(1)}, u32[]{:S(2)}, u32[]{:S(2)}) collective-permute-start(bf16[256,3840]{1,0:T(8,128)(2,1)} %get-tuple-element.103.refs_0_.refs_1_.refs_2_.refs_4_.refs_6_.refs_8_), channel_id=1, source_target_pairs={{0,4},{4,0},{8,12},{12,8},{16,20},{20,16},{24,28},{28,24},{1,5},{5... | collective-permute-start | bytes 5898248 | tf_op jit(solution)/shard_map/ppermute | solution.py:371
  40.9 13.2 %collective-permute-start.7 = (bf16[1536,256]{1,0:T(8,128)(2,1)}, bf16[1536,256]{1,0:T(8,128)(2,1)S(1)}, u32[]{:S(2)}, u32[]{:S(2)}) collective-permute-start(bf16[1536,256]{1,0:T(8,128)(2,1)} %get-tuple-element.108), channel_id=1, source_target_pairs={{0,4},{4,0},{8,12},{12,8},{16,20},{20,16},{24,28},{28,24},{1,5},{5... | collective-permute-start | bytes 2359304 | tf_op jit(solution)/shard_map/ppermute | solution.py:371
  41.0 41.1 %collective-permute-start.10 = (bf16[64,768]{1,0:T(8,128)(2,1)}, bf16[64,768]{1,0:T(8,128)(2,1)S(1)}, u32[]{:S(2)}, u32[]{:S(2)}) collective-permute-start(bf16[64,768]{1,0:T(8,128)(2,1)} %get-tuple-element.118), channel_id=1, source_target_pairs={{0,3},{1,0},{2,1},{3,2},{4,7},{5,4},{6,5},{7,6},{8,11},{9,8},{10,9... | collective-permute-start | bytes 294920 | tf_op jit(solution)/shard_map/ppermute | solution.py:380
  46.8 36.8 %collective-permute-start.11 = (bf16[64,768]{1,0:T(8,128)(2,1)}, bf16[64,768]{1,0:T(8,128)(2,1)S(1)}, u32[]{:S(2)}, u32[]{:S(2)}) collective-permute-start(bf16[64,768]{1,0:T(8,128)(2,1)} %get-tuple-element.119), channel_id=1, source_target_pairs={{0,2},{1,3},{2,0},{3,1},{4,6},{5,7},{6,4},{7,5},{8,10},{9,11},{10,... | collective-permute-start | bytes 294920 | tf_op jit(solution)/shard_map/ppermute | solution.py:380
  46.8 36.8 %collective-permute-start.12 = (bf16[64,768]{1,0:T(8,128)(2,1)}, bf16[64,768]{1,0:T(8,128)(2,1)}, u32[]{:S(2)}, u32[]{:S(2)}) collective-permute-start(bf16[64,768]{1,0:T(8,128)(2,1)} %get-tuple-element.120), channel_id=1, source_target_pairs={{0,1},{1,2},{2,3},{3,0},{4,5},{5,6},{6,7},{7,4},{8,9},{9,10},{10,1... | collective-permute-start | bytes 294920 | tf_op jit(solution)/shard_map/ppermute | solution.py:380
  54.2 29.4 %collective-permute-start.13 = (bf16[256,768]{1,0:T(8,128)(2,1)}, bf16[256,768]{1,0:T(8,128)(2,1)}, u32[]{:S(2)}, u32[]{:S(2)}) collective-permute-start(bf16[256,768]{1,0:T(8,128)(2,1)} %get-tuple-element.111.gb.refs_12_), channel_id=1, source_target_pairs={{0,4},{4,0},{8,12},{12,8},{16,20},{20,16},{24,28},{28,24},{1,5},{5... | collective-permute-start | bytes 1179656 | tf_op jit(solution)/shard_map/ppermute | solution.py:371
  62.4 16.4 %collective-permute-start.9 = (bf16[2,384,768]{2,1,0:T(8,128)(2,1)}, bf16[2,384,768]{2,1,0:T(8,128)(2,1)S(1)}, u32[]{:S(2)}, u32[]{:S(2)}) collective-permute-start(bf16[2,384,768]{2,1,0:T(8,128)(2,1)} %get-tuple-element.110), channel_id=1, source_target_pairs={{0,8},{4,20},{8,0},{12,28},{16,24},{20,4},{24,16},{28,12},{1,9},{5... | collective-permute-start | bytes 3538952 | tf_op jit(solution)/shard_map/ppermute | solution.py:374
  78.8 20.7 %collective-permute-start.15 = (bf16[256,2304]{1,0:T(8,128)(2,1)}, bf16[256,2304]{1,0:T(8,128)(2,1)}, u32[]{:S(2)}, u32[]{:S(2)}) collective-permute-start(bf16[256,2304]{1,0:T(8,128)(2,1)} %get-tuple-element.128.refs_2_.refs_4_.refs_6_), channel_id=1, source_target_pairs={{0,4},{4,0},{8,12},{12,8},{16,20},{20,16},{24,28},{28,24},{1,5},{5... | collective-permute-start | bytes 3538952 | tf_op jit(solution)/shard_map/ppermute | solution.py:371
  91.5 24.5 %collective-permute-start.17 = (bf16[2,96,3840]{2,1,0:T(8,128)(2,1)}, bf16[2,96,3840]{2,1,0:T(8,128)(2,1)S(1)}, u32[]{:S(2)}, u32[]{:S(2)}) collective-permute-start(bf16[2,96,3840]{2,1,0:T(8,128)(2,1)} %get-tuple-element.122), channel_id=1, source_target_pairs={{0,8},{4,20},{8,0},{12,28},{16,24},{20,4},{24,16},{28,12},{1,9},{5... | collective-permute-start | bytes 4423688 | tf_op jit(solution)/shard_map/ppermute | solution.py:374
  96.6 16.0 %collective-permute-start.16 = (bf16[2,96,768]{2,1,0:T(8,128)(2,1)}, bf16[2,96,768]{2,1,0:T(8,128)(2,1)S(1)}, u32[]{:S(2)}, u32[]{:S(2)}) collective-permute-start(bf16[2,96,768]{2,1,0:T(8,128)(2,1)} %get-tuple-element.124), channel_id=1, source_target_pairs={{0,1},{1,0},{2,3},{3,2},{4,5},{5,4},{6,7},{7,6},{8,9},{9,8},{10,11... | collective-permute-start | bytes 884744 | tf_op jit(solution)/shard_map/ppermute | solution.py:377
  105.5 16.0 %collective-permute-start.18 = (bf16[2,96,2304]{2,1,0:T(8,128)(2,1)}, bf16[2,96,2304]{2,1,0:T(8,128)(2,1)S(1)}, u32[]{:S(2)}, u32[]{:S(2)}) collective-permute-start(bf16[2,96,2304]{2,1,0:T(8,128)(2,1)} %get-tuple-element.127), channel_id=1, source_target_pairs={{0,8},{4,20},{8,0},{12,28},{16,24},{20,4},{24,16},{28,12},{1,9},{5... | collective-permute-start | bytes 2654216 | tf_op jit(solution)/shard_map/ppermute | solution.py:374
  111.1 31.5 %collective-permute-start.23 = (bf16[64,768]{1,0:T(8,128)(2,1)}, bf16[64,768]{1,0:T(8,128)(2,1)S(1)}, u32[]{:S(2)}, u32[]{:S(2)}) collective-permute-start(bf16[64,768]{1,0:T(8,128)(2,1)} %get-tuple-element.149), channel_id=1, source_target_pairs={{0,3},{1,0},{2,1},{3,2},{4,7},{5,4},{6,5},{7,6},{8,11},{9,8},{10,9... | collective-permute-start | bytes 294920 | tf_op jit(solution)/shard_map/ppermute | solution.py:380
  112.3 31.6 %collective-permute-start.24 = (bf16[64,768]{1,0:T(8,128)(2,1)}, bf16[64,768]{1,0:T(8,128)(2,1)S(1)}, u32[]{:S(2)}, u32[]{:S(2)}) collective-permute-start(bf16[64,768]{1,0:T(8,128)(2,1)} %get-tuple-element.150), channel_id=1, source_target_pairs={{0,2},{1,3},{2,0},{3,1},{4,6},{5,7},{6,4},{7,5},{8,10},{9,11},{10,... | collective-permute-start | bytes 294920 | tf_op jit(solution)/shard_map/ppermute | solution.py:380
  112.6 32.7 %collective-permute-start.25 = (bf16[64,768]{1,0:T(8,128)(2,1)}, bf16[64,768]{1,0:T(8,128)(2,1)S(1)}, u32[]{:S(2)}, u32[]{:S(2)}) collective-permute-start(bf16[64,768]{1,0:T(8,128)(2,1)} %get-tuple-element.151), channel_id=1, source_target_pairs={{0,1},{1,2},{2,3},{3,0},{4,5},{5,6},{6,7},{7,4},{8,9},{9,10},{10,1... | collective-permute-start | bytes 294920 | tf_op jit(solution)/shard_map/ppermute | solution.py:380
  124.4 12.5 %collective-permute-start.21 = (bf16[96,2304]{1,0:T(8,128)(2,1)}, bf16[96,2304]{1,0:T(8,128)(2,1)S(1)}, u32[]{:S(2)}, u32[]{:S(2)}) collective-permute-start(bf16[96,2304]{1,0:T(8,128)(2,1)} %second.5), channel_id=1, source_target_pairs={{0,16},{4,12},{8,24},{12,4},{16,0},{20,28},{24,8},{28,20},{1,17},{... | collective-permute-start | bytes 1327112 | tf_op jit(solution)/shard_map/ppermute | solution.py:374
  142.6 16.1 %collective-permute-start.30 = (bf16[2,24,2304]{2,1,0:T(8,128)(2,1)}, bf16[2,24,2304]{2,1,0:T(8,128)(2,1)S(1)}, u32[]{:S(2)}, u32[]{:S(2)}) collective-permute-start(bf16[2,24,2304]{2,1,0:T(8,128)(2,1)} %get-tuple-element.147), channel_id=1, source_target_pairs={{0,1},{1,0},{2,3},{3,2},{4,5},{5,4},{6,7},{7,6},{8,9},{9,8},{10,11... | collective-permute-start | bytes 663560 | tf_op jit(solution)/shard_map/ppermute | solution.py:377
  155.6 17.0 %collective-permute-start.32 = (bf16[24,3840]{1,0:T(8,128)(2,1)}, bf16[24,3840]{1,0:T(8,128)(2,1)S(1)}, u32[]{:S(2)}, u32[]{:S(2)}) collective-permute-start(bf16[24,3840]{1,0:T(8,128)(2,1)} %fourth.4), channel_id=1, source_target_pairs={{0,2},{1,3},{2,0},{3,1},{4,6},{5,7},{6,4},{7,5},{8,10},{9,11},{10,... | collective-permute-start | bytes 552968 | tf_op jit(solution)/shard_map/ppermute | solution.py:377
  157.8 13.5 %collective-permute-start.31 = (f32[24,128]{0,1:T(8,128)S(1)}, f32[24,128]{0,1:T(8,128)S(1)}, u32[]{:S(2)}, u32[]{:S(2)}) collective-permute-start(f32[24,128]{0,1:T(8,128)S(1)} %bitcast.56), channel_id=1, source_target_pairs={{0,2},{1,3},{2,0},{3,1},{4,6},{5,7},{6,4},{7,5},{8,10},{9,11},{10,... | collective-permute-start | bytes 36872 | tf_op jit(solution)/shard_map/ppermute | solution.py:377
  161.1 14.1 %collective-permute-start.33 = (bf16[24,2304]{1,0:T(8,128)(2,1)}, bf16[24,2304]{1,0:T(8,128)(2,1)S(1)}, u32[]{:S(2)}, u32[]{:S(2)}) collective-permute-start(bf16[24,2304]{1,0:T(8,128)(2,1)} %fourth.5), channel_id=1, source_target_pairs={{0,2},{1,3},{2,0},{3,1},{4,6},{5,7},{6,4},{7,5},{8,10},{9,11},{10,... | collective-permute-start | bytes 331784 | tf_op jit(solution)/shard_map/ppermute | solution.py:377
  (50 other events, 270.3 us)

commit v2 on v1

--- a/solution.py
+++ b/solution.py
@@ -145,8 +145,7 @@
     two, middle, mask, vec, w_up, b_up, w_down = refs[:7]
     cots = refs[7 : 7 + nb]
     act_keep, act_send, right_o, bsum = refs[7 + nb : 11 + nb]
-    outs = refs[11 + nb : 11 + 2 * nb]
-    acc = refs[11 + 2 * nb]
+    out_o, acc = refs[11 + nb :]
     j = pl.program_id(0)
     width = acc.shape[1]
 
@@ -169,9 +168,7 @@
     @pl.when(j == steps - 1)
     def _():
         col = column_of(mask[0:1, :])
-        out = (col * (middle[...] + (acc[...] + vec[BDOWN : BDOWN + 1, :]))).astype(BF16)
-        for s in range(nb):
-            outs[s][...] = out[s * rows : (s + 1) * rows, :]
+        out_o[...] = (col * (middle[...] + (acc[...] + vec[BDOWN : BDOWN + 1, :]))).astype(BF16)
 
 
 def down_kernel(rows, nb, steps, *refs):
@@ -243,19 +240,22 @@
     sums[2:8, :] = jnp.zeros((6, width), F32)
 
 
-def input_back_kernel(rows, nb, block, core, *refs):
+def input_back_kernel(rows, nb, block, core, band, *refs):
     slots = refs[:nb]
-    right, wq, wk, wv, gm, vec, down_sums, attend_sums = refs[nb : nb + 8]
-    outs = refs[nb + 8 : 2 * nb + 8]
-    keep_o, send_o = refs[2 * nb + 8 :]
+    right, wq, wk, wv, gm, vec, down_sums, attend_sums, up_cols = refs[nb : nb + 9]
+    result, own_o, near_o, far_o, keep_o, send_o, held = refs[nb + 9 :]
     width = gm.shape[1]
     grad = dot_nt(right[:, :width], wq[...])
     grad = grad + dot_nt(right[:, width : 2 * width], wk[...])
     grad = grad + dot_nt(right[:, 2 * width :], wv[...])
     n1, r1 = norm_stats(join(slots, rows).astype(F32))
     gx = (gm[...] + norm_back(grad, n1, r1, vec[GAIN1 : GAIN1 + 1, :])).astype(BF16)
-    for s in range(nb):
-        outs[s][...] = gx[s * rows : (s + 1) * rows, :]
+    held[...] = gx
+    for bits, out, at in ((0, own_o, 0), (1, near_o, 0), (3, near_o, 2 * rows), (2, far_o, 0)):
+        slot = lax.rem(band[0] - jnp.bitwise_xor(band[0], bits) + nb, nb)
+        tokens = pl.ds(pl.multiple_of(slot * rows, 16), rows)
+        out[at : at + rows, :] = result[tokens, :]
+        out[at + rows : at + 2 * rows, :] = held[tokens, :]
     table = jnp.concatenate(
         [
             down_sums[...], attend_sums[...], colsum(grad * n1), colsum(grad),
@@ -263,7 +263,7 @@
         ],
         axis=0,
     )
-    split_rows(jnp.transpose(table), block, core[0], keep_o, send_o)
+    split_rows(jnp.transpose(table) + up_cols[...], block, core[0], keep_o, send_o)
 
 
 def spread_kernel(rows, nb, band, crop_rows, crop_cols, x, keep_mask, *outs):
@@ -283,14 +283,15 @@
         outs[s][rows:, :] = jnp.where((slot == s) & (lane == s), flags, 0.0).astype(BF16)
 
 
-def gather_kernel(nb, band, *refs):
-    for s in range(nb):
-        image = lax.rem(band[0] + s, nb)
-        refs[2 * nb][image] = refs[s][...]
-        refs[2 * nb + 1][image] = refs[nb + s][...].astype(F32)
-
-
-def weight_kernel(groups, quarters, *refs):
+def gather_kernel(band, own, near, far, output, grad):
+    rows = output.shape[1]
+    for bits, ref, at in ((0, own, 0), (1, near, 0), (2, far, 0), (3, far, 2 * rows)):
+        image = jnp.bitwise_xor(band[0], bits)
+        output[image] = ref[at : at + rows, :]
+        grad[image] = ref[at + rows : at + 2 * rows, :].astype(F32)
+
+
+def weight_kernel(groups, extra, quarters, *refs):
     t = pl.program_id(0)
     parts, at = [], 0
     for widths in groups:
@@ -300,6 +301,9 @@
             right, right_got = refs[at : at + 2]
             at += 2
             parts.append((dot_nn(left[...], right[...]) + dot_nn(left_got[...], right_got[...])).astype(BF16))
+    if extra:
+        parts.append((refs[at][...] + refs[at + 1][...]).astype(BF16))
+        at += 2
     send, keep = refs[at:]
     g = parts[0] if len(parts) == 1 else jnp.concatenate(parts, axis=1)
 
@@ -325,15 +329,22 @@
         send_o[i] = held[pl.ds(pl.multiple_of(far * size, 8), size), :].astype(BF16)
 
 
-def last_kernel(widths, keep, got, more, *outs):
+def last_kernel(widths, vectors, keep, got, more, *outs):
     at = 0
     for w, out in zip(widths, outs):
         cols = pl.ds(at, w)
         out[...] = keep[0, :, cols] + got[0, :, cols].astype(F32) + more[:, cols].astype(F32)
         at += w
+    if vectors:
+        cols = pl.ds(at, COLS)
+        table = jnp.transpose(keep[0, :, cols] + got[0, :, cols].astype(F32) + more[:, cols].astype(F32))
+        for (first, n), out in zip(vectors, outs[len(widths) :]):
+            out[...] = jnp.concatenate([table[first + i : first + i + 1, :] for i in range(n)], axis=1)
 
 
 COLS = 128
+LIMIT = pltpu.CompilerParams(vmem_limit_bytes=20 * 1024 * 1024)
+USED = (16, 17, 8, 9, 2, 0, 1, 3)
 
 
 VM = pl.BlockSpec(memory_space=pltpu.VMEM)
@@ -345,7 +356,7 @@
 
 
 def cost(us):
-    return pl.CostEstimate(flops=us * 2500000000, bytes_accessed=us * 10000000, transcendentals=0)
+    return pl.CostEstimate(flops=int(us * 2500000000), bytes_accessed=int(us * 10000000), transcendentals=0)
 
 
 def after(x, *others):
@@ -403,8 +414,8 @@
 
 
 class Unit:
-    def __init__(self, links, rows, groups):
-        self.links = links
+    def __init__(self, links, rows, groups, extra=()):
+        self.links, self.vectors = links, []
         args, specs, widths = [], [], []
         tokens = groups[0][0].shape[1]
         self.block = block = rows // 4
@@ -419,7 +430,11 @@
                 args += [own, got]
                 specs.append(pl.BlockSpec((tokens, w), lambda t, s, i=own_at: (0, i)))
                 specs.append(pl.BlockSpec((tokens, w), lambda t, s, i=got_at: (0, i)))
-        self.widths = [w for ws in widths for w in ws]
+        for x in extra:
+            args.append(links.by_quarter(x))
+            specs.append(pl.BlockSpec((block, COLS), lambda t, s: (s[t], 0)))
+        self.extra = len(extra) > 0
+        self.widths = [w for ws in widths for w in ws] + [COLS] * self.extra
         self.cols = cols = sum(self.widths)
         p, q = links.p, links.q
         even = links.c == 0
@@ -432,7 +447,7 @@
         ).astype(jnp.int32)
         one = lambda x: jnp.asarray(x).astype(jnp.int32)
         self.send, self.keep = pl.pallas_call(
-            functools.partial(weight_kernel, widths),
+            functools.partial(weight_kernel, widths, self.extra),
             grid_spec=pltpu.PrefetchScalarGridSpec(
                 num_scalar_prefetch=1,
                 grid=(4,),
@@ -443,7 +458,8 @@
                 ],
             ),
             out_shape=[shape(2, block, cols)] * 2,
-            cost_estimate=cost(6),
+            cost_estimate=cost(0.1 if extra else 6),
+            compiler_params=LIMIT,
             name="weight_grad",
         )(quarters, *args)
         self.got = links.flip_by_core(self.send, 2, 4)
@@ -463,6 +479,7 @@
             out_specs=self.whole(*dims),
             out_shape=shape(*dims),
             cost_estimate=cost(2),
+            compiler_params=LIMIT,
             name="second",
         )(after(self.keep, *deps), self.got)
         self.more = self.links.flip_by_core(sent, 4, 2)
@@ -487,6 +504,7 @@
                 out_shape=[shape(2, size, cols, dtype=F32), shape(2, size, cols)],
                 scratch_shapes=[pltpu.VMEM((self.block, cols), F32)],
                 cost_estimate=cost(3),
+                compiler_params=LIMIT,
                 name="third",
             )(scalar(links.b), keep, self.got, self.more)
         self.near_got = links.flip_band(sent, 1)
@@ -502,6 +520,7 @@
             out_specs=self.whole(*dims),
             out_shape=shape(*dims),
             cost_estimate=cost(2),
+            compiler_params=LIMIT,
             name="fourth",
         )(after(self.near, *deps), self.near_got)
         self.far_got = self.links.flip_band(sent, 2)
@@ -510,61 +529,18 @@
     def last(self, *deps):
         dims = (self.size, self.cols)
         pick = pl.BlockSpec((1,) + dims, lambda _: (0, 0, 0))
+        vectors = self.vectors
+        outs = [(self.size, w) for w in self.widths] + [(1, n * self.size) for _, n in vectors]
         return pl.pallas_call(
-            functools.partial(last_kernel, self.widths),
+            functools.partial(last_kernel, self.widths, vectors),
             grid=(1,),
             in_specs=[pick, pick, self.whole(*dims)],
-            out_specs=[self.whole(self.size, w) for w in self.widths],
-            out_shape=[shape(self.size, w, dtype=F32) for w in self.widths],
+            out_specs=[self.whole(*d) for d in outs],
+            out_shape=[shape(*d, dtype=F32) for d in outs],
             cost_estimate=cost(2),
+            compiler_params=LIMIT,
             name="last",
         )(after(self.near, *deps), self.near_got, self.far_got)
-
-
-class Table:
-    def __init__(self, links, keep, send):
-        self.links, self.keep, self.send = links, keep, send
-
-    def start(self, *deps):
-        self.got = self.links.flip(after(self.send, *deps), 1)
-
-    def core(self, *deps):
-        links = self.links
-        x = links.by_quarter(after(self.keep, *deps) + self.got)
-        x = x.reshape(2, 2, -1, x.shape[1])
-        self.keep = take(x, links.p, 1)
-        self.send = take(x, 1 - links.p, 1)
-        self.got = links.flip(self.send, 2)
-        return self.send
-
-    def near(self, *deps):
-        links = self.links
-        x = after(self.keep, *deps) + self.got
-        self.keep = take(x, links.q, 0)
-        self.send = take(x, 1 - links.q, 0)
-        self.got = links.flip(self.send, 4)
-        return self.send
-
-    def band(self, *deps):
-        links, nb = self.links, self.links.nb
-        x = links.sum_hi(after(self.keep, *deps) + self.got)
-        x = x.reshape(2, 2, -1, x.shape[1])
-        low, high = links.b & 1, links.b >> 1
-        self.keep = take(x, low, 1)
-        self.send = take(x, 1 - low, 1)
-        self.got = links.flip_band(self.send, 1)
-        return self.send
-
-    def far(self, *deps):
-        high = self.links.b >> 1
-        x = after(self.keep, *deps) + self.got
-        self.keep = take(x, high, 0)
-        self.send = take(x, 1 - high, 0)
-        self.got = self.links.flip_band(self.send, 2)
-        return self.send
-
-    def last(self, *deps):
-        return after(self.keep, *deps) + self.got
 
 
 def per_device(
@@ -631,20 +607,17 @@
                 pl.BlockSpec((wide, width), lambda j, c: (j, 0)),
             ] + [fixed(rows, width)] * nb,
             out_specs=[pl.BlockSpec((wide // 2, tokens), lambda j, c: (j, 0))] * 2
-            + [fixed(tokens, width + hidden_width), tall(8, wide)]
-            + [fixed(rows, width)] * nb,
+            + [fixed(tokens, width + hidden_width), tall(8, wide), fixed(tokens, width)],
             scratch_shapes=[pltpu.VMEM((tokens, width), F32)],
         ),
         out_shape=[shape(hidden_width // 2, tokens)] * 2
-        + [shape(tokens, width + hidden_width), shape(8, hidden_width, dtype=F32)]
-        + [shape(rows, width)] * nb,
+        + [shape(tokens, width + hidden_width), shape(8, hidden_width, dtype=F32), full],
         cost_estimate=cost(10),
         name="up",
     )(core, two, middle, mask, vec, w_up, b_up_row, w_down, *cots)
-    act_keep, act_send, right, up_sums = up[:4]
+    act_keep, act_send, right, up_sums, result = up
     act_got = links.flip(act_send, 1)
     right_got = links.flip(right, 1)
-    out_blocks = [up[4]] + [links.band_shift(up[4 + s], -s) for s in range(1, nb)]
 
     grad_middle, grad_branch, down_sums = pl.pallas_call(
         functools.partial(down_kernel, rows, nb, steps),
@@ -665,6 +638,16 @@
         links, hidden_width // 2,
         [(after(act_keep, grad_branch), act_got, 0, [(width, right, 0, right_got, 0)])],
     )
+    unit_up = Unit(
+        links, half,
+        [
+            (
+                after(left_keep, unit_down.send), left_got, 2,
+                [(width, right, 1 + i, right_got, 1 + i) for i in range(hidden_width // width)],
+            ),
+            (left_keep, left_got, 1, [(width, grad_branch, 0, branch_got, 0)]),
+        ],
+    )
     low = lambda: pltpu.VMEM((width, tokens), BF16)
     back_right, attend_sums = pl.pallas_call(
         attend_back_kernel,
@@ -676,73 +659,71 @@
             pltpu.VMEM((width, tokens), F32), pltpu.VMEM((width, tokens), F32),
         ],
         cost_estimate=cost(11),
+        compiler_params=LIMIT,
         name="attend_back",
-    )(after(grad_branch, unit_down.send), q, k, v, mask, w_out)
+    )(after(grad_branch, unit_up.send), q, k, v, mask, w_out)
     back_got = links.flip(back_right, 1)
 
     mark = unit_down.second(back_right)
-    unit_up = Unit(
-        links, half,
-        [
-            (
-                after(left_keep, mark, *out_blocks), left_got, 2,
-                [(width, right, 1 + i, right_got, 1 + i) for i in range(hidden_width // width)],
-            ),
-            (left_keep, left_got, 1, [(width, grad_branch, 0, branch_got, 0)]),
-        ],
+    per_row = hidden_width // width
+    up_cols = up_sums[0].reshape(n_img * nb, per_row, -1).swapaxes(1, 2).reshape(width, per_row)
+    up_cols = jnp.pad(up_cols, ((0, 0), (18, COLS - 18 - per_row)))
+    back = pl.pallas_call(
+        functools.partial(input_back_kernel, rows, nb, block if aligned else half),
+        in_specs=[SM] * 2 + [VM] * (nb + 10),
+        out_specs=[VM] * 5,
+        out_shape=[shape(2 * rows, width), shape(4 * rows, width), shape(2 * rows, width)]
+        + [shape(half, COLS, dtype=F32)] * 2,
+        scratch_shapes=[pltpu.VMEM((tokens, width), BF16)],
+        cost_estimate=cost(5),
+        compiler_params=LIMIT,
+        name="input_back",
+    )(
+        core if aligned else jnp.zeros_like(core), band,
+        *slots, after(back_right, mark), w_query, w_key, w_value, grad_middle, vec, down_sums, attend_sums, up_cols,
+        result,
     )
-    mark = unit_down.third(unit_up.send)
+    blocks, table = back[:3], back[3:]
+    near_got = links.flip_band(blocks[1], 1)
+    if not aligned:
+        table = links.reclass(*table, block)
+    table_got = links.flip(table[1], 1)
+
     unit_qkv = Unit(
         links, half,
-        [(after(left_keep, mark), left_got, 0, [(width, back_right, i, back_got, i) for i in range(3)])],
+        [(after(left_keep, blocks[0]), left_got, 0, [(width, back_right, i, back_got, i) for i in range(3)])],
+        (table[0], table_got),
     )
-
-    back = pl.pallas_call(
-        functools.partial(input_back_kernel, rows, nb, block if aligned else half),
-        in_specs=[SM] + [VM] * (nb + 8),
-        out_specs=[VM] * (nb + 2),
-        out_shape=[shape(rows, width)] * nb + [shape(half, COLS, dtype=F32)] * 2,
-        cost_estimate=cost(5),
-        name="input_back",
-    )(
-        core if aligned else jnp.zeros_like(core),
-        *slots, after(back_right, unit_qkv.send), w_query, w_key, w_value, grad_middle, vec, down_sums, attend_sums,
-    )
-    table_pair = back[nb:]
-    if not aligned:
-        table_pair = links.reclass(*table_pair, block)
-    grad_blocks = [back[0]] + [links.band_shift(back[s], -s) for s in range(1, nb)]
-    mark = unit_down.fourth(back[0])
-    mark = unit_up.second(mark)
+    far_got = links.flip_band(jnp.concatenate([after(blocks[2], unit_qkv.send), near_got[2 * rows :, :]]), 2)
+    mark = unit_up.second(unit_qkv.send)
+    mark = unit_down.third(mark)
     mark = unit_qkv.second(mark)
-    up_cols = after(up_sums, mark)[0].reshape(width, hidden_width // width)
-    up_cols = jnp.pad(up_cols, ((0, 0), (18, COLS - 18 - hidden_width // width))).reshape(-1, 2, block, COLS)
-    class_of = lambda c: take(up_cols, c, 1).reshape(half, COLS)
-    table = Table(links, table_pair[0] + class_of(links.c), table_pair[1] + class_of(1 - links.c))
-    table.start()
     mark = unit_up.third(mark)
-    mark = table.core(mark)
+    mark = unit_down.fourth(mark)
     mark = unit_qkv.third(mark)
-    mark = table.near(mark)
-    (g_w_down,) = unit_down.last(mark, *grad_blocks)
-    mark = table.band(g_w_down)
     mark = unit_up.fourth(mark)
-    mark = table.far(mark)
     mark = unit_qkv.fourth(mark)
+    (g_w_down,) = unit_down.last(mark)
     output, grad_inputs = pl.pallas_call(
-        functools.partial(gather_kernel, nb),
-        in_specs=[SM] + [VM] * (2 * nb),
+        gather_kernel,
+        in_specs=[SM] + [VM] * 3,
         out_specs=[VM] * 2,
         out_shape=[shape(nb, rows, width), shape(nb, rows, width, dtype=F32)],
         cost_estimate=cost(2),
+        compiler_params=LIMIT,
         name="gather",
-    )(after(band, mark), *out_blocks, *grad_blocks)
-    cols = table.last(output)
+    )(after(band, g_w_down), blocks[0], near_got, far_got)
+    mark = output
     unit_up.widths = [hidden_width, width]
-    g_w_up, g_w_out = unit_up.last(cols)
-    g_w_query, g_w_key, g_w_value = unit_qkv.last(g_w_up)
-    sums = [cols[:, i] for i in range(18)]
-    g_b_up = cols[:, 18 : 18 + hidden_width // width].reshape(-1)
+    g_w_up, g_w_out = unit_up.last(mark)
+    if unit_qkv.size % 8 == 0:
+        unit_qkv.widths = [width] * 3
+        unit_qkv.vectors = [(i, 1) for i in USED] + [(18, per_row)]
+        g_w_query, g_w_key, g_w_value, *rest = unit_qkv.last(g_w_up)
+        sums = {i: x[0] for i, x in zip(USED + (18,), rest)}
+    else:
+        g_w_query, g_w_key, g_w_value, cols = unit_qkv.last(g_w_up)
+        sums = [cols[:, i] for i in range(18)] + [cols[:, 18 : 18 + per_row].swapaxes(0, 1).reshape(-1)]
     return (
         output,
         grad_inputs,
@@ -758,7 +739,7 @@
         sums[0],
         sums[1],
         g_w_up,
-        g_b_up,
+        sums[18],
         g_w_down,
         sums[3],
     )

time: 179 us -> 146 us (0.82)
  Pallas kernels: 91 us -> 55.4 us
  waiting for transfers between devices: 24.7 us -> 36.3 us
  local copies, waits for them, and re-layouts: 16.2 us -> 6.79 us
    ppermute x8, starting transfers between devices: 11.9 us -> 23.6 us  [flip_band(): return lax.ppermute(x, 'band', [(k, k ^ bit) for k in range(self.nb)])]
    pallas_call x7, Pallas kernels: 27.7 us -> 16.2 us  [the longest x3 12.8 us: __init__(): pl.pallas_call(functools.partial(weight_kernel, widths, self.extra), grid...]
    ppermute x12 -> x6, starting transfers between devices: 20.4 us -> 10.8 us  [band_shift(): lax.ppermute(x, 'band', [(k, (k + s) % self.nb) for k in range(self.nb)])]
    ppermute x6, waiting for transfers between devices: 9.12 us -> 17.8 us  [flip_by_core(): lax.ppermute(x, 'img', [(k, k ^ (odd if k & 1 else even)) for k in range(...]
    unnamed x80 -> x72, local copies, waits for them, and re-layouts: 12.4 us -> 4.56 us
    pallas_call x3, Pallas kernels: 8.22 us -> 1.25 us  [third(): pl.pallas_call(functools.partial(third_kernel, size), grid=(1,), in_specs...]
    pallas_call x3, Pallas kernels: 6.58 us -> 0.42 us  [second(): pl.pallas_call(second_kernel, grid=(1,), in_specs=[self.pick(1)] * 2, out...]
    pallas_call x3, Pallas kernels: 5.1 us -> 0.1 us  [fourth(): pl.pallas_call(second_kernel, grid=(1,), in_specs=[pick] * 2, out_specs=s...]
  transfers between devices with their start and end apart: 34 -> 26, of which waited for: 8 -> 8; matrix products, arithmetic and copies ran while one was open for 3% -> 2% of each run, Pallas kernels for 49% -> 36%
where the time goes in v2:
time: 146 us; the launch traced here: 145 us
  Pallas kernels  55.4 us (38%)
  starting transfers between devices  44.2 us (30%)
  waiting for transfers between devices  36.3 us (25%)
  local copies, waits for them, and re-layouts  6.79 us (5%)
    ppermute x8, starting transfers between devices, flip_band(): return lax.ppermute(x, 'band', [(k, k ^ bit) for k in range(self.nb)])  23.6 us
    ppermute x6, waiting for transfers between devices, flip_by_core(): lax.ppermute(x, 'img', [(k, k ^ (odd if k & 1 else even)) for k in range(...  17.8 us
    ppermute x8, waiting for transfers between devices, flip_band(): return lax.ppermute(x, 'band', [(k, k ^ bit) for k in range(self.nb)])  14.8 us
    pallas_call x3, Pallas kernels, __init__(): pl.pallas_call(functools.partial(weight_kernel, widths, self.extra), grid...  12.8 us
    ppermute x6, starting transfers between devices, band_shift(): lax.ppermute(x, 'band', [(k, (k + s) % self.nb) for k in range(self.nb)])  10.8 us
    pallas_call x1, Pallas kernels, per_device(): pl.pallas_call(functools.partial(up_kernel, rows, nb, steps, up_block), g...  9.86 us
    pallas_call x1, Pallas kernels, per_device(): pl.pallas_call(functools.partial(attend_kernel, rows, nb, block if aligne...  9.08 us
    ppermute x6, starting transfers between devices, flip_by_core(): lax.ppermute(x, 'img', [(k, k ^ (odd if k & 1 else even)) for k in range(...  8.06 us
  transfers between devices with their start and end apart: 26, of which 8 were waited for; matrix products, arithmetic and copies ran while one was open for 2% of the time, Pallas kernels for 36%

profile of v2, /device:TPU:0, one launch (start us, length us, event | category | flops | bytes accessed | tf_op | source)
XLA Modules:
  0.0 145.4 jit_solution(11313932504796943872)
XLA Ops:
  0.8 2.0 %spread.1 = (bf16[72,768]{1,0:T(8,128)(2,1)}, bf16[72,768]{1,0:T(8,128)(2,1)}, bf16[72,768]{1,0:T(8,128)(2,1)}, bf16[72,768]{1,0:T(8,128)(2,1)}) custom-call(s32[1]{0:T(128)} %bitcast.band, s32[4]{0:T(128)} %crop_rows.1, s32[4]{0:T(128)} %crop_cols.1, bf16[4,64,768]{2,1,0:T(8,128)(2,1)} %x.3, s32[4,64]{1,0:T(4,128)} %keep_mask.1), custom_call_target="tpu_custom_call" | custom-call | flops 5000000000 | bytes 20000000 | tf_op jit(solution)/shard_map/spread/pallas_call | solution.py:558
  2.8 3.1 %collective-permute-start = (bf16[72,768]{1,0:T(8,128)(2,1)}, bf16[72,768]{1,0:T(8,128)(2,1)S(1)}, u32[]{:S(2)}, u32[]{:S(2)}) collective-permute-start(bf16[72,768]{1,0:T(8,128)(2,1)} %get-tuple-element.94), channel_id=1, source_target_pairs={{0,1},{1,2},{2,3},{3,0},{4,5},{5,6},{6,7},{7,4},{8,9},{9,10},{10,1... | collective-permute-start | bytes 331784 | tf_op jit(solution)/shard_map/ppermute | solution.py:391
  5.8 2.6 %collective-permute-start.1 = (bf16[72,768]{1,0:T(8,128)(2,1)}, bf16[72,768]{1,0:T(8,128)(2,1)S(1)}, u32[]{:S(2)}, u32[]{:S(2)}) collective-permute-start(bf16[72,768]{1,0:T(8,128)(2,1)} %get-tuple-element.95), channel_id=1, source_target_pairs={{0,2},{1,3},{2,0},{3,1},{4,6},{5,7},{6,4},{7,5},{8,10},{9,11},{10,... | collective-permute-start | bytes 331784 | tf_op jit(solution)/shard_map/ppermute | solution.py:391
  12.9 2.8 %collective-permute-start.5 = (bf16[64,768]{1,0:T(8,128)(2,1)S(1)}, bf16[64,768]{1,0:T(8,128)(2,1)S(1)}, u32[]{:S(2)}, u32[]{:S(2)}) collective-permute-start(bf16[64,768]{1,0:T(8,128)(2,1)S(1)} %get-tuple-element.169), channel_id=1, source_target_pairs={{0,3},{1,0},{2,1},{3,2},{4,7},{5,4},{6,5},{7,6},{8,11},{9,8},{10,9... | collective-permute-start | bytes 294920 | tf_op jit(solution)/shard_map/ppermute | solution.py:391
  15.7 3.7 %collective-permute-done.1.refs_2_ = bf16[72,768]{1,0:T(8,128)(2,1)S(1)} collective-permute-done((bf16[72,768]{1,0:T(8,128)(2,1)}, bf16[72,768]{1,0:T(8,128)(2,1)S(1)}, u32[]{:S(2)}, u32[]{:S(2)}) %collective-permute-start.1) | collective-permute-done | bytes 110624 | tf_op jit(solution)/shard_map/ppermute | solution.py:391
  20.1 9.1 %attend.1 = (bf16[1152,256]{1,0:T(8,128)(2,1)}, bf16[1152,256]{1,0:T(8,128)(2,1)}, bf16[256,768]{1,0:T(8,128)(2,1)}, bf16[256,768]{1,0:T(8,128)(2,1)}, bf16[256,...) custom-call(s32[1]{0:T(128)} %bitcast.5.core, ...), custom_call_target="tpu_custom_call" | custom-call | flops 22499999744 | bytes 90000000 | tf_op jit(solution)/shard_map/attend/pallas_call | solution.py:579
  30.0 9.9 %up.1 = (bf16[1536,256]{1,0:T(8,128)(2,1)}, bf16[1536,256]{1,0:T(8,128)(2,1)}, bf16[256,3840]{1,0:T(8,128)(2,1)}, f32[8,3072]{1,0:T(8,128)}, bf16[256,768]{1,0:T(8,128)(2,1)}) custom-call(s32[1]{0:T(128)} %bitcast.5.core, bf16[256,768]{1,0:T(8,128)(2,1)} %get-tuple-element.97.refs_0_, f32[256,768]{1,0:T(8,128)} %get-tuple-element.104.refs_1_.refs_3_, ...), custom_call_target="tpu_custom_call" | custom-call | flops 24999999488 | bytes 100000000 | tf_op jit(solution)/shard_map/up/pallas_call | solution.py:599
  42.0 6.9 %down.1 = (f32[256,768]{1,0:T(8,128)}, bf16[256,768]{1,0:T(8,128)(2,1)}, f32[8,768]{1,0:T(8,128)}) custom-call(bf16[256,3840]{1,0:T(8,128)(2,1)} %get-tuple-element.102.refs_0_.refs_1_.refs_2_.refs_4_.refs_6_.refs_8_, bf16[256,3840]{1,0:T(8,128)(2,1)} %get-tuple-element.102.refs_0_.refs_1_.refs_2_.refs_4_.refs_6_.refs_8_, bf16[768,3072]{1,0:T(8,128)(2,1)} %refs_2_.1, ...), custom_call_target="tpu_custom_call" | custom-call | flops 17500000256 | bytes 70000000 | tf_op jit(solution)/shard_map/down/pallas_call | solution.py:622
  50.6 4.3 %weight_grad.3 = (bf16[2,384,768]{2,1,0:T(8,128)(2,1)S(1)}, bf16[2,384,768]{2,1,0:T(8,128)(2,1)S(1)}) custom-call(s32[4]{0:T(128)S(1)} %pad_add_fusion.quarters, bf16[1536,256]{1,0:T(8,128)(2,1)S(1)} %copy-done.16, bf16[1536,256]{1,0:T(8,128)(2,1)} %collective-permute-done.7.refs_1_, bf16[256,3840]{1,0:T(8,128)(2,1)S(1)} %copy-done.2, ...), custom_call_target="tpu_custom_call" | custom-call | flops 15000000512 | bytes 60000000 | tf_op jit(solution)/shard_map/weight_grad/pallas_call | solution.py:449
  56.4 5.4 %weight_grad.4 = (bf16[2,96,3840]{2,1,0:T(8,128)(2,1)S(1)}, bf16[2,96,3840]{2,1,0:T(8,128)(2,1)S(1)}) custom-call(s32[4]{0:T(128)S(1)} %pad_add_fusion.quarters, bf16[1152,256]{1,0:T(8,128)(2,1)S(1)} %copy-done, bf16[1152,256]{1,0:T(8,128)(2,1)S(1)} %collective-permute-done.6.refs_1_.refs_11_, bf16[256,3840]{1,0:T(8,128)(2,1)S(1)} %copy-done.2, ...), custom_call_target="tpu_custom_call" | custom-call | flops 15000000512 | bytes 60000000 | tf_op jit(solution)/shard_map/weight_grad/pallas_call | solution.py:449
  62.6 8.0 %attend_back.1 = (bf16[256,2304]{1,0:T(8,128)(2,1)S(1)}, f32[8,768]{1,0:T(8,128)S(1)}) custom-call(bf16[256,768]{1,0:T(8,128)(2,1)S(1)} %copy-done.7, bf16[256,768]{1,0:T(8,128)(2,1)S(1)} %copy-done.18, bf16[256,768]{1,0:T(8,128)(2,1)S(1)} %copy-done.19, bf16[256,768]{1,0:T(8,128)(2,1)S(1)} %copy-done.20, f32[8,256]{1,0:T(8,128)S(1)} %copy-done.22, ...), custom_call_target="tpu_custom_call" | custom-call | flops 27499999232 | bytes 110000000 | tf_op jit(solution)/shard_map/attend_back/pallas_call | solution.py:652
  76.7 3.8 %collective-permute-start.22 = (bf16[256,768]{1,0:T(8,128)(2,1)S(1)}, bf16[256,768]{1,0:T(8,128)(2,1)S(1)}, u32[]{:S(2)}, u32[]{:S(2)}) collective-permute-start(bf16[256,768]{1,0:T(8,128)(2,1)S(1)} %get-tuple-element.148), channel_id=1, source_target_pairs={{0,1},{1,0},{2,3},{3,2},{4,5},{5,4},{6,7},{7,6},{8,9},{9,8},{10,11... | collective-permute-start | bytes 1179656 | tf_op jit(solution)/shard_map/ppermute | solution.py:388
  80.5 3.1 %weight_grad.5 = (bf16[2,96,2432]{2,1,0:T(8,128)(2,1)S(1)}, bf16[2,96,2432]{2,1,0:T(8,128)(2,1)S(1)}) custom-call(s32[4]{0:T(128)S(1)} %pad_add_fusion.quarters, bf16[1152,256]{1,0:T(8,128)(2,1)S(1)} %copy-done, bf16[1152,256]{1,0:T(8,128)(2,1)S(1)} %collective-permute-done.6.refs_1_.refs_11_, ...), custom_call_target="tpu_custom_call" | custom-call | flops 250000000 | bytes 1000000 | tf_op jit(solution)/shard_map/weight_grad/pallas_call | solution.py:449
  85.1 8.2 %collective-permute-done.13.got = bf16[2,96,3840]{2,1,0:T(8,128)(2,1)S(1)} collective-permute-done((bf16[2,96,3840]{2,1,0:T(8,128)(2,1)S(1)}, bf16[2,96,3840]{2,1,0:T(8,128)(2,1)S(1)}, u32[]{:S(2)}, u32[]{:S(2)}) %collective-permute-start.13) | collective-permute-done | bytes 1474592 | tf_op jit(solution)/shard_map/ppermute | solution.py:385
  95.0 3.0 %collective-permute-start.23 = (bf16[256,768]{1,0:T(8,128)(2,1)S(1)}, bf16[256,768]{1,0:T(8,128)(2,1)S(1)}, u32[]{:S(2)}, u32[]{:S(2)}) collective-permute-start(bf16[256,768]{1,0:T(8,128)(2,1)S(1)} %pad_maximum_fusion), channel_id=1, source_target_pairs={{0,2},{1,3},{2,0},{3,1},{4,6},{5,7},{6,4},{7,5},{8,10},{9,11},{10,... | collective-permute-start | bytes 1179656 | tf_op jit(solution)/shard_map/ppermute | solution.py:388
  98.4 3.6 %collective-permute-start.17 = (bf16[2,96,768]{2,1,0:T(8,128)(2,1)S(1)}, bf16[2,96,768]{2,1,0:T(8,128)(2,1)S(1)}, u32[]{:S(2)}, u32[]{:S(2)}) collective-permute-start(bf16[2,96,768]{2,1,0:T(8,128)(2,1)S(1)} %get-tuple-element.135), channel_id=1, source_target_pairs={{0,1},{1,0},{2,3},{3,2},{4,5},{5,4},{6,7},{7,6},{8,9},{9,8},{10,11... | collective-permute-start | bytes 884744 | tf_op jit(solution)/shard_map/ppermute | solution.py:388
  102.0 9.3 %collective-permute-done.15.got = bf16[2,96,2432]{2,1,0:T(8,128)(2,1)S(1)} collective-permute-done((bf16[2,96,2432]{2,1,0:T(8,128)(2,1)S(1)}, bf16[2,96,2432]{2,1,0:T(8,128)(2,1)S(1)}, u32[]{:S(2)}, u32[]{:S(2)}) %collective-permute-start.15) | collective-permute-done | bytes 933920 | tf_op jit(solution)/shard_map/ppermute | solution.py:385
  113.4 3.9 %collective-permute-start.19 = (bf16[2,24,3840]{2,1,0:T(8,128)(2,1)S(1)}, bf16[2,24,3840]{2,1,0:T(8,128)(2,1)S(1)}, u32[]{:S(2)}, u32[]{:S(2)}) collective-permute-start(bf16[2,24,3840]{2,1,0:T(8,128)(2,1)S(1)} %get-tuple-element.138), channel_id=1, source_target_pairs={{0,1},{1,0},{2,3},{3,2},{4,5},{5,4},{6,7},{7,6},{8,9},{9,8},{10,11... | collective-permute-start | bytes 1105928 | tf_op jit(solution)/shard_map/ppermute | solution.py:388
  117.3 2.7 %collective-permute-start.21 = (bf16[96,768]{1,0:T(8,128)(2,1)S(1)}, bf16[96,768]{1,0:T(8,128)(2,1)S(1)}, u32[]{:S(2)}, u32[]{:S(2)}) collective-permute-start(bf16[96,768]{1,0:T(8,128)(2,1)S(1)} %fourth.3), channel_id=1, source_target_pairs={{0,2},{1,3},{2,0},{3,1},{4,6},{5,7},{6,4},{7,5},{8,10},{9,11},{10,... | collective-permute-start | bytes 442376 | tf_op jit(solution)/shard_map/ppermute | solution.py:388
  120.4 3.7 %collective-permute-start.20 = (bf16[2,24,2432]{2,1,0:T(8,128)(2,1)S(1)}, bf16[2,24,2432]{2,1,0:T(8,128)(2,1)S(1)}, u32[]{:S(2)}, u32[]{:S(2)}) collective-permute-start(bf16[2,24,2432]{2,1,0:T(8,128)(2,1)S(1)} %get-tuple-element.143), channel_id=1, source_target_pairs={{0,1},{1,0},{2,3},{3,2},{4,5},{5,4},{6,7},{7,6},{8,9},{9,8},{10,11... | collective-permute-start | bytes 700424 | tf_op jit(solution)/shard_map/ppermute | solution.py:388
  124.1 6.4 %collective-permute-done.19.got = bf16[2,24,3840]{2,1,0:T(8,128)(2,1)S(1)} collective-permute-done((bf16[2,24,3840]{2,1,0:T(8,128)(2,1)S(1)}, bf16[2,24,3840]{2,1,0:T(8,128)(2,1)S(1)}, u32[]{:S(2)}, u32[]{:S(2)}) %collective-permute-start.19) | collective-permute-done | bytes 368672 | tf_op jit(solution)/shard_map/ppermute | solution.py:388
  130.6 3.7 %collective-permute-done.20.got = bf16[2,24,2432]{2,1,0:T(8,128)(2,1)S(1)} collective-permute-done((bf16[2,24,2432]{2,1,0:T(8,128)(2,1)S(1)}, bf16[2,24,2432]{2,1,0:T(8,128)(2,1)S(1)}, u32[]{:S(2)}, u32[]{:S(2)}) %collective-permute-start.20) | collective-permute-done | bytes 233504 | tf_op jit(solution)/shard_map/ppermute | solution.py:388
  134.4 2.8 %collective-permute-start.25 = (bf16[24,2432]{1,0:T(8,128)(2,1)S(1)}, bf16[24,2432]{1,0:T(8,128)(2,1)S(1)}, u32[]{:S(2)}, u32[]{:S(2)}) collective-permute-start(bf16[24,2432]{1,0:T(8,128)(2,1)S(1)} %fourth.5), channel_id=1, source_target_pairs={{0,2},{1,3},{2,0},{3,1},{4,6},{5,7},{6,4},{7,5},{8,10},{9,11},{10,... | collective-permute-start | bytes 350216 | tf_op jit(solution)/shard_map/ppermute | solution.py:388
  139.0 4.2 %collective-permute-done.24.more = bf16[24,3840]{1,0:T(8,128)(2,1)S(1)} collective-permute-done((bf16[24,3840]{1,0:T(8,128)(2,1)S(1)}, bf16[24,3840]{1,0:T(8,128)(2,1)S(1)}, u32[]{:S(2)}, u32[]{:S(2)}) %collective-permute-start.24) | collective-permute-done | bytes 184352 | tf_op jit(solution)/shard_map/ppermute | solution.py:388
  (141 shorter events, 27.9 us)
Async XLA Ops:
  2.8 10.1 %collective-permute-start = (bf16[72,768]{1,0:T(8,128)(2,1)}, bf16[72,768]{1,0:T(8,128)(2,1)S(1)}, u32[]{:S(2)}, u32[]{:S(2)}) collective-permute-start(bf16[72,768]{1,0:T(8,128)(2,1)} %get-tuple-element.94), channel_id=1, source_target_pairs={{0,1},{1,2},{2,3},{3,0},{4,5},{5,6},{6,7},{7,4},{8,9},{9,10},{10,1... | collective-permute-start | bytes 331784 | tf_op jit(solution)/shard_map/ppermute | solution.py:391
  5.8 13.6 %collective-permute-start.1 = (bf16[72,768]{1,0:T(8,128)(2,1)}, bf16[72,768]{1,0:T(8,128)(2,1)S(1)}, u32[]{:S(2)}, u32[]{:S(2)}) collective-permute-start(bf16[72,768]{1,0:T(8,128)(2,1)} %get-tuple-element.95), channel_id=1, source_target_pairs={{0,2},{1,3},{2,0},{3,1},{4,6},{5,7},{6,4},{7,5},{8,10},{9,11},{10,... | collective-permute-start | bytes 331784 | tf_op jit(solution)/shard_map/ppermute | solution.py:391
  8.4 11.0 %collective-permute-start.2 = (bf16[72,768]{1,0:T(8,128)(2,1)}, bf16[72,768]{1,0:T(8,128)(2,1)S(1)}, u32[]{:S(2)}, u32[]{:S(2)}) collective-permute-start(bf16[72,768]{1,0:T(8,128)(2,1)} %get-tuple-element.96), channel_id=1, source_target_pairs={{0,3},{1,0},{2,1},{3,2},{4,7},{5,4},{6,5},{7,6},{8,11},{9,8},{10,9... | collective-permute-start | bytes 331784 | tf_op jit(solution)/shard_map/ppermute | solution.py:391
  10.4 18.8 %collective-permute-start.3 = (bf16[64,768]{1,0:T(8,128)(2,1)S(1)}, bf16[64,768]{1,0:T(8,128)(2,1)S(1)}, u32[]{:S(2)}, u32[]{:S(2)}) collective-permute-start(bf16[64,768]{1,0:T(8,128)(2,1)S(1)} %get-tuple-element.171), channel_id=1, source_target_pairs={{0,1},{1,2},{2,3},{3,0},{4,5},{5,6},{6,7},{7,4},{8,9},{9,10},{10,1... | collective-permute-start | bytes 294920 | tf_op jit(solution)/shard_map/ppermute | solution.py:391
  11.1 18.2 %collective-permute-start.4 = (bf16[64,768]{1,0:T(8,128)(2,1)S(1)}, bf16[64,768]{1,0:T(8,128)(2,1)S(1)}, u32[]{:S(2)}, u32[]{:S(2)}) collective-permute-start(bf16[64,768]{1,0:T(8,128)(2,1)S(1)} %get-tuple-element.170), channel_id=1, source_target_pairs={{0,2},{1,3},{2,0},{3,1},{4,6},{5,7},{6,4},{7,5},{8,10},{9,11},{10,... | collective-permute-start | bytes 294920 | tf_op jit(solution)/shard_map/ppermute | solution.py:391
  12.9 16.4 %collective-permute-start.5 = (bf16[64,768]{1,0:T(8,128)(2,1)S(1)}, bf16[64,768]{1,0:T(8,128)(2,1)S(1)}, u32[]{:S(2)}, u32[]{:S(2)}) collective-permute-start(bf16[64,768]{1,0:T(8,128)(2,1)S(1)} %get-tuple-element.169), channel_id=1, source_target_pairs={{0,3},{1,0},{2,1},{3,2},{4,7},{5,4},{6,5},{7,6},{8,11},{9,8},{10,9... | collective-permute-start | bytes 294920 | tf_op jit(solution)/shard_map/ppermute | solution.py:391
  29.2 12.8 %collective-permute-start.6 = (bf16[1152,256]{1,0:T(8,128)(2,1)}, bf16[1152,256]{1,0:T(8,128)(2,1)S(1)}, u32[]{:S(2)}, u32[]{:S(2)}) collective-permute-start(bf16[1152,256]{1,0:T(8,128)(2,1)} %get-tuple-element.103), channel_id=1, source_target_pairs={{0,4},{4,0},{8,12},{12,8},{16,20},{20,16},{24,28},{28,24},{1,5},{5... | collective-permute-start | bytes 1769480 | tf_op jit(solution)/shard_map/ppermute | solution.py:382
  39.8 9.6 %collective-permute-start.8 = (bf16[256,3840]{1,0:T(8,128)(2,1)}, bf16[256,3840]{1,0:T(8,128)(2,1)}, u32[]{:S(2)}, u32[]{:S(2)}) collective-permute-start(bf16[256,3840]{1,0:T(8,128)(2,1)} %get-tuple-element.102.refs_0_.refs_1_.refs_2_.refs_4_.refs_6_.refs_8_), channel_id=1, source_target_pairs={{0,4},{4,0},{8,12},{12,8},{16,20},{20,16},{24,28},{28,24},{1,5},{5... | collective-permute-start | bytes 5898248 | tf_op jit(solution)/shard_map/ppermute | solution.py:382
  40.5 8.9 %collective-permute-start.7 = (bf16[1536,256]{1,0:T(8,128)(2,1)}, bf16[1536,256]{1,0:T(8,128)(2,1)}, u32[]{:S(2)}, u32[]{:S(2)}) collective-permute-start(bf16[1536,256]{1,0:T(8,128)(2,1)} %get-tuple-element.107), channel_id=1, source_target_pairs={{0,4},{4,0},{8,12},{12,8},{16,20},{20,16},{24,28},{28,24},{1,5},{5... | collective-permute-start | bytes 2359304 | tf_op jit(solution)/shard_map/ppermute | solution.py:382
  54.9 16.3 %collective-permute-start.10 = (bf16[2,384,768]{2,1,0:T(8,128)(2,1)S(1)}, bf16[2,384,768]{2,1,0:T(8,128)(2,1)S(1)}, u32[]{:S(2)}, u32[]{:S(2)}) collective-permute-start(bf16[2,384,768]{2,1,0:T(8,128)(2,1)S(1)} %get-tuple-element.110), channel_id=1, source_target_pairs={{0,8},{4,20},{8,0},{12,28},{16,24},{20,4},{24,16},{28,12},{1,9},{5... | collective-permute-start | bytes 3538952 | tf_op jit(solution)/shard_map/ppermute | solution.py:385
  61.9 31.4 %collective-permute-start.13 = (bf16[2,96,3840]{2,1,0:T(8,128)(2,1)S(1)}, bf16[2,96,3840]{2,1,0:T(8,128)(2,1)S(1)}, u32[]{:S(2)}, u32[]{:S(2)}) collective-permute-start(bf16[2,96,3840]{2,1,0:T(8,128)(2,1)S(1)} %get-tuple-element.113), channel_id=1, source_target_pairs={{0,8},{4,20},{8,0},{12,28},{16,24},{20,4},{24,16},{28,12},{1,9},{5... | collective-permute-start | bytes 4423688 | tf_op jit(solution)/shard_map/ppermute | solution.py:385
  70.7 9.9 %collective-permute-start.11 = (bf16[256,2304]{1,0:T(8,128)(2,1)S(1)}, bf16[256,2304]{1,0:T(8,128)(2,1)S(1)}, u32[]{:S(2)}, u32[]{:S(2)}) collective-permute-start(bf16[256,2304]{1,0:T(8,128)(2,1)S(1)} %get-tuple-element.120.refs_4_.refs_2_.refs_6_), channel_id=1, source_target_pairs={{0,4},{4,0},{8,12},{12,8},{16,20},{20,16},{24,28},{28,24},{1,5},{5... | collective-permute-start | bytes 3538952 | tf_op jit(solution)/shard_map/ppermute | solution.py:382
  75.3 22.7 %collective-permute-start.14 = (bf16[384,768]{1,0:T(8,128)(2,1)S(1)}, bf16[384,768]{1,0:T(8,128)(2,1)S(1)}, u32[]{:S(2)}, u32[]{:S(2)}) collective-permute-start(bf16[384,768]{1,0:T(8,128)(2,1)S(1)} %second.3), channel_id=1, source_target_pairs={{0,16},{4,12},{8,24},{12,4},{16,0},{20,28},{24,8},{28,20},{1,17},{... | collective-permute-start | bytes 1769480 | tf_op jit(solution)/shard_map/ppermute | solution.py:385
  76.7 18.2 %collective-permute-start.22 = (bf16[256,768]{1,0:T(8,128)(2,1)S(1)}, bf16[256,768]{1,0:T(8,128)(2,1)S(1)}, u32[]{:S(2)}, u32[]{:S(2)}) collective-permute-start(bf16[256,768]{1,0:T(8,128)(2,1)S(1)} %get-tuple-element.148), channel_id=1, source_target_pairs={{0,1},{1,0},{2,3},{3,2},{4,5},{5,4},{6,7},{7,6},{8,9},{9,8},{10,11... | collective-permute-start | bytes 1179656 | tf_op jit(solution)/shard_map/ppermute | solution.py:388
  83.6 27.7 %collective-permute-start.15 = (bf16[2,96,2432]{2,1,0:T(8,128)(2,1)S(1)}, bf16[2,96,2432]{2,1,0:T(8,128)(2,1)S(1)}, u32[]{:S(2)}, u32[]{:S(2)}) collective-permute-start(bf16[2,96,2432]{2,1,0:T(8,128)(2,1)S(1)} %get-tuple-element.130), channel_id=1, source_target_pairs={{0,8},{4,20},{8,0},{12,28},{16,24},{20,4},{24,16},{28,12},{1,9},{5... | collective-permute-start | bytes 2801672 | tf_op jit(solution)/shard_map/ppermute | solution.py:385
  93.5 19.4 %collective-permute-start.16 = (bf16[96,3840]{1,0:T(8,128)(2,1)S(1)}, bf16[96,3840]{1,0:T(8,128)(2,1)S(1)}, u32[]{:S(2)}, u32[]{:S(2)}) collective-permute-start(bf16[96,3840]{1,0:T(8,128)(2,1)S(1)} %second.4), channel_id=1, source_target_pairs={{0,16},{4,12},{8,24},{12,4},{16,0},{20,28},{24,8},{28,20},{1,17},{... | collective-permute-start | bytes 2211848 | tf_op jit(solution)/shard_map/ppermute | solution.py:385
  95.0 42.9 %collective-permute-start.23 = (bf16[256,768]{1,0:T(8,128)(2,1)S(1)}, bf16[256,768]{1,0:T(8,128)(2,1)S(1)}, u32[]{:S(2)}, u32[]{:S(2)}) collective-permute-start(bf16[256,768]{1,0:T(8,128)(2,1)S(1)} %pad_maximum_fusion), channel_id=1, source_target_pairs={{0,2},{1,3},{2,0},{3,1},{4,6},{5,7},{6,4},{7,5},{8,10},{9,11},{10,... | collective-permute-start | bytes 1179656 | tf_op jit(solution)/shard_map/ppermute | solution.py:388
  98.4 18.9 %collective-permute-start.17 = (bf16[2,96,768]{2,1,0:T(8,128)(2,1)S(1)}, bf16[2,96,768]{2,1,0:T(8,128)(2,1)S(1)}, u32[]{:S(2)}, u32[]{:S(2)}) collective-permute-start(bf16[2,96,768]{2,1,0:T(8,128)(2,1)S(1)} %get-tuple-element.135), channel_id=1, source_target_pairs={{0,1},{1,0},{2,3},{3,2},{4,5},{5,4},{6,7},{7,6},{8,9},{9,8},{10,11... | collective-permute-start | bytes 884744 | tf_op jit(solution)/shard_map/ppermute | solution.py:388
  111.4 8.7 %collective-permute-start.18 = (bf16[96,2432]{1,0:T(8,128)(2,1)S(1)}, bf16[96,2432]{1,0:T(8,128)(2,1)S(1)}, u32[]{:S(2)}, u32[]{:S(2)}) collective-permute-start(bf16[96,2432]{1,0:T(8,128)(2,1)S(1)} %second.5), channel_id=1, source_target_pairs={{0,16},{4,12},{8,24},{12,4},{16,0},{20,28},{24,8},{28,20},{1,17},{... | collective-permute-start | bytes 1400840 | tf_op jit(solution)/shard_map/ppermute | solution.py:385
  113.4 17.1 %collective-permute-start.19 = (bf16[2,24,3840]{2,1,0:T(8,128)(2,1)S(1)}, bf16[2,24,3840]{2,1,0:T(8,128)(2,1)S(1)}, u32[]{:S(2)}, u32[]{:S(2)}) collective-permute-start(bf16[2,24,3840]{2,1,0:T(8,128)(2,1)S(1)} %get-tuple-element.138), channel_id=1, source_target_pairs={{0,1},{1,0},{2,3},{3,2},{4,5},{5,4},{6,7},{7,6},{8,9},{9,8},{10,11... | collective-permute-start | bytes 1105928 | tf_op jit(solution)/shard_map/ppermute | solution.py:388
  117.3 19.8 %collective-permute-start.21 = (bf16[96,768]{1,0:T(8,128)(2,1)S(1)}, bf16[96,768]{1,0:T(8,128)(2,1)S(1)}, u32[]{:S(2)}, u32[]{:S(2)}) collective-permute-start(bf16[96,768]{1,0:T(8,128)(2,1)S(1)} %fourth.3), channel_id=1, source_target_pairs={{0,2},{1,3},{2,0},{3,1},{4,6},{5,7},{6,4},{7,5},{8,10},{9,11},{10,... | collective-permute-start | bytes 442376 | tf_op jit(solution)/shard_map/ppermute | solution.py:388
  120.4 14.0 %collective-permute-start.20 = (bf16[2,24,2432]{2,1,0:T(8,128)(2,1)S(1)}, bf16[2,24,2432]{2,1,0:T(8,128)(2,1)S(1)}, u32[]{:S(2)}, u32[]{:S(2)}) collective-permute-start(bf16[2,24,2432]{2,1,0:T(8,128)(2,1)S(1)} %get-tuple-element.143), channel_id=1, source_target_pairs={{0,1},{1,0},{2,3},{3,2},{4,5},{5,4},{6,7},{7,6},{8,9},{9,8},{10,11... | collective-permute-start | bytes 700424 | tf_op jit(solution)/shard_map/ppermute | solution.py:388
  130.6 12.7 %collective-permute-start.24 = (bf16[24,3840]{1,0:T(8,128)(2,1)S(1)}, bf16[24,3840]{1,0:T(8,128)(2,1)S(1)}, u32[]{:S(2)}, u32[]{:S(2)}) collective-permute-start(bf16[24,3840]{1,0:T(8,128)(2,1)S(1)} %fourth.4), channel_id=1, source_target_pairs={{0,2},{1,3},{2,0},{3,1},{4,6},{5,7},{6,4},{7,5},{8,10},{9,11},{10,... | collective-permute-start | bytes 552968 | tf_op jit(solution)/shard_map/ppermute | solution.py:388
  134.4 10.1 %collective-permute-start.25 = (bf16[24,2432]{1,0:T(8,128)(2,1)S(1)}, bf16[24,2432]{1,0:T(8,128)(2,1)S(1)}, u32[]{:S(2)}, u32[]{:S(2)}) collective-permute-start(bf16[24,2432]{1,0:T(8,128)(2,1)S(1)} %fourth.5), channel_id=1, source_target_pairs={{0,2},{1,3},{2,0},{3,1},{4,6},{5,7},{6,4},{7,5},{8,10},{9,11},{10,... | collective-permute-start | bytes 350216 | tf_op jit(solution)/shard_map/ppermute | solution.py:388
  (38 other events, 204.4 us)

commit v3 on v2

--- a/solution.py
+++ b/solution.py
@@ -240,10 +240,16 @@
     sums[2:8, :] = jnp.zeros((6, width), F32)
 
 
+def by_band(rows, nb, band, x, own, near, far):
+    for bits, out, at in ((0, own, 0), (1, near, 0), (3, near, rows), (2, far, 0)):
+        slot = lax.rem(band[0] - jnp.bitwise_xor(band[0], bits) + nb, nb)
+        out[at : at + rows, :] = x[pl.ds(pl.multiple_of(slot * rows, 16), rows), :]
+
+
 def input_back_kernel(rows, nb, block, core, band, *refs):
     slots = refs[:nb]
     right, wq, wk, wv, gm, vec, down_sums, attend_sums, up_cols = refs[nb : nb + 9]
-    result, own_o, near_o, far_o, keep_o, send_o, held = refs[nb + 9 :]
+    own_o, near_o, far_o, keep_o, send_o, held = refs[nb + 9 :]
     width = gm.shape[1]
     grad = dot_nt(right[:, :width], wq[...])
     grad = grad + dot_nt(right[:, width : 2 * width], wk[...])
@@ -251,11 +257,7 @@
     n1, r1 = norm_stats(join(slots, rows).astype(F32))
     gx = (gm[...] + norm_back(grad, n1, r1, vec[GAIN1 : GAIN1 + 1, :])).astype(BF16)
     held[...] = gx
-    for bits, out, at in ((0, own_o, 0), (1, near_o, 0), (3, near_o, 2 * rows), (2, far_o, 0)):
-        slot = lax.rem(band[0] - jnp.bitwise_xor(band[0], bits) + nb, nb)
-        tokens = pl.ds(pl.multiple_of(slot * rows, 16), rows)
-        out[at : at + rows, :] = result[tokens, :]
-        out[at + rows : at + 2 * rows, :] = held[tokens, :]
+    by_band(rows, nb, band, held, own_o, near_o, far_o)
     table = jnp.concatenate(
         [
             down_sums[...], attend_sums[...], colsum(grad * n1), colsum(grad),
@@ -283,12 +285,12 @@
         outs[s][rows:, :] = jnp.where((slot == s) & (lane == s), flags, 0.0).astype(BF16)
 
 
-def gather_kernel(band, own, near, far, output, grad):
+def gather_kernel(band, *refs):
+    output, grad = refs[6:]
     rows = output.shape[1]
-    for bits, ref, at in ((0, own, 0), (1, near, 0), (2, far, 0), (3, far, 2 * rows)):
-        image = jnp.bitwise_xor(band[0], bits)
-        output[image] = ref[at : at + rows, :]
-        grad[image] = ref[at + rows : at + 2 * rows, :].astype(F32)
+    for out, (own, near, far) in ((output, refs[:3]), (grad, refs[3:6])):
+        for bits, ref, at in ((0, own, 0), (1, near, 0), (2, far, 0), (3, far, rows)):
+            out[jnp.bitwise_xor(band[0], bits)] = ref[at : at + rows, :].astype(out.dtype)
 
 
 def weight_kernel(groups, extra, quarters, *refs):
@@ -664,15 +666,25 @@
     )(after(grad_branch, unit_up.send), q, k, v, mask, w_out)
     back_got = links.flip(back_right, 1)
 
+    results = pl.pallas_call(
+        functools.partial(by_band, rows, nb),
+        in_specs=[SM, VM],
+        out_specs=[VM] * 3,
+        out_shape=[shape(rows, width), shape(2 * rows, width), shape(rows, width)],
+        cost_estimate=cost(1),
+        compiler_params=LIMIT,
+        name="by_band",
+    )(band, after(result, unit_up.send))
+    result_near = links.flip_band(results[1], 1)
     mark = unit_down.second(back_right)
     per_row = hidden_width // width
     up_cols = up_sums[0].reshape(n_img * nb, per_row, -1).swapaxes(1, 2).reshape(width, per_row)
     up_cols = jnp.pad(up_cols, ((0, 0), (18, COLS - 18 - per_row)))
     back = pl.pallas_call(
         functools.partial(input_back_kernel, rows, nb, block if aligned else half),
-        in_specs=[SM] * 2 + [VM] * (nb + 10),
+        in_specs=[SM] * 2 + [VM] * (nb + 9),
         out_specs=[VM] * 5,
-        out_shape=[shape(2 * rows, width), shape(4 * rows, width), shape(2 * rows, width)]
+        out_shape=[shape(rows, width), shape(2 * rows, width), shape(rows, width)]
         + [shape(half, COLS, dtype=F32)] * 2,
         scratch_shapes=[pltpu.VMEM((tokens, width), BF16)],
         cost_estimate=cost(5),
@@ -681,7 +693,6 @@
     )(
         core if aligned else jnp.zeros_like(core), band,
         *slots, after(back_right, mark), w_query, w_key, w_value, grad_middle, vec, down_sums, attend_sums, up_cols,
-        result,
     )
     blocks, table = back[:3], back[3:]
     near_got = links.flip_band(blocks[1], 1)
@@ -694,7 +705,8 @@
         [(after(left_keep, blocks[0]), left_got, 0, [(width, back_right, i, back_got, i) for i in range(3)])],
         (table[0], table_got),
     )
-    far_got = links.flip_band(jnp.concatenate([after(blocks[2], unit_qkv.send), near_got[2 * rows :, :]]), 2)
+    result_far = links.flip_band(jnp.concatenate([after(results[2], blocks[0]), result_near[rows:, :]]), 2)
+    far_got = links.flip_band(jnp.concatenate([after(blocks[2], unit_qkv.send), near_got[rows:, :]]), 2)
     mark = unit_up.second(unit_qkv.send)
     mark = unit_down.third(mark)
     mark = unit_qkv.second(mark)
@@ -706,13 +718,13 @@
     (g_w_down,) = unit_down.last(mark)
     output, grad_inputs = pl.pallas_call(
         gather_kernel,
-        in_specs=[SM] + [VM] * 3,
+        in_specs=[SM] + [VM] * 6,
         out_specs=[VM] * 2,
         out_shape=[shape(nb, rows, width), shape(nb, rows, width, dtype=F32)],
         cost_estimate=cost(2),
         compiler_params=LIMIT,
         name="gather",
-    )(after(band, g_w_down), blocks[0], near_got, far_got)
+    )(after(band, g_w_down), results[0], result_near, result_far, blocks[0], near_got, far_got)
     mark = output
     unit_up.widths = [hidden_width, width]
     g_w_up, g_w_out = unit_up.last(mark)

time: 146 us -> 144 us (0.986)
  waiting for transfers between devices: 36.3 us -> 30.5 us
  starting transfers between devices: 44.2 us -> 49.7 us
  local copies, waits for them, and re-layouts: 6.79 us -> 4.97 us
    ppermute x8 -> x10, starting transfers between devices: 23.6 us -> 29.4 us  [flip_band(): return lax.ppermute(x, 'band', [(k, k ^ bit) for k in range(self.nb)])]
    ppermute x8 -> x10, waiting for transfers between devices: 14.8 us -> 11 us  [flip_band(): return lax.ppermute(x, 'band', [(k, k ^ bit) for k in range(self.nb)])]
    ppermute x6, waiting for transfers between devices: 17.8 us -> 15.7 us  [flip_by_core(): lax.ppermute(x, 'img', [(k, k ^ (odd if k & 1 else even)) for k in range(...]
    unnamed x72, local copies, waits for them, and re-layouts: 4.56 us -> 2.73 us
  transfers between devices with their start and end apart: 26 -> 28, of which waited for: 8 -> 9; matrix products, arithmetic and copies ran while one was open for 2% -> 2% of each run, Pallas kernels for 36% -> 37%
where the time goes in v3:
time: 144 us; the launch traced here: 143 us
  Pallas kernels  55.4 us (38%)
  starting transfers between devices  49.7 us (35%)
  waiting for transfers between devices  30.5 us (21%)
  local copies, waits for them, and re-layouts  4.97 us (3%)
  between operations  1.5 us (1%)
    ppermute x10, starting transfers between devices, flip_band(): return lax.ppermute(x, 'band', [(k, k ^ bit) for k in range(self.nb)])  29.4 us
    ppermute x6, waiting for transfers between devices, flip_by_core(): lax.ppermute(x, 'img', [(k, k ^ (odd if k & 1 else even)) for k in range(...  15.7 us
    pallas_call x3, Pallas kernels, __init__(): pl.pallas_call(functools.partial(weight_kernel, widths, self.extra), grid...  12.8 us
    ppermute x10, waiting for transfers between devices, flip_band(): return lax.ppermute(x, 'band', [(k, k ^ bit) for k in range(self.nb)])  11 us
    ppermute x6, starting transfers between devices, band_shift(): lax.ppermute(x, 'band', [(k, (k + s) % self.nb) for k in range(self.nb)])  10.8 us
    pallas_call x1, Pallas kernels, per_device(): pl.pallas_call(functools.partial(up_kernel, rows, nb, steps, up_block), g...  9.86 us
    pallas_call x1, Pallas kernels, per_device(): pl.pallas_call(functools.partial(attend_kernel, rows, nb, block if aligne...  9.09 us
    pallas_call x1, Pallas kernels, per_device(): pl.pallas_call(attend_back_kernel, in_specs=[VM] * 6, out_specs=[VM] * 2,...  8.05 us
  transfers between devices with their start and end apart: 28, of which 9 were waited for; matrix products, arithmetic and copies ran while one was open for 2% of the time, Pallas kernels for 37%

profile of v3, /device:TPU:0, one launch (start us, length us, event | category | flops | bytes accessed | tf_op | source)
XLA Modules:
  0.0 143.4 jit_solution(9953516537649457938)
XLA Ops:
  2.8 3.1 %collective-permute-start = (bf16[72,768]{1,0:T(8,128)(2,1)}, bf16[72,768]{1,0:T(8,128)(2,1)S(1)}, u32[]{:S(2)}, u32[]{:S(2)}) collective-permute-start(bf16[72,768]{1,0:T(8,128)(2,1)} %get-tuple-element.99), channel_id=1, source_target_pairs={{0,1},{1,2},{2,3},{3,0},{4,5},{5,6},{6,7},{7,4},{8,9},{9,10},{10,1... | collective-permute-start | bytes 331784 | tf_op jit(solution)/shard_map/ppermute | solution.py:393
  5.8 2.6 %collective-permute-start.1 = (bf16[72,768]{1,0:T(8,128)(2,1)}, bf16[72,768]{1,0:T(8,128)(2,1)S(1)}, u32[]{:S(2)}, u32[]{:S(2)}) collective-permute-start(bf16[72,768]{1,0:T(8,128)(2,1)} %get-tuple-element.100), channel_id=1, source_target_pairs={{0,2},{1,3},{2,0},{3,1},{4,6},{5,7},{6,4},{7,5},{8,10},{9,11},{10,... | collective-permute-start | bytes 331784 | tf_op jit(solution)/shard_map/ppermute | solution.py:393
  12.9 2.8 %collective-permute-start.5 = (bf16[64,768]{1,0:T(8,128)(2,1)S(1)}, bf16[64,768]{1,0:T(8,128)(2,1)S(1)}, u32[]{:S(2)}, u32[]{:S(2)}) collective-permute-start(bf16[64,768]{1,0:T(8,128)(2,1)S(1)} %get-tuple-element.179), channel_id=1, source_target_pairs={{0,3},{1,0},{2,1},{3,2},{4,7},{5,4},{6,5},{7,6},{8,11},{9,8},{10,9... | collective-permute-start | bytes 294920 | tf_op jit(solution)/shard_map/ppermute | solution.py:393
  15.7 3.7 %collective-permute-done.1.refs_2_ = bf16[72,768]{1,0:T(8,128)(2,1)S(1)} collective-permute-done((bf16[72,768]{1,0:T(8,128)(2,1)}, bf16[72,768]{1,0:T(8,128)(2,1)S(1)}, u32[]{:S(2)}, u32[]{:S(2)}) %collective-permute-start.1) | collective-permute-done | bytes 110624 | tf_op jit(solution)/shard_map/ppermute | solution.py:393
  20.1 9.1 %attend.1 = (bf16[1152,256]{1,0:T(8,128)(2,1)}, bf16[1152,256]{1,0:T(8,128)(2,1)}, bf16[256,768]{1,0:T(8,128)(2,1)}, bf16[256,768]{1,0:T(8,128)(2,1)}, bf16[256,...) custom-call(s32[1]{0:T(128)} %bitcast.5.core, ...), custom_call_target="tpu_custom_call" | custom-call | flops 22499999744 | bytes 90000000 | tf_op jit(solution)/shard_map/attend/pallas_call | solution.py:581
  30.0 9.9 %up.1 = (bf16[1536,256]{1,0:T(8,128)(2,1)}, bf16[1536,256]{1,0:T(8,128)(2,1)}, bf16[256,3840]{1,0:T(8,128)(2,1)}, f32[8,3072]{1,0:T(8,128)}, bf16[256,768]{1,0:T(8,128)(2,1)}) custom-call(s32[1]{0:T(128)} %bitcast.5.core, bf16[256,768]{1,0:T(8,128)(2,1)} %get-tuple-element.102.refs_0_, f32[256,768]{1,0:T(8,128)} %get-tuple-element.109.refs_1_.refs_3_, ...), custom_call_target="tpu_custom_call" | custom-call | flops 24999999488 | bytes 100000000 | tf_op jit(solution)/shard_map/up/pallas_call | solution.py:601
  42.0 6.9 %down.1 = (f32[256,768]{1,0:T(8,128)}, bf16[256,768]{1,0:T(8,128)(2,1)}, f32[8,768]{1,0:T(8,128)}) custom-call(bf16[256,3840]{1,0:T(8,128)(2,1)} %get-tuple-element.107.refs_0_.refs_1_.refs_2_.refs_4_.refs_6_.refs_8_, bf16[256,3840]{1,0:T(8,128)(2,1)} %get-tuple-element.107.refs_0_.refs_1_.refs_2_.refs_4_.refs_6_.refs_8_, bf16[768,3072]{1,0:T(8,128)(2,1)} %refs_2_.1, ...), custom_call_target="tpu_custom_call" | custom-call | flops 17500000256 | bytes 70000000 | tf_op jit(solution)/shard_map/down/pallas_call | solution.py:624
  50.7 4.3 %weight_grad.3 = (bf16[2,384,768]{2,1,0:T(8,128)(2,1)S(1)}, bf16[2,384,768]{2,1,0:T(8,128)(2,1)S(1)}) custom-call(s32[4]{0:T(128)S(1)} %pad_add_fusion.quarters, bf16[1536,256]{1,0:T(8,128)(2,1)S(1)} %copy-done.17, bf16[1536,256]{1,0:T(8,128)(2,1)} %collective-permute-done.7.refs_1_, bf16[256,3840]{1,0:T(8,128)(2,1)S(1)} %copy-done.2, ...), custom_call_target="tpu_custom_call" | custom-call | flops 15000000512 | bytes 60000000 | tf_op jit(solution)/shard_map/weight_grad/pallas_call | solution.py:451
  56.4 5.4 %weight_grad.4 = (bf16[2,96,3840]{2,1,0:T(8,128)(2,1)S(1)}, bf16[2,96,3840]{2,1,0:T(8,128)(2,1)S(1)}) custom-call(s32[4]{0:T(128)S(1)} %pad_add_fusion.quarters, bf16[1152,256]{1,0:T(8,128)(2,1)S(1)} %copy-done, bf16[1152,256]{1,0:T(8,128)(2,1)S(1)} %collective-permute-done.6.refs_1_.refs_11_, bf16[256,3840]{1,0:T(8,128)(2,1)S(1)} %copy-done.2, ...), custom_call_target="tpu_custom_call" | custom-call | flops 15000000512 | bytes 60000000 | tf_op jit(solution)/shard_map/weight_grad/pallas_call | solution.py:451
  62.6 8.0 %attend_back.1 = (bf16[256,2304]{1,0:T(8,128)(2,1)S(1)}, f32[8,768]{1,0:T(8,128)S(1)}) custom-call(bf16[256,768]{1,0:T(8,128)(2,1)S(1)} %copy-done.7, bf16[256,768]{1,0:T(8,128)(2,1)S(1)} %copy-done.18, bf16[256,768]{1,0:T(8,128)(2,1)S(1)} %copy-done.19, bf16[256,768]{1,0:T(8,128)(2,1)S(1)} %copy-done.20, f32[8,256]{1,0:T(8,128)S(1)} %copy-done.22, ...), custom_call_target="tpu_custom_call" | custom-call | flops 27499999232 | bytes 110000000 | tf_op jit(solution)/shard_map/attend_back/pallas_call | solution.py:654
  70.9 3.7 %collective-permute-start.22 = (bf16[128,768]{1,0:T(8,128)(2,1)S(1)}, bf16[128,768]{1,0:T(8,128)(2,1)S(1)}, u32[]{:S(2)}, u32[]{:S(2)}) collective-permute-start(bf16[128,768]{1,0:T(8,128)(2,1)S(1)} %get-tuple-element.155), channel_id=1, source_target_pairs={{0,1},{1,0},{2,3},{3,2},{4,5},{5,4},{6,7},{7,6},{8,9},{9,8},{10,11... | collective-permute-start | bytes 589832 | tf_op jit(solution)/shard_map/ppermute | solution.py:390
  76.7 2.2 %collective-permute-start.24 = (bf16[128,768]{1,0:T(8,128)(2,1)S(1)}, bf16[128,768]{1,0:T(8,128)(2,1)S(1)}, u32[]{:S(2)}, u32[]{:S(2)}) collective-permute-start(bf16[128,768]{1,0:T(8,128)(2,1)S(1)} %get-tuple-element.158), channel_id=1, source_target_pairs={{0,1},{1,0},{2,3},{3,2},{4,5},{5,4},{6,7},{7,6},{8,9},{9,8},{10,11... | collective-permute-start | bytes 589832 | tf_op jit(solution)/shard_map/ppermute | solution.py:390
  82.1 2.8 %collective-permute-start.23 = (bf16[128,768]{1,0:T(8,128)(2,1)S(1)}, bf16[128,768]{1,0:T(8,128)(2,1)S(1)}, u32[]{:S(2)}, u32[]{:S(2)}) collective-permute-start(bf16[128,768]{1,0:T(8,128)(2,1)S(1)} %pad_maximum_fusion), channel_id=1, source_target_pairs={{0,2},{1,3},{2,0},{3,1},{4,6},{5,7},{6,4},{7,5},{8,10},{9,11},{10,... | collective-permute-start | bytes 589832 | tf_op jit(solution)/shard_map/ppermute | solution.py:390
  84.8 3.0 %weight_grad.5 = (bf16[2,96,2432]{2,1,0:T(8,128)(2,1)S(1)}, bf16[2,96,2432]{2,1,0:T(8,128)(2,1)S(1)}) custom-call(s32[4]{0:T(128)S(1)} %pad_add_fusion.quarters, bf16[1152,256]{1,0:T(8,128)(2,1)S(1)} %copy-done, bf16[1152,256]{1,0:T(8,128)(2,1)S(1)} %collective-permute-done.6.refs_1_.refs_11_, ...), custom_call_target="tpu_custom_call" | custom-call | flops 250000000 | bytes 1000000 | tf_op jit(solution)/shard_map/weight_grad/pallas_call | solution.py:451
  92.7 2.4 %collective-permute-done.14.more = bf16[384,768]{1,0:T(8,128)(2,1)S(1)} collective-permute-done((bf16[384,768]{1,0:T(8,128)(2,1)S(1)}, bf16[384,768]{1,0:T(8,128)(2,1)S(1)}, u32[]{:S(2)}, u32[]{:S(2)}) %collective-permute-start.14) | collective-permute-done | bytes 589856 | tf_op jit(solution)/shard_map/ppermute | solution.py:387
  95.6 3.8 %collective-permute-start.17 = (bf16[2,96,768]{2,1,0:T(8,128)(2,1)S(1)}, bf16[2,96,768]{2,1,0:T(8,128)(2,1)S(1)}, u32[]{:S(2)}, u32[]{:S(2)}) collective-permute-start(bf16[2,96,768]{2,1,0:T(8,128)(2,1)S(1)} %get-tuple-element.139), channel_id=1, source_target_pairs={{0,1},{1,0},{2,3},{3,2},{4,5},{5,4},{6,7},{7,6},{8,9},{9,8},{10,11... | collective-permute-start | bytes 884744 | tf_op jit(solution)/shard_map/ppermute | solution.py:390
  99.4 11.9 %collective-permute-done.15.got = bf16[2,96,2432]{2,1,0:T(8,128)(2,1)S(1)} collective-permute-done((bf16[2,96,2432]{2,1,0:T(8,128)(2,1)S(1)}, bf16[2,96,2432]{2,1,0:T(8,128)(2,1)S(1)}, u32[]{:S(2)}, u32[]{:S(2)}) %collective-permute-start.15) | collective-permute-done | bytes 933920 | tf_op jit(solution)/shard_map/ppermute | solution.py:387
  113.2 4.7 %collective-permute-start.19 = (bf16[2,24,3840]{2,1,0:T(8,128)(2,1)S(1)}, bf16[2,24,3840]{2,1,0:T(8,128)(2,1)S(1)}, u32[]{:S(2)}, u32[]{:S(2)}) collective-permute-start(bf16[2,24,3840]{2,1,0:T(8,128)(2,1)S(1)} %get-tuple-element.142), channel_id=1, source_target_pairs={{0,1},{1,0},{2,3},{3,2},{4,5},{5,4},{6,7},{7,6},{8,9},{9,8},{10,11... | collective-permute-start | bytes 1105928 | tf_op jit(solution)/shard_map/ppermute | solution.py:390
  118.0 2.8 %collective-permute-start.21 = (bf16[96,768]{1,0:T(8,128)(2,1)S(1)}, bf16[96,768]{1,0:T(8,128)(2,1)S(1)}, u32[]{:S(2)}, u32[]{:S(2)}) collective-permute-start(bf16[96,768]{1,0:T(8,128)(2,1)S(1)} %fourth.3), channel_id=1, source_target_pairs={{0,2},{1,3},{2,0},{3,1},{4,6},{5,7},{6,4},{7,5},{8,10},{9,11},{10,... | collective-permute-start | bytes 442376 | tf_op jit(solution)/shard_map/ppermute | solution.py:390
  121.1 3.7 %collective-permute-start.20 = (bf16[2,24,2432]{2,1,0:T(8,128)(2,1)S(1)}, bf16[2,24,2432]{2,1,0:T(8,128)(2,1)S(1)}, u32[]{:S(2)}, u32[]{:S(2)}) collective-permute-start(bf16[2,24,2432]{2,1,0:T(8,128)(2,1)S(1)} %get-tuple-element.147), channel_id=1, source_target_pairs={{0,1},{1,0},{2,3},{3,2},{4,5},{5,4},{6,7},{7,6},{8,9},{9,8},{10,11... | collective-permute-start | bytes 700424 | tf_op jit(solution)/shard_map/ppermute | solution.py:390
  124.8 5.0 %collective-permute-done.19.got = bf16[2,24,3840]{2,1,0:T(8,128)(2,1)S(1)} collective-permute-done((bf16[2,24,3840]{2,1,0:T(8,128)(2,1)S(1)}, bf16[2,24,3840]{2,1,0:T(8,128)(2,1)S(1)}, u32[]{:S(2)}, u32[]{:S(2)}) %collective-permute-start.19) | collective-permute-done | bytes 368672 | tf_op jit(solution)/shard_map/ppermute | solution.py:390
  129.8 2.1 %collective-permute-start.26 = (bf16[24,3840]{1,0:T(8,128)(2,1)S(1)}, bf16[24,3840]{1,0:T(8,128)(2,1)S(1)}, u32[]{:S(2)}, u32[]{:S(2)}) collective-permute-start(bf16[24,3840]{1,0:T(8,128)(2,1)S(1)} %fourth.4), channel_id=1, source_target_pairs={{0,2},{1,3},{2,0},{3,1},{4,6},{5,7},{6,4},{7,5},{8,10},{9,11},{10,... | collective-permute-start | bytes 552968 | tf_op jit(solution)/shard_map/ppermute | solution.py:390
  132.3 3.4 %collective-permute-start.27 = (bf16[24,2432]{1,0:T(8,128)(2,1)S(1)}, bf16[24,2432]{1,0:T(8,128)(2,1)S(1)}, u32[]{:S(2)}, u32[]{:S(2)}) collective-permute-start(bf16[24,2432]{1,0:T(8,128)(2,1)S(1)} %fourth.5), channel_id=1, source_target_pairs={{0,2},{1,3},{2,0},{3,1},{4,6},{5,7},{6,4},{7,5},{8,10},{9,11},{10,... | collective-permute-start | bytes 350216 | tf_op jit(solution)/shard_map/ppermute | solution.py:390
  137.5 3.7 %collective-permute-done.26.more = bf16[24,3840]{1,0:T(8,128)(2,1)S(1)} collective-permute-done((bf16[24,3840]{1,0:T(8,128)(2,1)S(1)}, bf16[24,3840]{1,0:T(8,128)(2,1)S(1)}, u32[]{:S(2)}, u32[]{:S(2)}) %collective-permute-start.26) | collective-permute-done | bytes 184352 | tf_op jit(solution)/shard_map/ppermute | solution.py:390
  (148 shorter events, 31.1 us)
Async XLA Ops:
  2.8 10.1 %collective-permute-start = (bf16[72,768]{1,0:T(8,128)(2,1)}, bf16[72,768]{1,0:T(8,128)(2,1)S(1)}, u32[]{:S(2)}, u32[]{:S(2)}) collective-permute-start(bf16[72,768]{1,0:T(8,128)(2,1)} %get-tuple-element.99), channel_id=1, source_target_pairs={{0,1},{1,2},{2,3},{3,0},{4,5},{5,6},{6,7},{7,4},{8,9},{9,10},{10,1... | collective-permute-start | bytes 331784 | tf_op jit(solution)/shard_map/ppermute | solution.py:393
  5.8 13.6 %collective-permute-start.1 = (bf16[72,768]{1,0:T(8,128)(2,1)}, bf16[72,768]{1,0:T(8,128)(2,1)S(1)}, u32[]{:S(2)}, u32[]{:S(2)}) collective-permute-start(bf16[72,768]{1,0:T(8,128)(2,1)} %get-tuple-element.100), channel_id=1, source_target_pairs={{0,2},{1,3},{2,0},{3,1},{4,6},{5,7},{6,4},{7,5},{8,10},{9,11},{10,... | collective-permute-start | bytes 331784 | tf_op jit(solution)/shard_map/ppermute | solution.py:393
  8.4 11.0 %collective-permute-start.2 = (bf16[72,768]{1,0:T(8,128)(2,1)}, bf16[72,768]{1,0:T(8,128)(2,1)S(1)}, u32[]{:S(2)}, u32[]{:S(2)}) collective-permute-start(bf16[72,768]{1,0:T(8,128)(2,1)} %get-tuple-element.101), channel_id=1, source_target_pairs={{0,3},{1,0},{2,1},{3,2},{4,7},{5,4},{6,5},{7,6},{8,11},{9,8},{10,9... | collective-permute-start | bytes 331784 | tf_op jit(solution)/shard_map/ppermute | solution.py:393
  10.4 18.8 %collective-permute-start.3 = (bf16[64,768]{1,0:T(8,128)(2,1)S(1)}, bf16[64,768]{1,0:T(8,128)(2,1)S(1)}, u32[]{:S(2)}, u32[]{:S(2)}) collective-permute-start(bf16[64,768]{1,0:T(8,128)(2,1)S(1)} %get-tuple-element.181), channel_id=1, source_target_pairs={{0,1},{1,2},{2,3},{3,0},{4,5},{5,6},{6,7},{7,4},{8,9},{9,10},{10,1... | collective-permute-start | bytes 294920 | tf_op jit(solution)/shard_map/ppermute | solution.py:393
  11.1 18.2 %collective-permute-start.4 = (bf16[64,768]{1,0:T(8,128)(2,1)S(1)}, bf16[64,768]{1,0:T(8,128)(2,1)S(1)}, u32[]{:S(2)}, u32[]{:S(2)}) collective-permute-start(bf16[64,768]{1,0:T(8,128)(2,1)S(1)} %get-tuple-element.180), channel_id=1, source_target_pairs={{0,2},{1,3},{2,0},{3,1},{4,6},{5,7},{6,4},{7,5},{8,10},{9,11},{10,... | collective-permute-start | bytes 294920 | tf_op jit(solution)/shard_map/ppermute | solution.py:393
  12.9 16.4 %collective-permute-start.5 = (bf16[64,768]{1,0:T(8,128)(2,1)S(1)}, bf16[64,768]{1,0:T(8,128)(2,1)S(1)}, u32[]{:S(2)}, u32[]{:S(2)}) collective-permute-start(bf16[64,768]{1,0:T(8,128)(2,1)S(1)} %get-tuple-element.179), channel_id=1, source_target_pairs={{0,3},{1,0},{2,1},{3,2},{4,7},{5,4},{6,5},{7,6},{8,11},{9,8},{10,9... | collective-permute-start | bytes 294920 | tf_op jit(solution)/shard_map/ppermute | solution.py:393
  29.2 12.8 %collective-permute-start.6 = (bf16[1152,256]{1,0:T(8,128)(2,1)}, bf16[1152,256]{1,0:T(8,128)(2,1)S(1)}, u32[]{:S(2)}, u32[]{:S(2)}) collective-permute-start(bf16[1152,256]{1,0:T(8,128)(2,1)} %get-tuple-element.108), channel_id=1, source_target_pairs={{0,4},{4,0},{8,12},{12,8},{16,20},{20,16},{24,28},{28,24},{1,5},{5... | collective-permute-start | bytes 1769480 | tf_op jit(solution)/shard_map/ppermute | solution.py:384
  39.8 9.6 %collective-permute-start.8 = (bf16[256,3840]{1,0:T(8,128)(2,1)}, bf16[256,3840]{1,0:T(8,128)(2,1)}, u32[]{:S(2)}, u32[]{:S(2)}) collective-permute-start(bf16[256,3840]{1,0:T(8,128)(2,1)} %get-tuple-element.107.refs_0_.refs_1_.refs_2_.refs_4_.refs_6_.refs_8_), channel_id=1, source_target_pairs={{0,4},{4,0},{8,12},{12,8},{16,20},{20,16},{24,28},{28,24},{1,5},{5... | collective-permute-start | bytes 5898248 | tf_op jit(solution)/shard_map/ppermute | solution.py:384
  54.9 19.7 %collective-permute-start.10 = (bf16[2,384,768]{2,1,0:T(8,128)(2,1)S(1)}, bf16[2,384,768]{2,1,0:T(8,128)(2,1)S(1)}, u32[]{:S(2)}, u32[]{:S(2)}) collective-permute-start(bf16[2,384,768]{2,1,0:T(8,128)(2,1)S(1)} %get-tuple-element.115), channel_id=1, source_target_pairs={{0,8},{4,20},{8,0},{12,28},{16,24},{20,4},{24,16},{28,12},{1,9},{5... | collective-permute-start | bytes 3538952 | tf_op jit(solution)/shard_map/ppermute | solution.py:387
  61.9 29.3 %collective-permute-start.13 = (bf16[2,96,3840]{2,1,0:T(8,128)(2,1)S(1)}, bf16[2,96,3840]{2,1,0:T(8,128)(2,1)S(1)}, u32[]{:S(2)}, u32[]{:S(2)}) collective-permute-start(bf16[2,96,3840]{2,1,0:T(8,128)(2,1)S(1)} %get-tuple-element.118), channel_id=1, source_target_pairs={{0,8},{4,20},{8,0},{12,28},{16,24},{20,4},{24,16},{28,12},{1,9},{5... | collective-permute-start | bytes 4423688 | tf_op jit(solution)/shard_map/ppermute | solution.py:387
  70.7 11.4 %collective-permute-start.11 = (bf16[256,2304]{1,0:T(8,128)(2,1)S(1)}, bf16[256,2304]{1,0:T(8,128)(2,1)S(1)}, u32[]{:S(2)}, u32[]{:S(2)}) collective-permute-start(bf16[256,2304]{1,0:T(8,128)(2,1)S(1)} %get-tuple-element.125.refs_4_.refs_2_.refs_6_), channel_id=1, source_target_pairs={{0,4},{4,0},{8,12},{12,8},{16,20},{20,16},{24,28},{28,24},{1,5},{5... | collective-permute-start | bytes 3538952 | tf_op jit(solution)/shard_map/ppermute | solution.py:384
  70.9 9.5 %collective-permute-start.22 = (bf16[128,768]{1,0:T(8,128)(2,1)S(1)}, bf16[128,768]{1,0:T(8,128)(2,1)S(1)}, u32[]{:S(2)}, u32[]{:S(2)}) collective-permute-start(bf16[128,768]{1,0:T(8,128)(2,1)S(1)} %get-tuple-element.155), channel_id=1, source_target_pairs={{0,1},{1,0},{2,3},{3,2},{4,5},{5,4},{6,7},{7,6},{8,9},{9,8},{10,11... | collective-permute-start | bytes 589832 | tf_op jit(solution)/shard_map/ppermute | solution.py:390
  76.7 12.7 %collective-permute-start.24 = (bf16[128,768]{1,0:T(8,128)(2,1)S(1)}, bf16[128,768]{1,0:T(8,128)(2,1)S(1)}, u32[]{:S(2)}, u32[]{:S(2)}) collective-permute-start(bf16[128,768]{1,0:T(8,128)(2,1)S(1)} %get-tuple-element.158), channel_id=1, source_target_pairs={{0,1},{1,0},{2,3},{3,2},{4,5},{5,4},{6,7},{7,6},{8,9},{9,8},{10,11... | collective-permute-start | bytes 589832 | tf_op jit(solution)/shard_map/ppermute | solution.py:390
  80.4 14.7 %collective-permute-start.14 = (bf16[384,768]{1,0:T(8,128)(2,1)S(1)}, bf16[384,768]{1,0:T(8,128)(2,1)S(1)}, u32[]{:S(2)}, u32[]{:S(2)}) collective-permute-start(bf16[384,768]{1,0:T(8,128)(2,1)S(1)} %second.3), channel_id=1, source_target_pairs={{0,16},{4,12},{8,24},{12,4},{16,0},{20,28},{24,8},{28,20},{1,17},{... | collective-permute-start | bytes 1769480 | tf_op jit(solution)/shard_map/ppermute | solution.py:387
  82.1 54.4 %collective-permute-start.23 = (bf16[128,768]{1,0:T(8,128)(2,1)S(1)}, bf16[128,768]{1,0:T(8,128)(2,1)S(1)}, u32[]{:S(2)}, u32[]{:S(2)}) collective-permute-start(bf16[128,768]{1,0:T(8,128)(2,1)S(1)} %pad_maximum_fusion), channel_id=1, source_target_pairs={{0,2},{1,3},{2,0},{3,1},{4,6},{5,7},{6,4},{7,5},{8,10},{9,11},{10,... | collective-permute-start | bytes 589832 | tf_op jit(solution)/shard_map/ppermute | solution.py:390
  87.9 23.3 %collective-permute-start.15 = (bf16[2,96,2432]{2,1,0:T(8,128)(2,1)S(1)}, bf16[2,96,2432]{2,1,0:T(8,128)(2,1)S(1)}, u32[]{:S(2)}, u32[]{:S(2)}) collective-permute-start(bf16[2,96,2432]{2,1,0:T(8,128)(2,1)S(1)} %get-tuple-element.134), channel_id=1, source_target_pairs={{0,8},{4,20},{8,0},{12,28},{16,24},{20,4},{24,16},{28,12},{1,9},{5... | collective-permute-start | bytes 2801672 | tf_op jit(solution)/shard_map/ppermute | solution.py:387
  89.5 47.0 %collective-permute-start.25 = (bf16[128,768]{1,0:T(8,128)(2,1)S(1)}, bf16[128,768]{1,0:T(8,128)(2,1)S(1)}, u32[]{:S(2)}, u32[]{:S(2)}) collective-permute-start(bf16[128,768]{1,0:T(8,128)(2,1)S(1)} %pad_maximum_fusion.1), channel_id=1, source_target_pairs={{0,2},{1,3},{2,0},{3,1},{4,6},{5,7},{6,4},{7,5},{8,10},{9,11},{10,... | collective-permute-start | bytes 589832 | tf_op jit(solution)/shard_map/ppermute | solution.py:390
  91.4 21.3 %collective-permute-start.16 = (bf16[96,3840]{1,0:T(8,128)(2,1)S(1)}, bf16[96,3840]{1,0:T(8,128)(2,1)S(1)}, u32[]{:S(2)}, u32[]{:S(2)}) collective-permute-start(bf16[96,3840]{1,0:T(8,128)(2,1)S(1)} %second.4), channel_id=1, source_target_pairs={{0,16},{4,12},{8,24},{12,4},{16,0},{20,28},{24,8},{28,20},{1,17},{... | collective-permute-start | bytes 2211848 | tf_op jit(solution)/shard_map/ppermute | solution.py:387
  95.6 22.4 %collective-permute-start.17 = (bf16[2,96,768]{2,1,0:T(8,128)(2,1)S(1)}, bf16[2,96,768]{2,1,0:T(8,128)(2,1)S(1)}, u32[]{:S(2)}, u32[]{:S(2)}) collective-permute-start(bf16[2,96,768]{2,1,0:T(8,128)(2,1)S(1)} %get-tuple-element.139), channel_id=1, source_target_pairs={{0,1},{1,0},{2,3},{3,2},{4,5},{5,4},{6,7},{7,6},{8,9},{9,8},{10,11... | collective-permute-start | bytes 884744 | tf_op jit(solution)/shard_map/ppermute | solution.py:390
  113.2 16.5 %collective-permute-start.19 = (bf16[2,24,3840]{2,1,0:T(8,128)(2,1)S(1)}, bf16[2,24,3840]{2,1,0:T(8,128)(2,1)S(1)}, u32[]{:S(2)}, u32[]{:S(2)}) collective-permute-start(bf16[2,24,3840]{2,1,0:T(8,128)(2,1)S(1)} %get-tuple-element.142), channel_id=1, source_target_pairs={{0,1},{1,0},{2,3},{3,2},{4,5},{5,4},{6,7},{7,6},{8,9},{9,8},{10,11... | collective-permute-start | bytes 1105928 | tf_op jit(solution)/shard_map/ppermute | solution.py:390
  118.0 17.6 %collective-permute-start.21 = (bf16[96,768]{1,0:T(8,128)(2,1)S(1)}, bf16[96,768]{1,0:T(8,128)(2,1)S(1)}, u32[]{:S(2)}, u32[]{:S(2)}) collective-permute-start(bf16[96,768]{1,0:T(8,128)(2,1)S(1)} %fourth.3), channel_id=1, source_target_pairs={{0,2},{1,3},{2,0},{3,1},{4,6},{5,7},{6,4},{7,5},{8,10},{9,11},{10,... | collective-permute-start | bytes 442376 | tf_op jit(solution)/shard_map/ppermute | solution.py:390
  121.1 11.2 %collective-permute-start.20 = (bf16[2,24,2432]{2,1,0:T(8,128)(2,1)S(1)}, bf16[2,24,2432]{2,1,0:T(8,128)(2,1)S(1)}, u32[]{:S(2)}, u32[]{:S(2)}) collective-permute-start(bf16[2,24,2432]{2,1,0:T(8,128)(2,1)S(1)} %get-tuple-element.147), channel_id=1, source_target_pairs={{0,1},{1,0},{2,3},{3,2},{4,5},{5,4},{6,7},{7,6},{8,9},{9,8},{10,11... | collective-permute-start | bytes 700424 | tf_op jit(solution)/shard_map/ppermute | solution.py:390
  129.8 11.4 %collective-permute-start.26 = (bf16[24,3840]{1,0:T(8,128)(2,1)S(1)}, bf16[24,3840]{1,0:T(8,128)(2,1)S(1)}, u32[]{:S(2)}, u32[]{:S(2)}) collective-permute-start(bf16[24,3840]{1,0:T(8,128)(2,1)S(1)} %fourth.4), channel_id=1, source_target_pairs={{0,2},{1,3},{2,0},{3,1},{4,6},{5,7},{6,4},{7,5},{8,10},{9,11},{10,... | collective-permute-start | bytes 552968 | tf_op jit(solution)/shard_map/ppermute | solution.py:390
  132.3 10.2 %collective-permute-start.27 = (bf16[24,2432]{1,0:T(8,128)(2,1)S(1)}, bf16[24,2432]{1,0:T(8,128)(2,1)S(1)}, u32[]{:S(2)}, u32[]{:S(2)}) collective-permute-start(bf16[24,2432]{1,0:T(8,128)(2,1)S(1)} %fourth.5), channel_id=1, source_target_pairs={{0,2},{1,3},{2,0},{3,1},{4,6},{5,7},{6,4},{7,5},{8,10},{9,11},{10,... | collective-permute-start | bytes 350216 | tf_op jit(solution)/shard_map/ppermute | solution.py:390
  (40 other events, 252.6 us)

commit v4 on v3

--- a/solution.py
+++ b/solution.py
@@ -678,7 +678,7 @@
     result_near = links.flip_band(results[1], 1)
     mark = unit_down.second(back_right)
     per_row = hidden_width // width
-    up_cols = up_sums[0].reshape(n_img * nb, per_row, -1).swapaxes(1, 2).reshape(width, per_row)
+    up_cols = after(up_sums, unit_down.send)[0].reshape(n_img * nb, per_row, -1).swapaxes(1, 2).reshape(width, per_row)
     up_cols = jnp.pad(up_cols, ((0, 0), (18, COLS - 18 - per_row)))
     back = pl.pallas_call(
         functools.partial(input_back_kernel, rows, nb, block if aligned else half),

time: 144 us -> 154 us (1.069)
  starting transfers between devices: 49.7 us -> 38.8 us
  local copies, waits for them, and re-layouts: 4.97 us -> 15.7 us
  Pallas kernels: 55.4 us -> 63.7 us
    ppermute x10, starting transfers between devices: 29.4 us -> 16.1 us  [flip_band(): return lax.ppermute(x, 'band', [(k, k ^ bit) for k in range(self.nb)])]
    unnamed x72 -> x94, local copies, waits for them, and re-layouts: 2.73 us -> 9.34 us
    ppermute x10, waiting for transfers between devices: 11 us -> 15.1 us  [flip_band(): return lax.ppermute(x, 'band', [(k, k ^ bit) for k in range(self.nb)])]
    ppermute x6, starting transfers between devices: 10.8 us -> 14.6 us  [band_shift(): lax.ppermute(x, 'band', [(k, (k + s) % self.nb) for k in range(self.nb)])]
    ppermute x6, waiting for transfers between devices: 3.68 us -> 0.02 us  [band_shift(): lax.ppermute(x, 'band', [(k, (k + s) % self.nb) for k in range(self.nb)])]
    pallas_call x3, Pallas kernels: 0.42 us -> 2.81 us  [second(): pl.pallas_call(second_kernel, grid=(1,), in_specs=[self.pick(1)] * 2, out...]
    pallas_call x3, Pallas kernels: 1.25 us -> 3.44 us  [third(): pl.pallas_call(functools.partial(third_kernel, size), grid=(1,), in_specs...]
    pallas_call x3, Pallas kernels: 12.8 us -> 14.8 us  [__init__(): pl.pallas_call(functools.partial(weight_kernel, widths, self.extra), grid...]
  transfers between devices with their start and end apart: 28 -> 28, of which waited for: 9 -> 7; matrix products, arithmetic and copies ran while one was open for 2% -> 5% of each run, Pallas kernels for 37% -> 40%
where the time goes in v4:
time: 154 us; the launch traced here: 153 us
  Pallas kernels  63.7 us (41%)
  starting transfers between devices  38.8 us (25%)
  waiting for transfers between devices  31.9 us (21%)
  local copies, waits for them, and re-layouts  15.7 us (10%)
    ppermute x6, waiting for transfers between devices, flip_by_core(): lax.ppermute(x, 'img', [(k, k ^ (odd if k & 1 else even)) for k in range(...  16.8 us
    ppermute x10, starting transfers between devices, flip_band(): return lax.ppermute(x, 'band', [(k, k ^ bit) for k in range(self.nb)])  16.1 us
    ppermute x10, waiting for transfers between devices, flip_band(): return lax.ppermute(x, 'band', [(k, k ^ bit) for k in range(self.nb)])  15.1 us
    pallas_call x3, Pallas kernels, __init__(): pl.pallas_call(functools.partial(weight_kernel, widths, self.extra), grid...  14.8 us
    ppermute x6, starting transfers between devices, band_shift(): lax.ppermute(x, 'band', [(k, (k + s) % self.nb) for k in range(self.nb)])  14.6 us
    pallas_call x1, Pallas kernels, per_device(): pl.pallas_call(functools.partial(up_kernel, rows, nb, steps, up_block), g...  9.93 us
    unnamed x94, local copies, waits for them, and re-layouts  9.34 us
    pallas_call x1, Pallas kernels, per_device(): pl.pallas_call(functools.partial(attend_kernel, rows, nb, block if aligne...  9.09 us
  transfers between devices with their start and end apart: 28, of which 7 were waited for; matrix products, arithmetic and copies ran while one was open for 5% of the time, Pallas kernels for 40%

profile of v4, /device:TPU:0, one launch (start us, length us, event | category | flops | bytes accessed | tf_op | source)
XLA Modules:
  0.0 152.9 jit_solution(2084943855656409887)
XLA Ops:
  0.8 2.0 %spread.1 = (bf16[72,768]{1,0:T(8,128)(2,1)}, bf16[72,768]{1,0:T(8,128)(2,1)}, bf16[72,768]{1,0:T(8,128)(2,1)}, bf16[72,768]{1,0:T(8,128)(2,1)}) custom-call(s32[1]{0:T(128)} %bitcast.band, s32[4]{0:T(128)} %crop_rows.1, s32[4]{0:T(128)} %crop_cols.1, bf16[4,64,768]{2,1,0:T(8,128)(2,1)} %x.3, s32[4,64]{1,0:T(4,128)} %keep_mask.1), custom_call_target="tpu_custom_call" | custom-call | flops 5000000000 | bytes 20000000 | tf_op jit(solution)/shard_map/spread/pallas_call | solution.py:560
  2.8 3.1 %collective-permute-start = (bf16[72,768]{1,0:T(8,128)(2,1)}, bf16[72,768]{1,0:T(8,128)(2,1)S(1)}, u32[]{:S(2)}, u32[]{:S(2)}) collective-permute-start(bf16[72,768]{1,0:T(8,128)(2,1)} %get-tuple-element.100), channel_id=1, source_target_pairs={{0,1},{1,2},{2,3},{3,0},{4,5},{5,6},{6,7},{7,4},{8,9},{9,10},{10,1... | collective-permute-start | bytes 331784 | tf_op jit(solution)/shard_map/ppermute | solution.py:393
  5.8 2.6 %collective-permute-start.1 = (bf16[72,768]{1,0:T(8,128)(2,1)}, bf16[72,768]{1,0:T(8,128)(2,1)S(1)}, u32[]{:S(2)}, u32[]{:S(2)}) collective-permute-start(bf16[72,768]{1,0:T(8,128)(2,1)} %get-tuple-element.101), channel_id=1, source_target_pairs={{0,2},{1,3},{2,0},{3,1},{4,6},{5,7},{6,4},{7,5},{8,10},{9,11},{10,... | collective-permute-start | bytes 331784 | tf_op jit(solution)/shard_map/ppermute | solution.py:393
  14.0 5.5 %collective-permute-start.3 = (bf16[64,768]{1,0:T(8,128)(2,1)S(1)}, bf16[64,768]{1,0:T(8,128)(2,1)S(1)}, u32[]{:S(2)}, u32[]{:S(2)}) collective-permute-start(bf16[64,768]{1,0:T(8,128)(2,1)S(1)} %get-tuple-element.183), channel_id=1, source_target_pairs={{0,1},{1,2},{2,3},{3,0},{4,5},{5,6},{6,7},{7,4},{8,9},{9,10},{10,1... | collective-permute-start | bytes 294920 | tf_op jit(solution)/shard_map/ppermute | solution.py:393
  20.2 9.1 %attend.1 = (bf16[1152,256]{1,0:T(8,128)(2,1)}, bf16[1152,256]{1,0:T(8,128)(2,1)}, bf16[256,768]{1,0:T(8,128)(2,1)}, bf16[256,768]{1,0:T(8,128)(2,1)}, bf16[256,...) custom-call(s32[1]{0:T(128)} %bitcast.5.core, ...), custom_call_target="tpu_custom_call" | custom-call | flops 22499999744 | bytes 90000000 | tf_op jit(solution)/shard_map/attend/pallas_call | solution.py:581
  30.1 9.9 %up.1 = (bf16[1536,256]{1,0:T(8,128)(2,1)}, bf16[1536,256]{1,0:T(8,128)(2,1)}, bf16[256,3840]{1,0:T(8,128)(2,1)}, f32[8,3072]{1,0:T(8,128)}, bf16[256,768]{1,0:T(8,128)(2,1)}) custom-call(s32[1]{0:T(128)} %bitcast.5.core, bf16[256,768]{1,0:T(8,128)(2,1)} %get-tuple-element.103.refs_0_, f32[256,768]{1,0:T(8,128)} %get-tuple-element.110.refs_1_.refs_3_, ...), custom_call_target="tpu_custom_call" | custom-call | flops 24999999488 | bytes 100000000 | tf_op jit(solution)/shard_map/up/pallas_call | solution.py:601
  40.7 6.9 %down.1 = (f32[256,768]{1,0:T(8,128)}, bf16[256,768]{1,0:T(8,128)(2,1)}, f32[8,768]{1,0:T(8,128)}) custom-call(bf16[256,3840]{1,0:T(8,128)(2,1)} %get-tuple-element.108.refs_0_.refs_1_.refs_2_.refs_4_.refs_6_.refs_8_, bf16[256,3840]{1,0:T(8,128)(2,1)} %get-tuple-element.108.refs_0_.refs_1_.refs_2_.refs_4_.refs_6_.refs_8_, bf16[768,3072]{1,0:T(8,128)(2,1)} %refs_2_.1, ...), custom_call_target="tpu_custom_call" | custom-call | flops 17500000256 | bytes 70000000 | tf_op jit(solution)/shard_map/down/pallas_call | solution.py:624
  49.3 5.4 %weight_grad.3 = (bf16[2,384,768]{2,1,0:T(8,128)(2,1)}, bf16[2,384,768]{2,1,0:T(8,128)(2,1)S(1)}) custom-call(s32[4]{0:T(128)S(1)} %pad_add_fusion.quarters, bf16[1536,256]{1,0:T(8,128)(2,1)S(1)} %copy-done.26, bf16[1536,256]{1,0:T(8,128)(2,1)} %collective-permute-done.7.refs_1_, bf16[256,3840]{1,0:T(8,128)(2,1)S(1)} %copy-done.4, ...), custom_call_target="tpu_custom_call" | custom-call | flops 15000000512 | bytes 60000000 | tf_op jit(solution)/shard_map/weight_grad/pallas_call | solution.py:451
  57.2 6.4 %weight_grad.4 = (bf16[2,96,3840]{2,1,0:T(8,128)(2,1)}, bf16[2,96,3840]{2,1,0:T(8,128)(2,1)S(1)}) custom-call(s32[4]{0:T(128)S(1)} %pad_add_fusion.quarters, bf16[1152,256]{1,0:T(8,128)(2,1)S(1)} %copy-done, bf16[1152,256]{1,0:T(8,128)(2,1)S(1)} %collective-permute-done.6.refs_1_.refs_11_, bf16[256,3840]{1,0:T(8,128)(2,1)S(1)} %copy-done.4, ...), custom_call_target="tpu_custom_call" | custom-call | flops 15000000512 | bytes 60000000 | tf_op jit(solution)/shard_map/weight_grad/pallas_call | solution.py:451
  65.3 8.0 %attend_back.1 = (bf16[256,2304]{1,0:T(8,128)(2,1)S(1)}, f32[8,768]{1,0:T(8,128)S(1)}) custom-call(bf16[256,768]{1,0:T(8,128)(2,1)S(1)} %copy-done.9, bf16[256,768]{1,0:T(8,128)(2,1)S(1)} %copy-done.27, bf16[256,768]{1,0:T(8,128)(2,1)S(1)} %copy-done.28, bf16[256,768]{1,0:T(8,128)(2,1)S(1)} %copy-done.29, f32[8,256]{1,0:T(8,128)S(1)} %copy-done.33, ...), custom_call_target="tpu_custom_call" | custom-call | flops 27499999232 | bytes 110000000 | tf_op jit(solution)/shard_map/attend_back/pallas_call | solution.py:654
  78.6 3.6 %collective-permute-start.22 = (bf16[128,768]{1,0:T(8,128)(2,1)}, bf16[128,768]{1,0:T(8,128)(2,1)}, u32[]{:S(2)}, u32[]{:S(2)}) collective-permute-start(bf16[128,768]{1,0:T(8,128)(2,1)} %get-tuple-element.157), channel_id=1, source_target_pairs={{0,1},{1,0},{2,3},{3,2},{4,5},{5,4},{6,7},{7,6},{8,9},{9,8},{10,11... | collective-permute-start | bytes 589832 | tf_op jit(solution)/shard_map/ppermute | solution.py:390
  82.2 1.8 %copy.38 = f32[32,24,4]{2,1,0:T(8,128)} copy(f32[32,24,4]{1,2,0:T(4,128)} %bitcast.27) | data formatting | bytes 24576 | tf_op jit(solution)/shard_map/transpose | solution.py:681
  92.8 2.7 %collective-permute-start.23 = (bf16[128,768]{1,0:T(8,128)(2,1)S(1)}, bf16[128,768]{1,0:T(8,128)(2,1)S(1)}, u32[]{:S(2)}, u32[]{:S(2)}) collective-permute-start(bf16[128,768]{1,0:T(8,128)(2,1)S(1)} %pad_maximum_fusion), channel_id=1, source_target_pairs={{0,2},{1,3},{2,0},{3,1},{4,6},{5,7},{6,4},{7,5},{8,10},{9,11},{10,... | collective-permute-start | bytes 589832 | tf_op jit(solution)/shard_map/ppermute | solution.py:390
  95.6 3.1 %weight_grad.5 = (bf16[2,96,2432]{2,1,0:T(8,128)(2,1)S(1)}, bf16[2,96,2432]{2,1,0:T(8,128)(2,1)S(1)}) custom-call(s32[4]{0:T(128)S(1)} %pad_add_fusion.quarters, bf16[1152,256]{1,0:T(8,128)(2,1)S(1)} %copy-done, bf16[1152,256]{1,0:T(8,128)(2,1)S(1)} %collective-permute-done.6.refs_1_.refs_11_, ...), custom_call_target="tpu_custom_call" | custom-call | flops 250000000 | bytes 1000000 | tf_op jit(solution)/shard_map/weight_grad/pallas_call | solution.py:451
  105.8 14.1 %collective-permute-done.15.got = bf16[2,96,2432]{2,1,0:T(8,128)(2,1)S(1)} collective-permute-done((bf16[2,96,2432]{2,1,0:T(8,128)(2,1)S(1)}, bf16[2,96,2432]{2,1,0:T(8,128)(2,1)S(1)}, u32[]{:S(2)}, u32[]{:S(2)}) %collective-permute-start.15) | collective-permute-done | bytes 933920 | tf_op jit(solution)/shard_map/ppermute | solution.py:387
  121.8 1.7 %collective-permute-start.21 = (bf16[96,768]{1,0:T(8,128)(2,1)S(1)}, bf16[96,768]{1,0:T(8,128)(2,1)S(1)}, u32[]{:S(2)}, u32[]{:S(2)}) collective-permute-start(bf16[96,768]{1,0:T(8,128)(2,1)S(1)} %fourth.3), channel_id=1, source_target_pairs={{0,2},{1,3},{2,0},{3,1},{4,6},{5,7},{6,4},{7,5},{8,10},{9,11},{10,... | collective-permute-start | bytes 442376 | tf_op jit(solution)/shard_map/ppermute | solution.py:390
  123.5 2.4 %collective-permute-start.19 = (bf16[2,24,3840]{2,1,0:T(8,128)(2,1)S(1)}, bf16[2,24,3840]{2,1,0:T(8,128)(2,1)S(1)}, u32[]{:S(2)}, u32[]{:S(2)}) collective-permute-start(bf16[2,24,3840]{2,1,0:T(8,128)(2,1)S(1)} %get-tuple-element.144), channel_id=1, source_target_pairs={{0,1},{1,0},{2,3},{3,2},{4,5},{5,4},{6,7},{7,6},{8,9},{9,8},{10,11... | collective-permute-start | bytes 1105928 | tf_op jit(solution)/shard_map/ppermute | solution.py:390
  125.9 2.7 %collective-permute-done.18.more = bf16[96,2432]{1,0:T(8,128)(2,1)S(1)} collective-permute-done((bf16[96,2432]{1,0:T(8,128)(2,1)S(1)}, bf16[96,2432]{1,0:T(8,128)(2,1)S(1)}, u32[]{:S(2)}, u32[]{:S(2)}) %collective-permute-start.18) | collective-permute-done | bytes 466976 | tf_op jit(solution)/shard_map/ppermute | solution.py:387
  129.0 2.1 %collective-permute-start.20 = (bf16[2,24,2432]{2,1,0:T(8,128)(2,1)S(1)}, bf16[2,24,2432]{2,1,0:T(8,128)(2,1)S(1)}, u32[]{:S(2)}, u32[]{:S(2)}) collective-permute-start(bf16[2,24,2432]{2,1,0:T(8,128)(2,1)S(1)} %get-tuple-element.149), channel_id=1, source_target_pairs={{0,1},{1,0},{2,3},{3,2},{4,5},{5,4},{6,7},{7,6},{8,9},{9,8},{10,11... | collective-permute-start | bytes 700424 | tf_op jit(solution)/shard_map/ppermute | solution.py:390
  131.1 6.7 %collective-permute-done.19.got = bf16[2,24,3840]{2,1,0:T(8,128)(2,1)S(1)} collective-permute-done((bf16[2,24,3840]{2,1,0:T(8,128)(2,1)S(1)}, bf16[2,24,3840]{2,1,0:T(8,128)(2,1)S(1)}, u32[]{:S(2)}, u32[]{:S(2)}) %collective-permute-start.19) | collective-permute-done | bytes 368672 | tf_op jit(solution)/shard_map/ppermute | solution.py:390
  137.8 2.2 %collective-permute-start.26 = (bf16[24,3840]{1,0:T(8,128)(2,1)S(1)}, bf16[24,3840]{1,0:T(8,128)(2,1)S(1)}, u32[]{:S(2)}, u32[]{:S(2)}) collective-permute-start(bf16[24,3840]{1,0:T(8,128)(2,1)S(1)} %fourth.4), channel_id=1, source_target_pairs={{0,2},{1,3},{2,0},{3,1},{4,6},{5,7},{6,4},{7,5},{8,10},{9,11},{10,... | collective-permute-start | bytes 552968 | tf_op jit(solution)/shard_map/ppermute | solution.py:390
  140.0 4.4 %collective-permute-done.20.got = bf16[2,24,2432]{2,1,0:T(8,128)(2,1)S(1)} collective-permute-done((bf16[2,24,2432]{2,1,0:T(8,128)(2,1)S(1)}, bf16[2,24,2432]{2,1,0:T(8,128)(2,1)S(1)}, u32[]{:S(2)}, u32[]{:S(2)}) %collective-permute-start.20) | collective-permute-done | bytes 233504 | tf_op jit(solution)/shard_map/ppermute | solution.py:390
  145.4 2.0 %gather.1 = (bf16[4,64,768]{2,1,0:T(8,128)(2,1)}, f32[4,64,768]{2,1,0:T(8,128)}) custom-call(s32[1]{0:T(128)} %bitcast.band, bf16[64,768]{1,0:T(8,128)(2,1)S(1)} %copy-done.23, bf16[128,768]{1,0:T(8,128)(2,1)} %collective-permute-done.22.refs_1_, bf16[128,768]{1,0:T(8,128)(2,1)S(1)} %collective-permute-done.23.refs_2_, ...), custom_call_target="tpu_custom_call" | custom-call | flops 5000000000 | bytes 20000000 | tf_op jit(solution)/shard_map/gather/pallas_call | solution.py:719
  147.4 2.9 %collective-permute-done.26.more = bf16[24,3840]{1,0:T(8,128)(2,1)S(1)} collective-permute-done((bf16[24,3840]{1,0:T(8,128)(2,1)S(1)}, bf16[24,3840]{1,0:T(8,128)(2,1)S(1)}, u32[]{:S(2)}, u32[]{:S(2)}) %collective-permute-start.26) | collective-permute-done | bytes 184352 | tf_op jit(solution)/shard_map/ppermute | solution.py:390
  (170 shorter events, 40.2 us)
Async XLA Ops:
  2.8 11.3 %collective-permute-start = (bf16[72,768]{1,0:T(8,128)(2,1)}, bf16[72,768]{1,0:T(8,128)(2,1)S(1)}, u32[]{:S(2)}, u32[]{:S(2)}) collective-permute-start(bf16[72,768]{1,0:T(8,128)(2,1)} %get-tuple-element.100), channel_id=1, source_target_pairs={{0,1},{1,2},{2,3},{3,0},{4,5},{5,6},{6,7},{7,4},{8,9},{9,10},{10,1... | collective-permute-start | bytes 331784 | tf_op jit(solution)/shard_map/ppermute | solution.py:393
  5.8 13.7 %collective-permute-start.1 = (bf16[72,768]{1,0:T(8,128)(2,1)}, bf16[72,768]{1,0:T(8,128)(2,1)S(1)}, u32[]{:S(2)}, u32[]{:S(2)}) collective-permute-start(bf16[72,768]{1,0:T(8,128)(2,1)} %get-tuple-element.101), channel_id=1, source_target_pairs={{0,2},{1,3},{2,0},{3,1},{4,6},{5,7},{6,4},{7,5},{8,10},{9,11},{10,... | collective-permute-start | bytes 331784 | tf_op jit(solution)/shard_map/ppermute | solution.py:393
  8.4 11.1 %collective-permute-start.2 = (bf16[72,768]{1,0:T(8,128)(2,1)}, bf16[72,768]{1,0:T(8,128)(2,1)S(1)}, u32[]{:S(2)}, u32[]{:S(2)}) collective-permute-start(bf16[72,768]{1,0:T(8,128)(2,1)} %get-tuple-element.102), channel_id=1, source_target_pairs={{0,3},{1,0},{2,1},{3,2},{4,7},{5,4},{6,5},{7,6},{8,11},{9,8},{10,9... | collective-permute-start | bytes 331784 | tf_op jit(solution)/shard_map/ppermute | solution.py:393
  10.4 18.9 %collective-permute-start.5 = (bf16[64,768]{1,0:T(8,128)(2,1)S(1)}, bf16[64,768]{1,0:T(8,128)(2,1)S(1)}, u32[]{:S(2)}, u32[]{:S(2)}) collective-permute-start(bf16[64,768]{1,0:T(8,128)(2,1)S(1)} %get-tuple-element.181), channel_id=1, source_target_pairs={{0,3},{1,0},{2,1},{3,2},{4,7},{5,4},{6,5},{7,6},{8,11},{9,8},{10,9... | collective-permute-start | bytes 294920 | tf_op jit(solution)/shard_map/ppermute | solution.py:393
  10.9 18.5 %collective-permute-start.4 = (bf16[64,768]{1,0:T(8,128)(2,1)S(1)}, bf16[64,768]{1,0:T(8,128)(2,1)S(1)}, u32[]{:S(2)}, u32[]{:S(2)}) collective-permute-start(bf16[64,768]{1,0:T(8,128)(2,1)S(1)} %get-tuple-element.182), channel_id=1, source_target_pairs={{0,2},{1,3},{2,0},{3,1},{4,6},{5,7},{6,4},{7,5},{8,10},{9,11},{10,... | collective-permute-start | bytes 294920 | tf_op jit(solution)/shard_map/ppermute | solution.py:393
  14.0 15.4 %collective-permute-start.3 = (bf16[64,768]{1,0:T(8,128)(2,1)S(1)}, bf16[64,768]{1,0:T(8,128)(2,1)S(1)}, u32[]{:S(2)}, u32[]{:S(2)}) collective-permute-start(bf16[64,768]{1,0:T(8,128)(2,1)S(1)} %get-tuple-element.183), channel_id=1, source_target_pairs={{0,1},{1,2},{2,3},{3,0},{4,5},{5,6},{6,7},{7,4},{8,9},{9,10},{10,1... | collective-permute-start | bytes 294920 | tf_op jit(solution)/shard_map/ppermute | solution.py:393
  29.3 11.4 %collective-permute-start.6 = (bf16[1152,256]{1,0:T(8,128)(2,1)}, bf16[1152,256]{1,0:T(8,128)(2,1)S(1)}, u32[]{:S(2)}, u32[]{:S(2)}) collective-permute-start(bf16[1152,256]{1,0:T(8,128)(2,1)} %get-tuple-element.109), channel_id=1, source_target_pairs={{0,4},{4,0},{8,12},{12,8},{16,20},{20,16},{24,28},{28,24},{1,5},{5... | collective-permute-start | bytes 1769480 | tf_op jit(solution)/shard_map/ppermute | solution.py:384
  47.6 9.6 %collective-permute-start.9 = (bf16[256,768]{1,0:T(8,128)(2,1)}, bf16[256,768]{1,0:T(8,128)(2,1)S(1)}, u32[]{:S(2)}, u32[]{:S(2)}) collective-permute-start(bf16[256,768]{1,0:T(8,128)(2,1)} %get-tuple-element.120.refs_12_.gb), channel_id=1, source_target_pairs={{0,4},{4,0},{8,12},{12,8},{16,20},{20,16},{24,28},{28,24},{1,5},{5... | collective-permute-start | bytes 1179656 | tf_op jit(solution)/shard_map/ppermute | solution.py:384
  55.7 29.6 %collective-permute-start.10 = (bf16[2,384,768]{2,1,0:T(8,128)(2,1)}, bf16[2,384,768]{2,1,0:T(8,128)(2,1)}, u32[]{:S(2)}, u32[]{:S(2)}) collective-permute-start(bf16[2,384,768]{2,1,0:T(8,128)(2,1)} %get-tuple-element.116), channel_id=1, source_target_pairs={{0,8},{4,20},{8,0},{12,28},{16,24},{20,4},{24,16},{28,12},{1,9},{5... | collective-permute-start | bytes 3538952 | tf_op jit(solution)/shard_map/ppermute | solution.py:387
  64.7 36.0 %collective-permute-start.13 = (bf16[2,96,3840]{2,1,0:T(8,128)(2,1)}, bf16[2,96,3840]{2,1,0:T(8,128)(2,1)}, u32[]{:S(2)}, u32[]{:S(2)}) collective-permute-start(bf16[2,96,3840]{2,1,0:T(8,128)(2,1)} %get-tuple-element.119), channel_id=1, source_target_pairs={{0,8},{4,20},{8,0},{12,28},{16,24},{20,4},{24,16},{28,12},{1,9},{5... | collective-permute-start | bytes 4423688 | tf_op jit(solution)/shard_map/ppermute | solution.py:387
  73.9 18.9 %collective-permute-start.11 = (bf16[256,2304]{1,0:T(8,128)(2,1)S(1)}, bf16[256,2304]{1,0:T(8,128)(2,1)S(1)}, u32[]{:S(2)}, u32[]{:S(2)}) collective-permute-start(bf16[256,2304]{1,0:T(8,128)(2,1)S(1)} %get-tuple-element.126.refs_4_.refs_2_.refs_6_), channel_id=1, source_target_pairs={{0,4},{4,0},{8,12},{12,8},{16,20},{20,16},{24,28},{28,24},{1,5},{5... | collective-permute-start | bytes 3538952 | tf_op jit(solution)/shard_map/ppermute | solution.py:384
  78.6 11.8 %collective-permute-start.22 = (bf16[128,768]{1,0:T(8,128)(2,1)}, bf16[128,768]{1,0:T(8,128)(2,1)}, u32[]{:S(2)}, u32[]{:S(2)}) collective-permute-start(bf16[128,768]{1,0:T(8,128)(2,1)} %get-tuple-element.157), channel_id=1, source_target_pairs={{0,1},{1,0},{2,3},{3,2},{4,5},{5,4},{6,7},{7,6},{8,9},{9,8},{10,11... | collective-permute-start | bytes 589832 | tf_op jit(solution)/shard_map/ppermute | solution.py:390
  90.1 10.3 %collective-permute-start.24 = (bf16[128,768]{1,0:T(8,128)(2,1)S(1)}, bf16[128,768]{1,0:T(8,128)(2,1)S(1)}, u32[]{:S(2)}, u32[]{:S(2)}) collective-permute-start(bf16[128,768]{1,0:T(8,128)(2,1)S(1)} %get-tuple-element.160), channel_id=1, source_target_pairs={{0,1},{1,0},{2,3},{3,2},{4,5},{5,4},{6,7},{7,6},{8,9},{9,8},{10,11... | collective-permute-start | bytes 589832 | tf_op jit(solution)/shard_map/ppermute | solution.py:390
  91.3 12.4 %collective-permute-start.14 = (bf16[384,768]{1,0:T(8,128)(2,1)S(1)}, bf16[384,768]{1,0:T(8,128)(2,1)S(1)}, u32[]{:S(2)}, u32[]{:S(2)}) collective-permute-start(bf16[384,768]{1,0:T(8,128)(2,1)S(1)} %second.3), channel_id=1, source_target_pairs={{0,16},{4,12},{8,24},{12,4},{16,0},{20,28},{24,8},{28,20},{1,17},{... | collective-permute-start | bytes 1769480 | tf_op jit(solution)/shard_map/ppermute | solution.py:387
  92.8 52.6 %collective-permute-start.23 = (bf16[128,768]{1,0:T(8,128)(2,1)S(1)}, bf16[128,768]{1,0:T(8,128)(2,1)S(1)}, u32[]{:S(2)}, u32[]{:S(2)}) collective-permute-start(bf16[128,768]{1,0:T(8,128)(2,1)S(1)} %pad_maximum_fusion), channel_id=1, source_target_pairs={{0,2},{1,3},{2,0},{3,1},{4,6},{5,7},{6,4},{7,5},{8,10},{9,11},{10,... | collective-permute-start | bytes 589832 | tf_op jit(solution)/shard_map/ppermute | solution.py:390
  98.7 21.2 %collective-permute-start.15 = (bf16[2,96,2432]{2,1,0:T(8,128)(2,1)S(1)}, bf16[2,96,2432]{2,1,0:T(8,128)(2,1)S(1)}, u32[]{:S(2)}, u32[]{:S(2)}) collective-permute-start(bf16[2,96,2432]{2,1,0:T(8,128)(2,1)S(1)} %get-tuple-element.136), channel_id=1, source_target_pairs={{0,8},{4,20},{8,0},{12,28},{16,24},{20,4},{24,16},{28,12},{1,9},{5... | collective-permute-start | bytes 2801672 | tf_op jit(solution)/shard_map/ppermute | solution.py:387
  100.5 44.9 %collective-permute-start.25 = (bf16[128,768]{1,0:T(8,128)(2,1)S(1)}, bf16[128,768]{1,0:T(8,128)(2,1)S(1)}, u32[]{:S(2)}, u32[]{:S(2)}) collective-permute-start(bf16[128,768]{1,0:T(8,128)(2,1)S(1)} %pad_maximum_fusion.1), channel_id=1, source_target_pairs={{0,2},{1,3},{2,0},{3,1},{4,6},{5,7},{6,4},{7,5},{8,10},{9,11},{10,... | collective-permute-start | bytes 589832 | tf_op jit(solution)/shard_map/ppermute | solution.py:390
  102.1 18.0 %collective-permute-start.16 = (bf16[96,3840]{1,0:T(8,128)(2,1)S(1)}, bf16[96,3840]{1,0:T(8,128)(2,1)S(1)}, u32[]{:S(2)}, u32[]{:S(2)}) collective-permute-start(bf16[96,3840]{1,0:T(8,128)(2,1)S(1)} %second.4), channel_id=1, source_target_pairs={{0,16},{4,12},{8,24},{12,4},{16,0},{20,28},{24,8},{28,20},{1,17},{... | collective-permute-start | bytes 2211848 | tf_op jit(solution)/shard_map/ppermute | solution.py:387
  105.1 16.6 %collective-permute-start.17 = (bf16[2,96,768]{2,1,0:T(8,128)(2,1)S(1)}, bf16[2,96,768]{2,1,0:T(8,128)(2,1)S(1)}, u32[]{:S(2)}, u32[]{:S(2)}) collective-permute-start(bf16[2,96,768]{2,1,0:T(8,128)(2,1)S(1)} %get-tuple-element.141), channel_id=1, source_target_pairs={{0,1},{1,0},{2,3},{3,2},{4,5},{5,4},{6,7},{7,6},{8,9},{9,8},{10,11... | collective-permute-start | bytes 884744 | tf_op jit(solution)/shard_map/ppermute | solution.py:390
  120.0 8.6 %collective-permute-start.18 = (bf16[96,2432]{1,0:T(8,128)(2,1)S(1)}, bf16[96,2432]{1,0:T(8,128)(2,1)S(1)}, u32[]{:S(2)}, u32[]{:S(2)}) collective-permute-start(bf16[96,2432]{1,0:T(8,128)(2,1)S(1)} %second.5), channel_id=1, source_target_pairs={{0,16},{4,12},{8,24},{12,4},{16,0},{20,28},{24,8},{28,20},{1,17},{... | collective-permute-start | bytes 1400840 | tf_op jit(solution)/shard_map/ppermute | solution.py:387
  121.8 22.9 %collective-permute-start.21 = (bf16[96,768]{1,0:T(8,128)(2,1)S(1)}, bf16[96,768]{1,0:T(8,128)(2,1)S(1)}, u32[]{:S(2)}, u32[]{:S(2)}) collective-permute-start(bf16[96,768]{1,0:T(8,128)(2,1)S(1)} %fourth.3), channel_id=1, source_target_pairs={{0,2},{1,3},{2,0},{3,1},{4,6},{5,7},{6,4},{7,5},{8,10},{9,11},{10,... | collective-permute-start | bytes 442376 | tf_op jit(solution)/shard_map/ppermute | solution.py:390
  123.5 14.3 %collective-permute-start.19 = (bf16[2,24,3840]{2,1,0:T(8,128)(2,1)S(1)}, bf16[2,24,3840]{2,1,0:T(8,128)(2,1)S(1)}, u32[]{:S(2)}, u32[]{:S(2)}) collective-permute-start(bf16[2,24,3840]{2,1,0:T(8,128)(2,1)S(1)} %get-tuple-element.144), channel_id=1, source_target_pairs={{0,1},{1,0},{2,3},{3,2},{4,5},{5,4},{6,7},{7,6},{8,9},{9,8},{10,11... | collective-permute-start | bytes 1105928 | tf_op jit(solution)/shard_map/ppermute | solution.py:390
  129.0 15.4 %collective-permute-start.20 = (bf16[2,24,2432]{2,1,0:T(8,128)(2,1)S(1)}, bf16[2,24,2432]{2,1,0:T(8,128)(2,1)S(1)}, u32[]{:S(2)}, u32[]{:S(2)}) collective-permute-start(bf16[2,24,2432]{2,1,0:T(8,128)(2,1)S(1)} %get-tuple-element.149), channel_id=1, source_target_pairs={{0,1},{1,0},{2,3},{3,2},{4,5},{5,4},{6,7},{7,6},{8,9},{9,8},{10,11... | collective-permute-start | bytes 700424 | tf_op jit(solution)/shard_map/ppermute | solution.py:390
  137.8 12.5 %collective-permute-start.26 = (bf16[24,3840]{1,0:T(8,128)(2,1)S(1)}, bf16[24,3840]{1,0:T(8,128)(2,1)S(1)}, u32[]{:S(2)}, u32[]{:S(2)}) collective-permute-start(bf16[24,3840]{1,0:T(8,128)(2,1)S(1)} %fourth.4), channel_id=1, source_target_pairs={{0,2},{1,3},{2,0},{3,1},{4,6},{5,7},{6,4},{7,5},{8,10},{9,11},{10,... | collective-permute-start | bytes 552968 | tf_op jit(solution)/shard_map/ppermute | solution.py:390
  (51 other events, 268.6 us)
